TPU v7x, 32 devices: a whole 2x2x4 slice. The times are simulated.
32 devices in a mesh: parts: 2 (over x), store: 16 (over z, y, core).
Axes of the slice: x: 2, y: 2, z: 4, core: 2. Of those that a mesh axis runs over, the one named last changes fastest.
Arguments:
- store_feats: bfloat16 [131072, 256], P(('parts', 'store')), parts along dimension 0
- requests: int32 [512, 8], P(('parts', 'store')), parts along dimension 0, may hold values from 0 to 4095, as said below
- node_slots: int32 [128, 256], P(('parts', 'store')), parts along dimension 0, may hold values from 0 to 127, as said below
- edges: int32 [128, 1024, 2], P(('parts', 'store')), parts along dimension 0, may hold values from 0 to 255
- pairs: int32 [128, 64, 2], P(('parts', 'store')), parts along dimension 0, may hold values from 0 to 255
- targets: float32 [128, 64], P(('parts', 'store')), parts along dimension 0, may hold values from -6 to 6
- w_qkv: bfloat16 [256, 768], replicated, may hold values from -0.375 to 0.375
- w_o: bfloat16 [256, 256], replicated, may hold values from -0.375 to 0.375
- w_msg: bfloat16 [256, 256], replicated, may hold values from -0.375 to 0.375
- w_up: bfloat16 [256, 512], replicated, may hold values from -0.375 to 0.375
- w_down: bfloat16 [512, 256], replicated, may hold values from -0.25 to 0.25
- w_read: float32 [256], replicated, may hold values from -0.375 to 0.375
Outputs:
- preds: float32 [128, 64], P(('parts', 'store')), parts along dimension 0
- loss: float32 [2], P('parts'), parts along dimension 0
- g_qkv: float32 [512, 768], P(('parts', 'store')), parts along dimension 0
- g_o: float32 [512, 256], P(('parts', 'store')), parts along dimension 0
- g_msg: float32 [512, 256], P(('parts', 'store')), parts along dimension 0
- g_up: float32 [512, 512], P(('parts', 'store')), parts along dimension 0
- g_down: float32 [1024, 256], P(('parts', 'store')), parts along dimension 0
There are 2 independent parts, one for each index of `parts`. A program takes and returns all parts, laid end to end along the dimension named above; an argument that names none is the same for every part. Nothing has to cross between parts.
Inputs may be any that keep to these rules, and one draw needn't show every extreme that they name: Each row of requests starts with 1 to 8 distinct row numbers and holds zeros after them; every device fetches 8 rows from some owner, and some owner serves 8 rows to every device. `node_slots`: A node's slot o * 8 + c always names one of the leading entries c (those before the zero padding; a leading entry may itself be row 0) of the request row of owner o on the subgraph's device.
All inputs are finite; a program needn't handle non-finite values.
Results may differ from a plain program's by a relative error of at most 0.015.
The roundings to bfloat16 on the way count: a program that leaves them out, or rounds other values in their place, can miss the bound.
Values may be sent and summed in bfloat16 or wider, within the bound.
No kernel may reach another device: no remote copies, remote signals or barrier semaphores. Data moves between devices by JAX's collectives and lax.ppermute only.
A program may use at most 128 MiB of HBM per device.

v0:
```python
import jax
import jax.numpy as jnp
from jax import lax
from jax.sharding import PartitionSpec as P


def layer_norm(value):
    mean = jnp.mean(value, axis=-1, keepdims=True)
    centred = value - mean
    var = jnp.mean(centred * centred, axis=-1, keepdims=True)
    return centred * lax.rsqrt(var + 1e-05)


def adjacency(edges, width):
    iota = jnp.arange(width, dtype=jnp.int32)
    src_hot = (edges[:, :, 0][:, :, None] == iota).astype(jnp.bfloat16)
    dst_hot = (edges[:, :, 1][:, :, None] == iota).astype(jnp.bfloat16)
    counts = jnp.einsum("bei,bej->bij", dst_hot, src_hot, preferred_element_type=jnp.float32)
    deg_inv = 1.0 / (1.0 + jnp.sum(counts, axis=-1))
    return (counts.astype(jnp.bfloat16), deg_inv)


def objective_of(x_nodes, adj, deg_inv, pairs, targets, w_read, w_qkv, w_o, w_msg, w_up, w_down):
    batch, width, feats = x_nodes.shape
    heads = 8
    head_dim = feats // heads
    flat = x_nodes.reshape(batch * width, feats)
    qkv = jnp.dot(flat, w_qkv, preferred_element_type=jnp.float32).astype(jnp.bfloat16)
    qkv = qkv.reshape(batch, width, 3, heads, head_dim)
    query, keys, values = (qkv[:, :, 0], qkv[:, :, 1], qkv[:, :, 2])
    scores = jnp.einsum(
        "bqhd,bkhd->bhqk", query, keys, preferred_element_type=jnp.float32
    ) * head_dim ** (-0.5)
    top = jnp.max(scores, axis=-1, keepdims=True)
    expo = jnp.exp(scores - top)
    probs = (expo / jnp.sum(expo, axis=-1, keepdims=True)).astype(jnp.bfloat16)
    att = jnp.einsum("bhqk,bkhd->bqhd", probs, values, preferred_element_type=jnp.float32).astype(
        jnp.bfloat16
    )
    attn_out = jnp.dot(att.reshape(batch * width, feats), w_o, preferred_element_type=jnp.float32)
    xw = (
        jnp.dot(flat, w_msg, preferred_element_type=jnp.float32)
        .astype(jnp.bfloat16)
        .reshape(batch, width, feats)
    )
    agg = (
        jnp.einsum("bij,bjf->bif", adj, xw, preferred_element_type=jnp.float32)
        + xw.astype(jnp.float32)
    ) * deg_inv[:, :, None]
    base = flat.astype(jnp.float32)
    hidden_h = (
        layer_norm(base + jax.nn.relu(agg.reshape(batch * width, feats)))
        + layer_norm(base + attn_out)
    ).astype(jnp.bfloat16)
    upper = jnp.dot(hidden_h, w_up, preferred_element_type=jnp.float32)
    gated = jax.nn.gelu(upper, approximate=True).astype(jnp.bfloat16)
    mixed = jnp.dot(gated, w_down, preferred_element_type=jnp.float32)
    out = layer_norm(hidden_h.astype(jnp.float32) + mixed).reshape(batch, width, feats)
    left = jnp.take_along_axis(out, pairs[:, :, 0][:, :, None], axis=1)
    right = jnp.take_along_axis(out, pairs[:, :, 1][:, :, None], axis=1)
    preds = jnp.sum(left * right * w_read, axis=-1)
    diff = preds - targets
    objective = jnp.sum(diff * diff) / (batch * pairs.shape[1])
    return (objective, preds)


def local_step(x_nodes, edges, pairs, targets, w_read, weights):
    adj, deg_inv = adjacency(edges, x_nodes.shape[1])

    def wrapped(w_qkv, w_o, w_msg, w_up, w_down):
        return objective_of(
            x_nodes, adj, deg_inv, pairs, targets, w_read, w_qkv, w_o, w_msg, w_up, w_down
        )

    objective, pullback, preds = jax.vjp(wrapped, *weights, has_aux=True)
    grads = pullback(jnp.ones((), objective.dtype))
    return (objective, preds, grads)


def shards(
    store_feats,
    requests,
    node_slots,
    edges,
    pairs,
    targets,
    w_qkv,
    w_o,
    w_msg,
    w_up,
    w_down,
    w_read,
):
    feats = store_feats.shape[1]
    groups = lax.axis_size("store")
    picked = jnp.take(
        store_feats,
        lax.all_to_all(requests, "store", split_axis=0, concat_axis=0, tiled=True),
        axis=0,
    )
    fetched = lax.all_to_all(picked, "store", split_axis=0, concat_axis=0, tiled=True)
    x_nodes = jnp.take(fetched.reshape(-1, feats), node_slots, axis=0)
    weights = (w_qkv, w_o, w_msg, w_up, w_down)
    objective, preds, grads = local_step(x_nodes, edges, pairs, targets, w_read, weights)
    terms = tuple((g.astype(jnp.float32) for g in grads))
    column = jnp.full((groups, 1), objective, jnp.float32)
    summed = (
        lax.psum_scatter(terms[0], "store", scatter_dimension=0, tiled=True),
        lax.psum_scatter(terms[1], "store", scatter_dimension=0, tiled=True),
        lax.psum_scatter(terms[2], "store", scatter_dimension=0, tiled=True),
        lax.psum_scatter(terms[3], "store", scatter_dimension=0, tiled=True),
        lax.psum_scatter(terms[4], "store", scatter_dimension=0, tiled=True),
        lax.psum_scatter(column, "store", scatter_dimension=0, tiled=True),
    )
    total_obj = summed[5][0, 0]
    shares = summed[:5]
    loss = (total_obj / groups).reshape(1)
    return (preds, loss, shares[0], shares[1], shares[2], shares[3], shares[4])


def solution(mesh):
    in_specs = (
        P(("parts", "store"), None),
        P(("parts", "store"), None),
        P(("parts", "store"), None),
        P(("parts", "store"), None, None),
        P(("parts", "store"), None, None),
        P(("parts", "store"), None),
        P(),
        P(),
        P(),
        P(),
        P(),
        P(),
    )
    out_specs = (
        P(("parts", "store"), None),
        P("parts"),
        P(("parts", "store"), None),
        P(("parts", "store"), None),
        P(("parts", "store"), None),
        P(("parts", "store"), None),
        P(("parts", "store"), None),
    )
    return jax.shard_map(shards, mesh=mesh, in_specs=in_specs, out_specs=out_specs, check_vma=False)
```

profile of v0, /device:TPU:0, one launch (start us, length us, event | category | flops | bytes accessed | tf_op | source)
XLA Modules:
  0.0 434.5 jit_solution(15611235698115017215)
XLA Ops:
  7.2 1.5 copy.48
  8.7 7.4 %all-to-all-start = ((s32[16,1,8]{2,1,0:T(1,128)}), s32[16,1,8]{2,1,0:T(1,128)S(1)}, u32[]{:S(2)}, u32[]{:S(2)}) async-start(s32[16,1,8]{2,1,0:T(1,128)} %copy.48), calls=%async_computation | async-start | bytes 16384 | tf_op jit(solution)/shard_map/all_to_all | solution.py:98
  16.1 0.7 compare_and_fusion.3
  16.8 0.7 fusion.68
  17.5 0.8 compare_and_fusion.1
  18.3 0.9 fusion.81
  19.1 1.6 fusion.83
  20.8 1.6 all-to-all-done
  22.8 0.8 gather_fusion
  23.6 0.7 bitcast_select_fusion
  24.3 4.4 %all-to-all-start.1 = ((bf16[16,8,256]{2,1,0:T(8,128)(2,1)}), bf16[16,8,256]{2,1,0:T(8,128)(2,1)S(1)}, u32[]{:S(2)}, u32[]{:S(2)}) async-start(bf16[16,8,256]{2,1,0:T(8,128)(2,1)} %bitcast_select_fusion), calls=%async_computation.1 | async-start | bytes 131072 | tf_op jit(solution)/shard_map/all_to_all | solution.py:101
  29.1 6.6 %all-to-all-done.1 = bf16[16,8,256]{2,1,0:T(8,128)(2,1)S(1)} async-done(((bf16[16,8,256]{2,1,0:T(8,128)(2,1)}), bf16[16,8,256]{2,1,0:T(8,128)(2,1)S(1)}, u32[]{:S(2)}, u32[]{:S(2)}) %all-to-all-start.1) | async-done | bytes 65568 | tf_op jit(solution)/shard_map/all_to_all | solution.py:101
  35.6 3.9 gather_fusion.1
  40.0 1.8 convolution_convert_fusion.1
  41.8 2.6 copy.54
  44.4 3.9 reshape.253
  48.2 1.9 fusion.80
  50.2 0.9 fusion.52
  51.1 0.9 broadcast_compare_fusion
  52.5 1.3 multiply_reduce_fusion
  53.8 1.6 fusion.13
  55.4 1.6 copy-done.2
  57.0 4.5 %convert_reduce_fusion = (f32[4,8,256]{2,1,0:T(8,128)S(1)}, pred[4,8,256,256]{2,3,1,0:T(32,128)(4,1)}, bf16[4,8,256,256]{2,3,1,0:T(8,128)(2,1)S(1)}) fusion(f32[4,8,256]{2,1,0:T(8,128)S(1)} %get-tuple-element.47, f32[4,8,256,256]{2,3,1,0:T(8,128)S(1)} %get-tuple-element.48, f32[4,8,256]{2,1,0:T(8,128)S(1)} %fusion.13), kind=kLoop, calls=%fused_computation.12 | loop fusion | flops 14671872 | bytes 14778368 | tf_op jit(solution)/shard_map/jvp()/reduce_sum | solution.py:34
  61.6 0.7 fusion.34
  62.3 1.3 copy-done.4
  64.1 0.8 copy-done.17
  64.8 1.0 fusion.82
  66.2 9.7 %add_convert_fusion = bf16[1024,256]{1,0:T(8,128)(2,1)S(1)} fusion(f32[1024,256]{1,0:T(8,128)S(1)} %get-tuple-element.50, f32[1024]{0:T(1024)S(1)} %fusion.66, f32[1024]{0:T(1024)S(1)} %broadcast_multiply_fusion.1, f32[1024]{0:T(1024)S(1)} %rsqrt.30, f32[1024]{0:T(1024)S(1)} %bitcast.155, f32[4,256,256]{2,1,0:T(8,128)S(1)} %get-tuple-element.35, ...), kind=kLoop, calls=%fused_computation.95 | loop fusion | flops 2359296 | bytes 3163136 | tf_op jit(solution)/shard_map/jvp()/convert_element_type | solution.py:54
  76.4 0.7 copy-done.43
  77.1 0.9 fusion.84
  78.8 0.6 copy-done.8
  79.7 2.0 gather_fusion.3
  81.8 2.0 gather_fusion.2
  84.0 0.6 add_multiply_fusion.11
  84.8 0.8 pad_maximum_fusion
  85.7 36.5 %scatter_fusion = f32[4,256,256]{2,1,0:T(8,128)S(1)} fusion(f32[4,256,256]{2,1,0:T(8,128)S(1)} %max.15, s32[512]{0:T(512)S(1)} %bitcast.138, f32[512,256]{1,0:T(8,128)} %bitcast.151), kind=kCustom, calls=%fused_computation.4 | custom fusion | flops 131072 | bytes 1576960 | tf_op jit(solution)/shard_map/transpose(jvp())/add_any | solution.py:59
  122.3 1.8 fusion.45
  124.1 0.6 fusion.79
  124.8 0.9 copy-done.29
  125.7 1.9 fusion.15
  127.7 1.3 fusion.44
  129.2 1.4 fusion.53
  130.7 2.9 fusion.78
  134.2 1.2 reshape.258
  135.4 3.2 fusion.40
  138.6 1.1 fusion.41
  139.9 6.8 %fusion.3 = (f32[4,8,256]{2,1,0:T(8,128)S(1)}, bf16[4,8,256,256]{2,3,1,0:T(8,128)(2,1)}) fusion(f32[4,8,256]{2,1,0:T(8,128)S(1)} %multiply_divide_fusion, f32[4,8,256]{2,1,0:T(8,128)S(1)} %get-tuple-element.47, f32[4,8,256,256]{2,3,1,0:T(8,128)} %copy-done.2, bf16[4,256,1,8,32]{1,0,4,3,2:T(4,128)(2,1)S(1)} %copy-done.26, bf16[4,8,32,256]{3,0,2,1:T(4,128)(2,1)} %bitcast.149), kind=kOutput, calls=%fused_computation.10 | convolution fusion | flops 148889600 | bytes 13729792 | tf_op jit(solution)/shard_map/transpose(jvp(bhqk,bkhd->bqhd))/dot_general | solution.py:37
  146.7 1.3 fusion.37
  148.1 6.3 %fusion.76 = (f32[4,8,256]{2,1,0:T(8,128)S(1)}, f32[4,8,256,256]{2,3,1,0:T(8,128)S(1)}) fusion(f32[4,8,256]{2,1,0:T(8,128)S(1)} %get-tuple-element.47, f32[4,8,256,256]{2,3,1,0:T(8,128)} %copy-done.2, f32[4,8,256]{2,1,0:T(8,128)S(1)} %neg.20, f32[4,8,256]{2,1,0:T(8,128)S(1)} %fusion.13, bf16[4,8,256,256]{2,3,1,0:T(8,128)(2,1)} %get-tuple-element.59), kind=kLoop, calls=%fused_computation.180 | loop fusion | flops 14671872 | bytes 21102592 | tf_op jit(solution)/shard_map/transpose(jvp())/reduce_sum | solution.py:35
  154.5 2.5 fusion.31
  157.0 1.5 copy-done.3
  158.7 1.8 fusion.36
  160.5 6.0 %fusion.32 = bf16[4,256,1,8,32]{1,4,3,0,2:T(8,128)(2,1)} fusion(f32[4,8,256,256]{2,3,1,0:T(8,128)} %copy-done.3, pred[4,8,256,256]{2,3,1,0:T(32,128)(4,1)S(1)} %copy-done.7, f32[4,8,256]{2,1,0:T(8,128)S(1)} %negate_divide_fusion, bf16[4,256,1,8,32]{1,0,4,3,2:T(4,128)(2,1)S(1)} %copy-done.11), kind=kOutput, calls=%fused_computation.74 | convolution fusion | flops 140771328 | bytes 11567104 | tf_op jit(solution)/shard_map/transpose(jvp(bqhd,bkhd->bhqk))/dot_general | solution.py:31
  166.6 3.6 fusion.35
  170.4 1.4 copy.66
  172.2 0.7 copy-done.16
  172.9 1.5 fusion.28
  174.4 0.6 dynamic-slice
  175.7 30.4 %all-reduce.3 = f32[16,1]{1,0:T(8,128)S(1)} all-reduce(f32[16,1]{1,0:T(8,128)S(1)} %broadcast_in_dim.103), channel_id=2, replica_groups=mesh['parts'=2,'store'=16] {'store'}, use_global_device_ids=true, to_apply=%region_11.13.clone | all-reduce | flops 16 | bytes 128
  206.1 1.1 fusion.85
  207.2 42.7 %reduce-scatter.8.cloned.1.call-done = f32[16,256]{1,0:T(8,128)} async-done(((f32[256,256]{1,0:T(8,128)}), f32[16,256]{1,0:T(8,128)}) %reduce-scatter.8.cloned.1.call-update) | async-done | bytes 16400 | tf_op jit(solution)/shard_map/reduce_scatter | solution.py:109
  249.8 59.0 %reduce-scatter.12.cloned.1.call-done = f32[16,512]{1,0:T(8,128)} async-done(((f32[256,512]{1,0:T(8,128)}), f32[16,512]{1,0:T(8,128)}) %reduce-scatter.12.cloned.1.call-update) | async-done | bytes 32784 | tf_op jit(solution)/shard_map/reduce_scatter | solution.py:111
  308.8 59.2 %reduce-scatter.14.cloned.1.call-done = f32[32,256]{1,0:T(8,128)} async-done(((f32[512,256]{1,0:T(8,128)}), f32[32,256]{1,0:T(8,128)}) %reduce-scatter.14.cloned.1.call-update) | async-done | bytes 32784 | tf_op jit(solution)/shard_map/reduce_scatter | solution.py:112
  368.1 59.5 %reduce-scatter.6.cloned.1.call-done = f32[16,768]{1,0:T(8,128)} async-done(((f32[256,768]{1,0:T(8,128)}), f32[16,768]{1,0:T(8,128)}) %reduce-scatter.6.cloned.1.call-update) | async-done | bytes 49168 | tf_op jit(solution)/shard_map/reduce_scatter | solution.py:108
  (148 shorter events, 6.4 us)
Async XLA Ops:
  7.2 15.6 %copy-start = (bf16[4096,256]{1,0:T(8,128)(2,1)S(1)}, bf16[4096,256]{1,0:T(8,128)(2,1)}, u32[]{:S(2)}) copy-start(bf16[4096,256]{1,0:T(8,128)(2,1)} %param.14) | copy-start | bytes 6291460
  8.7 13.7 %all-to-all-start = ((s32[16,1,8]{2,1,0:T(1,128)}), s32[16,1,8]{2,1,0:T(1,128)S(1)}, u32[]{:S(2)}, u32[]{:S(2)}) async-start(s32[16,1,8]{2,1,0:T(1,128)} %copy.48), calls=%async_computation | async-start | bytes 16384 | tf_op jit(solution)/shard_map/all_to_all | solution.py:98
  20.8 29.4 %copy-start.36 = (bf16[4,256,256]{1,2,0:T(8,128)(2,1)}, bf16[4,256,256]{1,2,0:T(8,128)(2,1)S(1)}, u32[]{:S(2)}) copy-start(bf16[4,256,256]{1,2,0:T(8,128)(2,1)S(1)} %get-tuple-element.52) | copy-start | bytes 1572868
  24.3 11.3 %all-to-all-start.1 = ((bf16[16,8,256]{2,1,0:T(8,128)(2,1)}), bf16[16,8,256]{2,1,0:T(8,128)(2,1)S(1)}, u32[]{:S(2)}, u32[]{:S(2)}) async-start(bf16[16,8,256]{2,1,0:T(8,128)(2,1)} %bitcast_select_fusion), calls=%async_computation.1 | async-start | bytes 131072 | tf_op jit(solution)/shard_map/all_to_all | solution.py:101
  28.7 178.4 %reduce-scatter.10.cloned.1.call-start = ((), (), s32[]{:S(2)}) async-start(), calls=%async_computation.9 | async-start | bytes 278528 | tf_op jit(solution)/shard_map/reduce_scatter | solution.py:110
  35.6 3.9 copy-start.45
  35.6 4.3 copy-start.39
  50.2 2.3 copy-start.10
  50.2 2.3 copy-start.12
  50.2 11.4 %copy-start.25 = (bf16[4,256,1,8,32]{1,0,4,3,2:T(4,128)(2,1)}, bf16[4,256,1,8,32]{1,0,4,3,2:T(4,128)(2,1)S(1)}, u32[]{:S(2)}) copy-start(bf16[4,256,1,8,32]{1,0,4,3,2:T(4,128)(2,1)S(1)} %get-tuple-element.32) | copy-start | bytes 1572868
  51.1 1.4 copy-start.14
  53.8 3.2 copy-start.2
  61.6 2.0 copy-start.4
  63.5 1.3 copy-start.37
  64.0 0.8 copy-start.17
  65.8 10.2 %copy-start.5 = (f32[1024,256]{1,0:T(8,128)}, f32[1024,256]{1,0:T(8,128)S(1)}, u32[]{:S(2)}) copy-start(f32[1024,256]{1,0:T(8,128)S(1)} %get-tuple-element.50) | copy-start | bytes 3145732
  65.8 10.1 %copy-start.34 = (bf16[256,512]{1,0:T(8,128)(2,1)S(1)}, bf16[256,512]{1,0:T(8,128)(2,1)}, u32[]{:S(2)}) copy-start(bf16[256,512]{1,0:T(8,128)(2,1)} %param.23) | copy-start | bytes 786436
  76.0 2.1 copy-start.19
  76.0 1.1 copy-start.43
  77.1 1.3 copy-start.28
  78.4 1.0 copy-start.8
  79.7 4.0 copy-start.41
  81.8 2.3 copy-start.42
  84.0 38.3 %copy-start.40 = (f32[4,64]{1,0:T(4,128)}, f32[4,64]{1,0:T(4,128)S(1)}, u32[]{:S(2)}) copy-start(f32[4,64]{1,0:T(4,128)S(1)} %multiply_reduce_fusion.4) | copy-start | bytes 3076
  122.3 1.8 copy-start.9
  124.1 1.6 copy-start.29
  124.1 1.6 copy-start.44
  124.8 2.8 copy-start.21
  125.7 2.0 copy-start.35
  127.6 1.3 copy-start.23
  127.6 1.6 copy-start.6
  128.9 1.7 copy-start.33
  130.7 2.9 copy-start.38
  133.6 1.8 copy-start.15
  134.1 4.5 %copy-start.18 = (bf16[32,8,4,256]{3,1,2,0:T(8,128)(2,1)S(1)}, bf16[32,8,4,256]{3,1,2,0:T(8,128)(2,1)}, u32[]{:S(2)}) copy-start(bf16[32,8,4,256]{3,1,2,0:T(8,128)(2,1)} %copy-done.17) | copy-start | bytes 1572868
  135.4 4.5 %copy-start.26 = (bf16[4,256,1,8,32]{1,0,4,3,2:T(4,128)(2,1)S(1)}, bf16[4,256,1,8,32]{1,0,4,3,2:T(4,128)(2,1)}, u32[]{:S(2)}) copy-start(bf16[4,256,1,8,32]{1,0,4,3,2:T(4,128)(2,1)} %copy-done.25) | copy-start | bytes 1572868
  138.6 111.3 %reduce-scatter.8.cloned.1.call-start = ((), (), s32[]{:S(2)}) async-start(), calls=%async_computation.8 | async-start | bytes 278528 | tf_op jit(solution)/shard_map/reduce_scatter | solution.py:109
  139.8 169.0 %reduce-scatter.12.cloned.1.call-start = ((), (), s32[]{:S(2)}) async-start(), calls=%async_computation.10 | async-start | bytes 557056 | tf_op jit(solution)/shard_map/reduce_scatter | solution.py:111
  139.9 6.9 %copy-start.20 = (bf16[1024,256]{1,0:T(8,128)(2,1)S(1)}, bf16[1024,256]{1,0:T(8,128)(2,1)}, u32[]{:S(2)}) copy-start(bf16[1024,256]{1,0:T(8,128)(2,1)} %copy-done.19) | copy-start | bytes 1572868
  139.9 6.9 %copy-start.24 = (bf16[1024,512]{1,0:T(8,128)(2,1)S(1)}, bf16[1024,512]{1,0:T(8,128)(2,1)}, u32[]{:S(2)}) copy-start(bf16[1024,512]{1,0:T(8,128)(2,1)} %copy-done.23) | copy-start | bytes 3145732
  148.0 220.1 %reduce-scatter.14.cloned.1.call-start = ((), (), s32[]{:S(2)}) async-start(), calls=%async_computation.11 | async-start | bytes 557056 | tf_op jit(solution)/shard_map/reduce_scatter | solution.py:112
  148.1 6.4 %copy-start.7 = (pred[4,8,256,256]{2,3,1,0:T(32,128)(4,1)S(1)}, pred[4,8,256,256]{2,3,1,0:T(32,128)(4,1)}, u32[]{:S(2)}) copy-start(pred[4,8,256,256]{2,3,1,0:T(32,128)(4,1)} %get-tuple-element.20) | copy-start | bytes 6291460
  148.1 6.4 %copy-start.13 = (bf16[4,256,1,8,32]{1,0,4,3,2:T(4,128)(2,1)S(1)}, bf16[4,256,1,8,32]{1,0,4,3,2:T(4,128)(2,1)}, u32[]{:S(2)}) copy-start(bf16[4,256,1,8,32]{1,0,4,3,2:T(4,128)(2,1)} %copy-done.12) | copy-start | bytes 1572868
  154.4 4.1 copy-start.3
  154.5 4.1 copy-start.22
  154.5 4.2 copy-start.30
  158.7 1.8 copy-start.11
  160.5 6.1 %copy-start.27 = (bf16[4,256,8,32]{1,0,3,2:T(4,128)(2,1)S(1)}, bf16[4,256,8,32]{1,0,3,2:T(4,128)(2,1)}, u32[]{:S(2)}) copy-start(bf16[4,256,8,32]{1,0,3,2:T(4,128)(2,1)} %reshape.258) | copy-start | bytes 1572868
  166.5 3.7 copy-start.31
  166.6 3.7 copy-start.32
  166.6 261.0 %reduce-scatter.6.cloned.1.call-start = ((), (), s32[]{:S(2)}) async-start(), calls=%async_computation.7 | async-start | bytes 835584 | tf_op jit(solution)/shard_map/reduce_scatter | solution.py:108
  171.8 1.0 copy-start.16
  171.8 255.8 %copy-start.1 = (bf16[4096,256]{1,0:T(8,128)(2,1)S(1)}, bf16[4096,256]{1,0:T(8,128)(2,1)}, u32[]{:S(2)}) copy-start(bf16[4096,256]{1,0:T(8,128)(2,1)} %param.14) | copy-start | bytes 6291460
  172.2 2.2 copy-start.46
Sparse Core Ops, SparseCore 0:
  138.7 52.6 reduce-scatter.9
  195.5 54.3 reduce-scatter.7
  253.9 54.8 reduce-scatter.11
  313.2 54.8 reduce-scatter.13
  372.1 55.4 reduce-scatter.5
where the time goes:
time: 443 us; the launch traced here: 435 us
  waiting for transfers between devices  229 us (52%)
  other arithmetic  73.8 us (17%)
  matrix products  40.4 us (9%)
  local copies, waits for them, and re-layouts  33.5 us (8%)
  blocking collectives  30.4 us (7%)
  between operations  15.7 us (4%)
  starting transfers between devices  12 us (3%)
    reduce_scatter x1, waiting for transfers between devices, shards(): lax.psum_scatter(terms[0], 'store', scatter_dimension=0, tiled=True)  59.5 us
    reduce_scatter x1, waiting for transfers between devices, shards(): lax.psum_scatter(terms[4], 'store', scatter_dimension=0, tiled=True)  59.2 us
    reduce_scatter x1, waiting for transfers between devices, shards(): lax.psum_scatter(terms[3], 'store', scatter_dimension=0, tiled=True)  59 us
    reduce_scatter x1, waiting for transfers between devices, shards(): lax.psum_scatter(terms[1], 'store', scatter_dimension=0, tiled=True)  42.7 us
    add_any x2, other arithmetic, objective_of(): left = jnp.take_along_axis(out, pairs[:, :, 0][:, :, None], axis=1)  36.6 us
    unnamed x1, blocking collectives  30.4 us
    dot_general x3, matrix products, objective_of(): jnp.einsum('bhqk,bkhd->bqhd', probs, values, preferred_element_type=jnp.f...  11.1 us
    unnamed x102, local copies, waits for them, and re-layouts  10.1 us
  transfers between devices with their start and end apart: 7, of which 6 were waited for; matrix products, arithmetic and copies ran while one was open for 9% of the time, Pallas kernels for 0%

commit v1 on v0

v1 whole, which is shorter than its diff:
```python
import jax
import jax.numpy as jnp
from jax import lax
from jax.experimental import pallas as pl
from jax.experimental.pallas import tpu as pltpu
from jax.sharding import PartitionSpec as P

HEADS = 8
BF = jnp.bfloat16
F32 = jnp.float32


def _nn(a, b):
    return lax.dot_general(a, b, (((1,), (0,)), ((), ())), preferred_element_type=F32)


def _nt(a, b):
    return lax.dot_general(a, b, (((1,), (1,)), ((), ())), preferred_element_type=F32)


def _tn(a, b):
    return lax.dot_general(a, b, (((0,), (0,)), ((), ())), preferred_element_type=F32)


def _split(v):
    hi = v.astype(BF)
    lo = (v - hi.astype(F32)).astype(BF)
    return hi, lo


def _norm(v):
    c = v - jnp.mean(v, axis=0, keepdims=True)
    r = lax.rsqrt(jnp.mean(c * c, axis=0, keepdims=True) + 1e-05)
    return c * r, r


def _norm_back(d, y, r):
    m1 = jnp.mean(d, axis=0, keepdims=True)
    m2 = jnp.mean(d * y, axis=0, keepdims=True)
    return (d - m1 - y * m2) * r


GELU_C = 0.7978845608028654
GELU_A = 0.044715
LOG2E = 1.4426950408889634


def _step_kernel(
    slots_ref, edges_ref, pairs_ref, targets_ref, fetched_ref,
    wqkv_ref, wo_ref, wmsg_ref, wup_ref, wdown_ref, wread_ref,
    preds_ref, obj_ref, gqkv_ref, go_ref, gmsg_ref, gup_ref, gdown_ref,
    wqmT, woT, wupT, wdownT, fetT, wcol, pf_s, y_s, dy_s, att_s,
    acc_qm, acc_o, acc_up, acc_down,
):
    b = pl.program_id(0)
    subs = pl.num_programs(0)
    feats = wo_ref.shape[0]
    nodes = slots_ref.shape[1]
    rows = fetched_ref.shape[0]
    n_edges = edges_ref.shape[2]
    n_pairs = pairs_ref.shape[2]
    hd = feats // HEADS
    scale = hd ** -0.5
    n_all = subs_static(preds_ref) * n_pairs

    @pl.when(b == 0)
    def _():
        wqmT[0 : 3 * feats, :] = wqkv_ref[...].T
        wqmT[3 * feats : 4 * feats, :] = wmsg_ref[...].T
        woT[...] = wo_ref[...].T
        wupT[...] = wup_ref[...].T
        wdownT[...] = wdown_ref[...].T
        fetT[...] = fetched_ref[...].T
        wcol[...] = jnp.broadcast_to(wread_ref[...], (2 * n_pairs, feats)).T
        acc_qm[...] = jnp.zeros_like(acc_qm)
        acc_o[...] = jnp.zeros_like(acc_o)
        acc_up[...] = jnp.zeros_like(acc_up)
        acc_down[...] = jnp.zeros_like(acc_down)
        obj_ref[...] = jnp.zeros_like(obj_ref)

    slot = slots_ref[pl.ds(b, 1), :]
    pick = (lax.broadcasted_iota(jnp.int32, (rows, nodes), 0) == slot).astype(F32).astype(BF)
    xT = _nn(fetT[...], pick).astype(BF)
    base = xT.astype(F32)
    y_s[...] = _nn(wqmT[...], xT).astype(BF)
    src = edges_ref[0, 0:1, :]
    dst = edges_ref[0, 1:2, :]
    it = lax.broadcasted_iota(jnp.int32, (nodes, n_edges), 0)
    srcT = (it == src).astype(F32).astype(BF)
    dstT = (it == dst).astype(F32).astype(BF)
    cnt = _nt(srcT, dstT)
    deg_inv = 1.0 / (1.0 + jnp.sum(cnt, axis=0, keepdims=True))
    adjT = cnt.astype(BF)
    xw = y_s[3 * feats : 4 * feats, :]
    agg = (_nn(xw, adjT) + xw.astype(F32)) * deg_inv
    for h in range(HEADS):
        qT = y_s[h * hd : (h + 1) * hd, :]
        kT = y_s[feats + h * hd : feats + (h + 1) * hd, :]
        vT = y_s[2 * feats + h * hd : 2 * feats + (h + 1) * hd, :]
        s = _tn(kT, qT)
        e = jnp.exp2((s - jnp.max(s, axis=0, keepdims=True)) * (scale * LOG2E))
        pf = e * (1.0 / jnp.sum(e, axis=0, keepdims=True))
        pf_s[h] = pf
        att_s[h * hd : (h + 1) * hd, :] = _nn(vT, pf.astype(BF)).astype(BF)
    attT = att_s[...]
    n1, r1 = _norm(base + jnp.maximum(agg, 0.0))
    n2, r2 = _norm(base + _nn(woT[...], attT))
    hT = (n1 + n2).astype(BF)
    up = _nn(wupT[...], hT)
    th = jnp.tanh(GELU_C * (up + GELU_A * (up * up * up)))
    half = 0.5 * (1.0 + th)
    gT = (up * half).astype(BF)
    dgelu = half + 0.5 * up * (1.0 - th * th) * (GELU_C * (1.0 + (3.0 * GELU_A) * (up * up)))
    out, r3 = _norm(hT.astype(F32) + _nn(wdownT[...], gT))
    prs = jnp.concatenate([pairs_ref[0, 0:1, :], pairs_ref[0, 1:2, :]], axis=1)
    hot = (lax.broadcasted_iota(jnp.int32, (nodes, 2 * n_pairs), 0) == prs).astype(F32).astype(BF)
    hi, lo = _split(out)
    lr = _nn(hi, hot) + _nn(lo, hot)
    rl = pltpu.roll(lr, n_pairs, 1) * wcol[...]
    preds = jnp.sum(lr * rl, axis=0, keepdims=True)
    tgt = targets_ref[pl.ds(b, 1), :]
    diff = preds - jnp.concatenate([tgt, tgt], axis=1)
    preds_ref[pl.ds(b, 1), :] = preds[:, 0:n_pairs]
    sq = diff[:, 0:n_pairs] * diff[:, 0:n_pairs]
    obj_ref[...] += jnp.broadcast_to(jnp.sum(sq, axis=1, keepdims=True) / n_all, obj_ref.shape)
    dlr = (diff * (2.0 / n_all)) * rl
    hi, lo = _split(dlr)
    dout = _nt(hi, hot) + _nt(lo, hot)
    do = _norm_back(dout, out, r3).astype(BF)
    dg = _nn(wdown_ref[...], do).astype(BF)
    acc_down[...] += _nt(gT, do)
    dup = (dgelu * dg.astype(F32)).astype(BF)
    acc_up[...] += _nt(hT, dup)
    dh = _nn(wup_ref[...], dup).astype(BF)
    dl = (do.astype(F32) + dh.astype(F32)).astype(BF).astype(F32)
    dagg = jnp.where(agg > 0.0, _norm_back(dl, n1, r1), 0.0) * deg_inv
    dagg = dagg.astype(BF)
    dxw = _nt(dagg, adjT).astype(BF)
    dy_s[3 * feats : 4 * feats, :] = (dxw.astype(F32) + dagg.astype(F32)).astype(BF)
    da = _norm_back(dl, n2, r2).astype(BF)
    acc_o[...] += _nt(attT, da)
    datt = _nn(wo_ref[...], da).astype(BF)
    for h in range(HEADS):
        qT = y_s[h * hd : (h + 1) * hd, :]
        kT = y_s[feats + h * hd : feats + (h + 1) * hd, :]
        vT = y_s[2 * feats + h * hd : 2 * feats + (h + 1) * hd, :]
        dh_ = datt[h * hd : (h + 1) * hd, :]
        pf = pf_s[h]
        dp = _tn(vT, dh_).astype(BF).astype(F32)
        dv = _nt(dh_, pf.astype(BF)).astype(BF)
        t = dp * pf
        ds = ((t - pf * jnp.sum(t, axis=0, keepdims=True)) * scale).astype(BF)
        dy_s[h * hd : (h + 1) * hd, :] = _nn(kT, ds).astype(BF)
        dy_s[feats + h * hd : feats + (h + 1) * hd, :] = _nt(qT, ds).astype(BF)
        dy_s[2 * feats + h * hd : 2 * feats + (h + 1) * hd, :] = dv
    acc_qm[...] += _nt(xT, dy_s[...])

    @pl.when(b == subs - 1)
    def _():
        gqkv_ref[...] = acc_qm[:, 0 : 3 * feats].astype(BF)
        gmsg_ref[...] = acc_qm[:, 3 * feats : 4 * feats].astype(BF)
        go_ref[...] = acc_o[...].astype(BF)
        gup_ref[...] = acc_up[...].astype(BF)
        gdown_ref[...] = acc_down[...].astype(BF)


def subs_static(ref):
    return ref.shape[0]


def local_step(fetched, node_slots, edges, pairs, targets, w_qkv, w_o, w_msg, w_up, w_down, w_read):
    subs, nodes = node_slots.shape
    rows, feats = fetched.shape
    hidden = w_up.shape[1]
    n_edges = edges.shape[1]
    n_pairs = pairs.shape[1]

    def whole(shape):
        return pl.BlockSpec(shape, lambda b: (0,) * len(shape))

    return pl.pallas_call(
        _step_kernel,
        grid=(subs,),
        in_specs=[
            whole((subs, nodes)),
            pl.BlockSpec((1, 2, n_edges), lambda b: (b, 0, 0)),
            pl.BlockSpec((1, 2, n_pairs), lambda b: (b, 0, 0)),
            whole((subs, n_pairs)),
            whole((rows, feats)),
            whole((feats, 3 * feats)),
            whole((feats, feats)),
            whole((feats, feats)),
            whole((feats, hidden)),
            whole((hidden, feats)),
            whole((1, feats)),
        ],
        out_specs=[
            whole((subs, n_pairs)),
            whole((8, 128)),
            whole((feats, 3 * feats)),
            whole((feats, feats)),
            whole((feats, feats)),
            whole((feats, hidden)),
            whole((hidden, feats)),
        ],
        out_shape=[
            jax.ShapeDtypeStruct((subs, n_pairs), F32),
            jax.ShapeDtypeStruct((8, 128), F32),
            jax.ShapeDtypeStruct((feats, 3 * feats), BF),
            jax.ShapeDtypeStruct((feats, feats), BF),
            jax.ShapeDtypeStruct((feats, feats), BF),
            jax.ShapeDtypeStruct((feats, hidden), BF),
            jax.ShapeDtypeStruct((hidden, feats), BF),
        ],
        scratch_shapes=[
            pltpu.VMEM((4 * feats, feats), BF),
            pltpu.VMEM((feats, feats), BF),
            pltpu.VMEM((hidden, feats), BF),
            pltpu.VMEM((feats, hidden), BF),
            pltpu.VMEM((feats, rows), BF),
            pltpu.VMEM((feats, 2 * n_pairs), F32),
            pltpu.VMEM((HEADS, nodes, nodes), F32),
            pltpu.VMEM((4 * feats, nodes), BF),
            pltpu.VMEM((4 * feats, nodes), BF),
            pltpu.VMEM((feats, nodes), BF),
            pltpu.VMEM((feats, 4 * feats), F32),
            pltpu.VMEM((feats, feats), F32),
            pltpu.VMEM((feats, hidden), F32),
            pltpu.VMEM((hidden, feats), F32),
        ],
        compiler_params=pltpu.CompilerParams(
            dimension_semantics=("arbitrary",), vmem_limit_bytes=48 << 20
        ),
        name="graph_step",
    )(
        node_slots, edges.transpose(0, 2, 1), pairs.transpose(0, 2, 1), targets, fetched,
        w_qkv, w_o, w_msg, w_up, w_down, w_read.reshape(1, feats),
    )


def _halving(parts, obj, groups):
    idx = lax.axis_index("store")
    bits = groups.bit_length() - 1
    c = jnp.concatenate(parts, axis=2)
    tail = c.shape[1:]
    y = c.reshape((2,) * bits + tail)
    for b in range(bits):
        ax = bits - 1 - b
        bit = (idx >> b) & 1
        perm = [(i, i ^ (1 << b)) for i in range(groups)]
        send = lax.dynamic_slice_in_dim(y, 1 - bit, 1, ax).astype(BF)
        got = lax.ppermute(send, "store", perm)
        obj = obj + lax.ppermute(obj, "store", perm)
        y = lax.dynamic_slice_in_dim(y, bit, 1, ax).astype(F32) + got.astype(F32)
    return y.reshape(tail), obj


def shards(
    store_feats, requests, node_slots, edges, pairs, targets,
    w_qkv, w_o, w_msg, w_up, w_down, w_read,
):
    feats = store_feats.shape[1]
    groups = lax.axis_size("store")
    picked = jnp.take(
        store_feats,
        lax.all_to_all(requests, "store", split_axis=0, concat_axis=0, tiled=True),
        axis=0,
        mode="clip",
    )
    fetched = lax.all_to_all(picked, "store", split_axis=0, concat_axis=0, tiled=True)
    preds, obj, *grads = local_step(
        fetched.reshape(-1, feats), node_slots, edges, pairs, targets,
        w_qkv, w_o, w_msg, w_up, w_down, w_read,
    )
    power = groups & (groups - 1) == 0
    if power and all(g.shape[0] % groups == 0 for g in grads):
        rows = feats // groups
        parts = [g.reshape(groups, -1, g.shape[1]) for g in grads]
        split = []
        for p in parts:
            split += [p[:, i : i + rows] for i in range(0, p.shape[1], rows)]
        total, obj = _halving(split, obj, groups)
        at, shares = 0, []
        for p in parts:
            pieces = []
            for _ in range(0, p.shape[1], rows):
                pieces.append(total[:, at : at + p.shape[2]])
                at += p.shape[2]
            shares.append(pieces[0] if len(pieces) == 1 else jnp.concatenate(pieces, axis=0))
        total_obj = obj[0, 0]
    else:
        shares = [
            lax.psum_scatter(g.astype(F32), "store", scatter_dimension=0, tiled=True)
            for g in grads
        ]
        total_obj = lax.psum(obj[0, 0], "store")
    loss = (total_obj / groups).reshape(1)
    return (preds, loss, *shares)


def solution(mesh):
    rows = P(("parts", "store"), None)
    deep = P(("parts", "store"), None, None)
    in_specs = (rows, rows, rows, deep, deep, rows, P(), P(), P(), P(), P(), P())
    out_specs = (rows, P("parts"), rows, rows, rows, rows, rows)
    return jax.shard_map(shards, mesh=mesh, in_specs=in_specs, out_specs=out_specs, check_vma=False)
```

time: 443 us -> 110 us (0.25); the launches traced: 435 us -> 109 us
  waiting for transfers between devices: 229 us -> 31.9 us
  other arithmetic: 73.8 us -> 4.7 us
  matrix products: 40.4 us -> 0 us
  Pallas kernels: 0 us -> 31.6 us
  local copies, waits for them, and re-layouts: 33.5 us -> 16.3 us
  blocking collectives: 30.4 us -> 13.6 us
  between operations: 15.7 us -> 2.6 us
    reduce_scatter x5 -> x0, waiting for transfers between devices: 220 us -> none  [the longest x1 59.5 us: shards(): lax.psum_scatter(terms[0], 'store', scatter_dimension=0, tiled=True)]
    dot_general x21 -> x0, matrix products: 40.4 us -> none  [the longest x3 11.1 us: objective_of(): jnp.einsum('bhqk,bkhd->bqhd', probs, values, preferred_element_type=jnp.f...]
    add_any x4 -> x0, other arithmetic: 37.3 us -> none  [the longest x2 36.6 us: objective_of(): left = jnp.take_along_axis(out, pairs[:, :, 0][:, :, None], axis=1)]
    pallas_call x0 -> x1, Pallas kernels: none -> 31.6 us  [local_step(): pl.pallas_call(_step_kernel, grid=(subs,), in_specs=[whole((subs, nodes))...]
    unnamed x1 -> x0, blocking collectives: 30.4 us -> none
    ppermute x0 -> x8, waiting for transfers between devices: none -> 25.1 us  [the longest x4 16.4 us: _halving(): got = lax.ppermute(send, 'store', perm)]
    reduce_sum x11 -> x0, other arithmetic: 20.4 us -> none  [the longest x1 6.3 us: objective_of(): expo = jnp.exp(scores - top)]
    all_to_all x0 -> x1, blocking collectives: none -> 13.6 us  [shards(): lax.all_to_all(requests, 'store', split_axis=0, concat_axis=0, tiled=True)]
  transfers between devices with their start and end apart: 7 -> 9, of which waited for: 6 -> 8; matrix products, arithmetic and copies ran while one was open for 9% -> 0% of each run, Pallas kernels for 0% -> 0%
where the time goes in v1:
time: 110 us; the launch traced here: 109 us
  waiting for transfers between devices  31.9 us (29%)
  Pallas kernels  31.6 us (29%)
  local copies, waits for them, and re-layouts  16.3 us (15%)
  blocking collectives  13.6 us (12%)
  starting transfers between devices  8.35 us (8%)
  other arithmetic  4.7 us (4%)
  between operations  2.6 us (2%)
    pallas_call x1, Pallas kernels, local_step(): pl.pallas_call(_step_kernel, grid=(subs,), in_specs=[whole((subs, nodes))...  31.6 us
    ppermute x4, waiting for transfers between devices, _halving(): got = lax.ppermute(send, 'store', perm)  16.4 us
    all_to_all x1, blocking collectives, shards(): lax.all_to_all(requests, 'store', split_axis=0, concat_axis=0, tiled=True)  13.6 us
    unnamed x31, local copies, waits for them, and re-layouts  10.1 us
    ppermute x4, waiting for transfers between devices, _halving(): obj = obj + lax.ppermute(obj, 'store', perm)  8.69 us
    all_to_all x1, waiting for transfers between devices, shards(): lax.all_to_all(picked, 'store', split_axis=0, concat_axis=0, tiled=True)  6.85 us
    ppermute x4, starting transfers between devices, _halving(): obj = obj + lax.ppermute(obj, 'store', perm)  4.2 us
    all_to_all x1, starting transfers between devices, shards(): lax.all_to_all(picked, 'store', split_axis=0, concat_axis=0, tiled=True)  3.49 us
  transfers between devices with their start and end apart: 9, of which 8 were waited for; matrix products, arithmetic and copies ran while one was open for 0% of the time, Pallas kernels for 0%

profile of v1, /device:TPU:0, one launch (start us, length us, event | category | flops | bytes accessed | tf_op | source)
XLA Modules:
  0.0 109.1 jit_solution(1361507816017839781)
XLA Ops:
  0.6 0.0 copy-start
  0.6 0.9 copy.21
  1.6 13.6 %all_to_all.14 = s32[16,1,8]{2,1,0:T(1,128)S(1)} all-to-all(s32[16,1,8]{2,1,0:T(1,128)S(1)} %copy.21), channel_id=1, replica_groups=mesh['parts'=2,'store'=16] {'store'}, dimensions={0} | all-to-all | bytes 1024 | tf_op jit(solution)/shard_map/all_to_all | solution.py:266
  15.1 0.5 broadcast.7
  15.6 0.7 reduce.3
  16.3 0.1 reshape.57
  16.4 0.0 copy-done
  16.4 1.5 %gather_fusion = bf16[128,256]{1,0:T(8,128)(2,1)} fusion(bf16[4096,256]{1,0:T(8,128)(2,1)S(1)} %copy-done, s32[1024]{0:T(1024)S(1)} %pad_clamp_fusion), kind=kCustom, calls=%fused_computation | custom fusion | bytes 131584 | tf_op jit(solution)/shard_map/jit(_take)/gather | solution.py:264
  17.9 3.5 %all-to-all-start.1 = ((bf16[16,8,256]{2,1,0:T(8,128)(2,1)}), bf16[16,8,256]{2,1,0:T(8,128)(2,1)S(1)}, u32[]{:S(2)}, u32[]{:S(2)}) async-start(bf16[16,8,256]{2,1,0:T(8,128)(2,1)} %bitcast.3), calls=%async_computation.1 | async-start | bytes 131072 | tf_op jit(solution)/shard_map/all_to_all | solution.py:270
  21.4 6.9 %all-to-all-done.1 = bf16[16,8,256]{2,1,0:T(8,128)(2,1)S(1)} async-done(((bf16[16,8,256]{2,1,0:T(8,128)(2,1)}), bf16[16,8,256]{2,1,0:T(8,128)(2,1)S(1)}, u32[]{:S(2)}, u32[]{:S(2)}) %all-to-all-start.1) | async-done | bytes 65568 | tf_op jit(solution)/shard_map/all_to_all | solution.py:270
  28.3 0.0 copy-start.1
  28.3 1.0 copy-done.1
  29.3 0.0 copy-start.2
  29.3 0.9 copy-done.2
  30.2 0.0 copy-start.3
  30.2 0.9 copy-done.3
  31.2 0.0 copy-start.4
  31.2 0.9 copy-done.4
  32.1 0.0 copy-start.5
  32.1 0.9 copy-done.5
  33.0 0.0 copy-start.6
  33.0 0.8 copy-done.6
  33.7 0.0 copy-start.7
  33.7 0.7 copy-done.7
  34.4 0.0 copy-start.8
  34.4 0.7 copy-done.8
  35.1 0.0 copy-start.9
  35.1 0.7 copy-done.9
  35.8 0.0 copy-start.10
  35.8 0.7 copy-done.10
  36.5 31.6 %graph_step.1 = (f32[4,64]{1,0:T(4,128)}, f32[8,128]{1,0:T(8,128)S(1)}, bf16[256,768]{1,0:T(8,128)(2,1)S(1)}, bf16[256,256]{1,0:T(8,128)(2,1)S(1)}, bf16[256,256...) custom-call(s32[4,256]{1,0:T(4,128)S(1)} %copy-done.7, s32[4,2,1024]{2,1,0:T(2,128)S(1)} %bitcast.22, ...), custom_call_target="tpu_custom_call" | custom-call | tf_op jit(solution)/shard_map/graph_step/pallas_call | solution.py:181
  68.2 0.0 copy-start.11
  68.2 1.0 copy-done.11
  69.3 0.1 collective-permute-start.4
  69.4 2.1 %collective-permute-done.4 = bf16[2,2,2,1,16,2304]{5,4,3,2,1,0:T(8,128)(2,1)} collective-permute-done((bf16[2,2,2,1,16,2304]{5,4,3,2,1,0:T(8,128)(2,1)S(1)}, bf16[2,2,2,1,16,2304]{5,4,3,2,1,0:T(8,128)(2,1)}, u32[]{:S(2)}, u32[]{:S(2)}) %collective-permute-start.4) | collective-permute-done | bytes 589856 | tf_op jit(solution)/shard_map/ppermute | solution.py:252
  71.5 1.4 %convert_add_fusion = f32[2,2,2,1,16,2304]{5,4,3,2,1,0:T(8,128)S(1)} fusion(bf16[2,2,2,1,16,2304]{5,4,3,2,1,0:T(8,128)(2,1)} %collective-permute-done.4, bf16[2,2,2,2,16,2304]{5,4,3,2,1,0:T(8,128)(2,1)} %copy-done.11, s32[]{:T(128)S(6)} %select_n.24), kind=kLoop, calls=%fused_computation.1 | loop fusion | flops 884736 | bytes 2359300 | tf_op jit(solution)/shard_map/add | solution.py:254
  72.8 0.8 dynamic-slice_convert_fusion
  73.6 0.1 collective-permute-start.5
  73.7 9.3 %collective-permute-done.5 = bf16[2,2,1,1,16,2304]{5,4,3,2,1,0:T(8,128)(2,1)} collective-permute-done((bf16[2,2,1,1,16,2304]{5,4,3,2,1,0:T(8,128)(2,1)}, bf16[2,2,1,1,16,2304]{5,4,3,2,1,0:T(8,128)(2,1)}, u32[]{:S(2)}, u32[]{:S(2)}) %collective-permute-start.5) | collective-permute-done | bytes 294944 | tf_op jit(solution)/shard_map/ppermute | solution.py:252
  83.0 1.0 convert_add_fusion.1
  84.0 0.0 copy-start.12
  84.0 0.8 copy-done.12
  84.8 0.2 collective-permute-start.6
  85.0 5.0 %collective-permute-done.6 = bf16[2,1,1,1,16,2304]{5,4,3,2,1,0:T(8,128)(2,1)S(1)} collective-permute-done((bf16[2,1,1,1,16,2304]{5,4,3,2,1,0:T(8,128)(2,1)S(1)}, bf16[2,1,1,1,16,2304]{5,4,3,2,1,0:T(8,128)(2,1)S(1)}, u32[]{:S(2)}, u32[]{:S(2)}) %collective-permute-start.6) | collective-permute-done | bytes 147488 | tf_op jit(solution)/shard_map/ppermute | solution.py:252
  90.1 1.0 convert_add_fusion.2
  91.1 0.3 collective-permute-start.7
  91.4 0.0 collective-permute-start
  91.4 1.2 %collective-permute-done = f32[8,128]{1,0:T(8,128)S(1)} collective-permute-done((f32[8,128]{1,0:T(8,128)S(1)}, f32[8,128]{1,0:T(8,128)S(1)}, u32[]{:S(2)}, u32[]{:S(2)}) %collective-permute-start) | collective-permute-done | bytes 4128 | tf_op jit(solution)/shard_map/ppermute | solution.py:253
  92.5 0.6 collective-permute-start.1
  93.2 3.0 %collective-permute-done.1 = f32[8,128]{1,0:T(8,128)S(1)} collective-permute-done((f32[8,128]{1,0:T(8,128)S(1)}, f32[8,128]{1,0:T(8,128)S(1)}, u32[]{:S(2)}, u32[]{:S(2)}) %collective-permute-start.1) | collective-permute-done | bytes 4128 | tf_op jit(solution)/shard_map/ppermute | solution.py:253
  96.1 0.9 collective-permute-start.2
  97.0 2.8 %collective-permute-done.2 = f32[8,128]{1,0:T(8,128)S(1)} collective-permute-done((f32[8,128]{1,0:T(8,128)S(1)}, f32[8,128]{1,0:T(8,128)S(1)}, u32[]{:S(2)}, u32[]{:S(2)}) %collective-permute-start.2) | collective-permute-done | bytes 4128 | tf_op jit(solution)/shard_map/ppermute | solution.py:253
  99.8 2.7 %collective-permute-start.3 = (f32[8,128]{1,0:T(8,128)S(1)}, f32[8,128]{1,0:T(8,128)S(1)}, u32[]{:S(2)}, u32[]{:S(2)}) collective-permute-start(f32[8,128]{1,0:T(8,128)S(1)} %add.54), channel_id=1, source_target_pairs={{0,8},{1,9},{2,10},{3,11},{4,12},{5,13},{6,14},{7,15},{8,0},{9,1},... | collective-permute-start | bytes 12296 | tf_op jit(solution)/shard_map/ppermute | solution.py:253
  102.5 1.8 %collective-permute-done.3 = f32[8,128]{1,0:T(8,128)S(1)} collective-permute-done((f32[8,128]{1,0:T(8,128)S(1)}, f32[8,128]{1,0:T(8,128)S(1)}, u32[]{:S(2)}, u32[]{:S(2)}) %collective-permute-start.3) | collective-permute-done | bytes 4128 | tf_op jit(solution)/shard_map/ppermute | solution.py:253
  104.3 0.5 slice.27
  105.4 0.0 collective-permute-done.7
  105.5 0.6 slice.40
  106.1 0.6 fusion.1
  106.7 0.6 slice.43
  107.3 0.6 pad_maximum_fusion
  (16 shorter events, 0.2 us)
Async XLA Ops:
  0.6 15.8 %copy-start = (bf16[4096,256]{1,0:T(8,128)(2,1)S(1)}, bf16[4096,256]{1,0:T(8,128)(2,1)}, u32[]{:S(2)}) copy-start(bf16[4096,256]{1,0:T(8,128)(2,1)} %param.12) | copy-start | bytes 6291460
  17.9 10.4 %all-to-all-start.1 = ((bf16[16,8,256]{2,1,0:T(8,128)(2,1)}), bf16[16,8,256]{2,1,0:T(8,128)(2,1)S(1)}, u32[]{:S(2)}, u32[]{:S(2)}) async-start(bf16[16,8,256]{2,1,0:T(8,128)(2,1)} %bitcast.3), calls=%async_computation.1 | async-start | bytes 131072 | tf_op jit(solution)/shard_map/all_to_all | solution.py:270
  28.3 1.0 copy-start.1
  29.3 0.9 copy-start.2
  30.2 0.9 copy-start.3
  31.2 0.9 copy-start.4
  32.1 0.9 copy-start.5
  33.0 0.8 copy-start.6
  33.7 0.7 copy-start.7
  34.4 0.7 copy-start.8
  35.1 0.7 copy-start.9
  35.8 0.7 copy-start.10
  68.2 1.0 copy-start.11
  69.3 2.2 %collective-permute-start.4 = (bf16[2,2,2,1,16,2304]{5,4,3,2,1,0:T(8,128)(2,1)S(1)}, bf16[2,2,2,1,16,2304]{5,4,3,2,1,0:T(8,128)(2,1)}, u32[]{:S(2)}, u32[]{:S(2)}) collective-permute-start(bf16[2,2,2,1,16,2304]{5,4,3,2,1,0:T(8,128)(2,1)S(1)} %constant_dynamic-slice_fusion), channel_id=1, source_target_pairs={{0,1},{1,0},{2,3},{3,2},{4,5},{5,4},{6,7},{7,6},{8,9},{9,8},{10,11... | collective-permute-start | bytes 1769480 | tf_op jit(solution)/shard_map/ppermute | solution.py:252
  73.6 9.4 %collective-permute-start.5 = (bf16[2,2,1,1,16,2304]{5,4,3,2,1,0:T(8,128)(2,1)}, bf16[2,2,1,1,16,2304]{5,4,3,2,1,0:T(8,128)(2,1)}, u32[]{:S(2)}, u32[]{:S(2)}) collective-permute-start(bf16[2,2,1,1,16,2304]{5,4,3,2,1,0:T(8,128)(2,1)} %dynamic-slice_convert_fusion), channel_id=1, source_target_pairs={{0,2},{1,3},{2,0},{3,1},{4,6},{5,7},{6,4},{7,5},{8,10},{9,11},{10,... | collective-permute-start | bytes 884744 | tf_op jit(solution)/shard_map/ppermute | solution.py:252
  84.0 0.8 copy-start.12
  84.8 5.2 %collective-permute-start.6 = (bf16[2,1,1,1,16,2304]{5,4,3,2,1,0:T(8,128)(2,1)S(1)}, bf16[2,1,1,1,16,2304]{5,4,3,2,1,0:T(8,128)(2,1)S(1)}, u32[]{:S(2)}, u32[]{:S(2)}) collective-permute-start(bf16[2,1,1,1,16,2304]{5,4,3,2,1,0:T(8,128)(2,1)S(1)} %dynamic-slice_convert_fusion.1), channel_id=1, source_target_pairs={{0,4},{1,5},{2,6},{3,7},{4,0},{5,1},{6,2},{7,3},{8,12},{9,13},{10,... | collective-permute-start | bytes 442376 | tf_op jit(solution)/shard_map/ppermute | solution.py:252
  91.1 14.4 %collective-permute-start.7 = (bf16[1,1,1,1,16,2304]{5,4,3,2,1,0:T(8,128)(2,1)S(1)}, bf16[1,1,1,1,16,2304]{5,4,3,2,1,0:T(8,128)(2,1)S(1)}, u32[]{:S(2)}, u32[]{:S(2)}) collective-permute-start(bf16[1,1,1,1,16,2304]{5,4,3,2,1,0:T(8,128)(2,1)S(1)} %dynamic-slice_convert_fusion.2), channel_id=1, source_target_pairs={{0,8},{1,9},{2,10},{3,11},{4,12},{5,13},{6,14},{7,15},{8,0},{9,1},... | collective-permute-start | bytes 221192 | tf_op jit(solution)/shard_map/ppermute | solution.py:252
  91.4 1.2 %collective-permute-start = (f32[8,128]{1,0:T(8,128)S(1)}, f32[8,128]{1,0:T(8,128)S(1)}, u32[]{:S(2)}, u32[]{:S(2)}) collective-permute-start(f32[8,128]{1,0:T(8,128)S(1)} %get-tuple-element.15), channel_id=1, source_target_pairs={{0,1},{1,0},{2,3},{3,2},{4,5},{5,4},{6,7},{7,6},{8,9},{9,8},{10,11... | collective-permute-start | bytes 12296 | tf_op jit(solution)/shard_map/ppermute | solution.py:253
  92.5 3.6 %collective-permute-start.1 = (f32[8,128]{1,0:T(8,128)S(1)}, f32[8,128]{1,0:T(8,128)S(1)}, u32[]{:S(2)}, u32[]{:S(2)}) collective-permute-start(f32[8,128]{1,0:T(8,128)S(1)} %add.52), channel_id=1, source_target_pairs={{0,2},{1,3},{2,0},{3,1},{4,6},{5,7},{6,4},{7,5},{8,10},{9,11},{10,... | collective-permute-start | bytes 12296 | tf_op jit(solution)/shard_map/ppermute | solution.py:253
  96.1 3.6 %collective-permute-start.2 = (f32[8,128]{1,0:T(8,128)S(1)}, f32[8,128]{1,0:T(8,128)S(1)}, u32[]{:S(2)}, u32[]{:S(2)}) collective-permute-start(f32[8,128]{1,0:T(8,128)S(1)} %add.53), channel_id=1, source_target_pairs={{0,4},{1,5},{2,6},{3,7},{4,0},{5,1},{6,2},{7,3},{8,12},{9,13},{10,... | collective-permute-start | bytes 12296 | tf_op jit(solution)/shard_map/ppermute | solution.py:253
  99.8 4.5 %collective-permute-start.3 = (f32[8,128]{1,0:T(8,128)S(1)}, f32[8,128]{1,0:T(8,128)S(1)}, u32[]{:S(2)}, u32[]{:S(2)}) collective-permute-start(f32[8,128]{1,0:T(8,128)S(1)} %add.54), channel_id=1, source_target_pairs={{0,8},{1,9},{2,10},{3,11},{4,12},{5,13},{6,14},{7,15},{8,0},{9,1},... | collective-permute-start | bytes 12296 | tf_op jit(solution)/shard_map/ppermute | solution.py:253

commit v2 on v0

v2 whole, which is shorter than its diff:
```python
import jax
import jax.numpy as jnp
from jax import lax
from jax.experimental import pallas as pl
from jax.experimental.pallas import tpu as pltpu
from jax.sharding import PartitionSpec as P

HEADS = 8
BF = jnp.bfloat16
F32 = jnp.float32


def _nn(a, b):
    return lax.dot_general(a, b, (((1,), (0,)), ((), ())), preferred_element_type=F32)


def _nt(a, b):
    return lax.dot_general(a, b, (((1,), (1,)), ((), ())), preferred_element_type=F32)


def _tn(a, b):
    return lax.dot_general(a, b, (((0,), (0,)), ((), ())), preferred_element_type=F32)


def _split(v):
    hi = v.astype(BF)
    lo = (v - hi.astype(F32)).astype(BF)
    return hi, lo


def _norm(v):
    c = v - jnp.mean(v, axis=0, keepdims=True)
    r = lax.rsqrt(jnp.mean(c * c, axis=0, keepdims=True) + 1e-05)
    return c * r, r


def _norm_back(d, y, r):
    m1 = jnp.mean(d, axis=0, keepdims=True)
    m2 = jnp.mean(d * y, axis=0, keepdims=True)
    return (d - m1 - y * m2) * r


GELU_C = 0.7978845608028654
GELU_A = 0.044715
LOG2E = 1.4426950408889634

LANES = 128


def _prep_kernel(
    wqkv_h, wo_h, wmsg_h, wup_h, wdown_h, edges_h, pairs_h, slots_h, wread_h, *refs
):
    results = refs[:9]
    pick, wqmT, adjT, deg, woT, wupT, wdownT, hot, wcol = refs[9:18]
    wqkv, wmsg, wo, wup, wdown, edges, pairs, slots, wread, sems, out_sems = refs[18:]
    moves = [
        (edges_h, edges), (slots_h, slots), (pairs_h, pairs), (wread_h, wread),
        (wqkv_h, wqkv), (wmsg_h, wmsg), (wo_h, wo), (wup_h, wup), (wdown_h, wdown),
    ]
    copies = [pltpu.make_async_copy(s, d, sems.at[i]) for i, (s, d) in enumerate(moves)]
    sends = [
        pltpu.make_async_copy(s, d, out_sems.at[i])
        for i, (s, d) in enumerate(zip(refs[9:18], results))
    ]
    for c in copies:
        c.start()
    feats = wo.shape[0]
    subs, nodes = slots.shape
    rows = pick.shape[0]
    n_edges = edges.shape[2]
    n_pairs = pairs.shape[2]
    for c in copies[:4]:
        c.wait()
    it = lax.broadcasted_iota(jnp.int32, (nodes, n_edges), 0)
    ip = lax.broadcasted_iota(jnp.int32, (nodes, 2 * n_pairs), 0)
    ir = lax.broadcasted_iota(jnp.int32, (rows, nodes), 0)

    @pl.loop(0, subs)
    def _(b):
        e = edges[b]
        srcT = (it == e[0:1, :]).astype(F32).astype(BF)
        dstT = (it == e[1:2, :]).astype(F32).astype(BF)
        cnt = _nt(srcT, dstT)
        deg[pl.ds(b, 1), :] = 1.0 / (1.0 + jnp.sum(cnt, axis=0, keepdims=True))
        adjT[b] = cnt.astype(BF)
        p = pairs[b]
        prs = jnp.concatenate([p[0:1, :], p[1:2, :]], axis=1)
        hot[b] = (ip == prs).astype(F32).astype(BF)
        at = pl.ds(pl.multiple_of(b * nodes, LANES), nodes)
        pick[:, at] = (ir == slots[pl.ds(b, 1), :]).astype(F32).astype(BF)

    wcol[...] = jnp.broadcast_to(wread[...], (2 * n_pairs, feats)).T
    for i in (0, 2, 3, 7, 8):
        sends[i].start()
    for c in copies[4:]:
        c.wait()
    wqmT[0 : 3 * feats, :] = wqkv[...].T
    wqmT[3 * feats : 4 * feats, :] = wmsg[...].T
    sends[1].start()
    woT[...] = wo[...].T
    sends[4].start()
    wupT[...] = wup[...].T
    sends[5].start()
    wdownT[...] = wdown[...].T
    sends[6].start()
    for c in sends:
        c.wait()


def _hbm(*arrays):
    return [pltpu.with_memory_space_constraint(v, pltpu.HBM) for v in arrays]


def _prep(w_qkv, w_o, w_msg, w_up, w_down, edges, pairs, node_slots, w_read, rows):
    feats, hidden = w_up.shape
    subs, nodes = node_slots.shape
    n_edges, n_pairs = edges.shape[1], pairs.shape[1]
    out = [
        ((rows, subs * nodes), BF), ((4 * feats, feats), BF), ((subs, nodes, nodes), BF),
        ((subs, nodes), F32), ((feats, feats), BF), ((hidden, feats), BF), ((feats, hidden), BF),
        ((subs, nodes, 2 * n_pairs), BF), ((feats, 2 * n_pairs), F32),
    ]
    return pl.pallas_call(
        _prep_kernel,
        in_specs=[pl.BlockSpec(memory_space=pltpu.HBM)] * 9,
        out_specs=[pl.BlockSpec(memory_space=pltpu.HBM)] * len(out),
        out_shape=[pltpu.HBM(s, d) for s, d in out],
        scratch_shapes=[pltpu.VMEM(s, d) for s, d in out]
        + [
            pltpu.VMEM((feats, 3 * feats), BF),
            pltpu.VMEM((feats, feats), BF),
            pltpu.VMEM((feats, feats), BF),
            pltpu.VMEM((feats, hidden), BF),
            pltpu.VMEM((hidden, feats), BF),
            pltpu.VMEM((subs, 2, n_edges), jnp.int32),
            pltpu.VMEM((subs, 2, n_pairs), jnp.int32),
            pltpu.VMEM((subs, nodes), jnp.int32),
            pltpu.VMEM((1, feats), F32),
            pltpu.SemaphoreType.DMA((9,)),
            pltpu.SemaphoreType.DMA((9,)),
        ],
        compiler_params=pltpu.CompilerParams(vmem_limit_bytes=24 << 20),
        cost_estimate=pl.CostEstimate(
            flops=2 * subs * nodes * nodes * n_edges, bytes_accessed=8 << 20, transcendentals=0
        ),
        name="prep",
    )(
        *_hbm(
            w_qkv, w_o, w_msg, w_up, w_down, edges.transpose(0, 2, 1),
            pairs.transpose(0, 2, 1), node_slots, w_read.reshape(1, feats),
        )
    )


FWD_GROUP = 1
MID_GROUP = 2
BWD_GROUP = 1


def _over(subs, group, stage):
    if subs % group:
        group = 1
    if group == subs:
        for b in range(subs):
            stage(b)
    else:

        @pl.loop(0, subs // group)
        def _(i):
            for k in range(group):
                stage(i * group + k)


def _step_kernel(packed, *refs):
    fetched_ref = refs[0]
    sources = refs[1:14]
    preds_ref = refs[14]
    outs = refs[15 : 15 + (2 if packed else 6)]
    refs = refs[15 + len(outs) :]
    (
        pick, wqmT, adjT, deg, woT, wupT, wdownT, hot_ref, wcol, targets_ref, wo, wup, wdown,
    ) = refs[:13]
    (
        x_s, y_s, dy_s, att_s, datt_s, h_s, g_s, do_s, dup_s, da_s, pf_s, obj_s, gq_s, gu_s, gd_s,
        sems,
    ) = refs[13:]
    copies = [
        pltpu.make_async_copy(s, d, sems.at[i]) for i, (s, d) in enumerate(zip(sources, refs[:13]))
    ]
    for c in copies:
        c.start()
    feats = wo.shape[0]
    hidden = wup.shape[1]
    subs, nodes = deg.shape
    n_pairs = targets_ref.shape[1]
    n_all = subs * n_pairs
    hd = feats // HEADS
    scale = hd ** -0.5

    def lanes(b):
        if isinstance(b, int):
            return slice(b * nodes, (b + 1) * nodes)
        return pl.ds(pl.multiple_of(b * nodes, LANES), nodes)

    def head(part, h):
        return slice(part * feats + h * hd, part * feats + (h + 1) * hd)

    obj_s[...] = jnp.zeros_like(obj_s)
    fetT = fetched_ref[...].T
    copies[0].wait()
    x_s[...] = _nn(fetT, pick[...]).astype(BF)
    copies[1].wait()
    y_s[...] = _nn(wqmT[...], x_s[...]).astype(BF)

    def attend(b):
        at = lanes(b)
        for h in range(HEADS):
            s = _tn(y_s[head(1, h), at], y_s[head(0, h), at])
            e = jnp.exp2((s - jnp.max(s, axis=0, keepdims=True)) * (scale * LOG2E))
            pf = e * (1.0 / jnp.sum(e, axis=0, keepdims=True))
            pf_s[b, h] = pf
            att_s[head(0, h), at] = _nn(y_s[head(2, h), at], pf.astype(BF)).astype(BF)

    _over(subs, FWD_GROUP, attend)
    for c in copies[2:]:
        c.wait()

    def middle(b):
        at = lanes(b)
        base = x_s[:, at].astype(F32)
        xw = y_s[3 * feats : 4 * feats, at]
        dinv = deg[pl.ds(b, 1), :]
        agg = (_nn(xw, adjT[b]) + xw.astype(F32)) * dinv
        n1, r1 = _norm(base + jnp.maximum(agg, 0.0))
        n2, r2 = _norm(base + _nn(woT[...], att_s[:, at]))
        hT = (n1 + n2).astype(BF)
        h_s[:, at] = hT
        up = _nn(wupT[...], hT)
        sq = up * up
        th = jnp.tanh((GELU_C * up) * (1.0 + GELU_A * sq))
        half = 0.5 + 0.5 * th
        gT = (up * half).astype(BF)
        g_s[:, at] = gT
        dgelu = half + (0.5 * up) * (1.0 - th * th) * (GELU_C + (3.0 * GELU_A * GELU_C) * sq)
        out, r3 = _norm(hT.astype(F32) + _nn(wdownT[...], gT))
        hot = hot_ref[b]
        hi, lo = _split(out)
        lr = _nn(hi, hot) + _nn(lo, hot)
        rl = pltpu.roll(lr, n_pairs, 1) * wcol[...]
        preds = jnp.sum(lr * rl, axis=0, keepdims=True)
        tgt = targets_ref[pl.ds(b, 1), :]
        diff = preds - jnp.concatenate([tgt, tgt], axis=1)
        preds_ref[pl.ds(b, 1), :] = preds[:, 0:n_pairs]
        obj_s[0:1, 0:n_pairs] += diff[:, 0:n_pairs] * diff[:, 0:n_pairs]
        hi, lo = _split((diff * (2.0 / n_all)) * rl)
        do = _norm_back(_nt(hi, hot) + _nt(lo, hot), out, r3).astype(BF)
        do_s[:, at] = do
        dg = _nn(wdown[...], do).astype(BF)
        dup = (dgelu * dg.astype(F32)).astype(BF)
        dup_s[:, at] = dup
        dh = _nn(wup[...], dup).astype(BF)
        dl = (do.astype(F32) + dh.astype(F32)).astype(BF).astype(F32)
        dagg = (jnp.where(agg > 0.0, _norm_back(dl, n1, r1), 0.0) * dinv).astype(BF)
        dxw = _nt(dagg, adjT[b]).astype(BF)
        dy_s[3 * feats : 4 * feats, at] = (dxw.astype(F32) + dagg.astype(F32)).astype(BF)
        da = _norm_back(dl, n2, r2).astype(BF)
        da_s[:, at] = da
        datt_s[:, at] = _nn(wo[...], da).astype(BF)

    _over(subs, MID_GROUP, middle)

    def attend_back(b):
        at = lanes(b)
        for h in range(HEADS):
            d = datt_s[head(0, h), at]
            pf = pf_s[b, h]
            dp = _tn(y_s[head(2, h), at], d).astype(BF).astype(F32)
            dy_s[head(2, h), at] = _nt(d, pf.astype(BF)).astype(BF)
            t = dp * pf
            ds = ((t - pf * jnp.sum(t, axis=0, keepdims=True)) * scale).astype(BF)
            dy_s[head(0, h), at] = _nn(y_s[head(1, h), at], ds).astype(BF)
            dy_s[head(1, h), at] = _nt(y_s[head(0, h), at], ds).astype(BF)

    _over(subs, BWD_GROUP, attend_back)

    gq_s[:, 4 * feats :] = _nt(att_s[...], da_s[...]).astype(BF)
    gu_s[...] = _nt(h_s[...], dup_s[...]).astype(BF)
    gd_s[...] = _nt(g_s[...], do_s[...]).astype(BF)
    gq_s[:, 0 : 4 * feats] = _nt(x_s[...], dy_s[...]).astype(BF)
    obj = jnp.sum(obj_s[0:1, :], axis=1, keepdims=True) / n_all
    if packed:
        keep_ref, send_ref = outs
        slabs, rows, width = keep_ref.shape
        core = lax.axis_index("store") % 2
        obj_block = _spread(obj, rows)
        cut = feats * 5
        for ref, side in ((keep_ref, core), (send_ref, 1 - core)):
            for j in range(slabs):
                d = 2 * j + side
                r = pl.ds(pl.multiple_of(d * rows, rows), rows)
                ref[j, :, 0:cut] = gq_s[r, :]
                ref[j, :, cut : cut + hidden] = gu_s[r, :]
                for i in range(hidden // feats):
                    r = pl.ds(pl.multiple_of(d * (rows * hidden // feats) + i * rows, rows), rows)
                    w = cut + hidden + i * feats
                    ref[j, :, w : w + feats] = gd_s[r, :]
                ref[j, :, width - LANES : width] = obj_block
    else:
        obj_ref, gqkv_ref, go_ref, gmsg_ref, gup_ref, gdown_ref = outs
        obj_ref[...] = jnp.broadcast_to(obj, obj_ref.shape)
        gqkv_ref[...] = gq_s[:, 0 : 3 * feats]
        gmsg_ref[...] = gq_s[:, 3 * feats : 4 * feats]
        go_ref[...] = gq_s[:, 4 * feats :]
        gup_ref[...] = gu_s[...]
        gdown_ref[...] = gd_s[...]


def _spread(value, rows):
    full = jnp.broadcast_to(value, (rows, LANES))
    hi = full.astype(BF).astype(F32)
    mid = (full - hi).astype(BF).astype(F32)
    lo = full - hi - mid
    lane = lax.broadcasted_iota(jnp.int32, (rows, LANES), 1)
    return jnp.where(lane < 32, hi, jnp.where(lane < 64, mid, jnp.where(lane < 96, lo, 0.0))).astype(BF)


def _gather_terms(block):
    return block[0:1, 0:1] + block[0:1, 32:33] + block[0:1, 64:65]


def _pair_kernel(a_ref, b_ref, o_ref):
    slabs, rows, width = o_ref.shape
    o_ref[...] = (a_ref[...].astype(F32) + b_ref[...].astype(F32)).astype(BF)
    blk = a_ref[0, :, width - LANES : width].astype(F32), b_ref[0, :, width - LANES : width].astype(F32)
    obj = _spread(_gather_terms(blk[0]) + _gather_terms(blk[1]), rows)
    for j in range(slabs):
        o_ref[j, :, width - LANES : width] = obj


def _final_kernel(in_ref, loss_ref, gqkv, go, gmsg, gup, gdown):
    slabs, rows, width = in_ref.shape
    total = in_ref[0].astype(F32)
    for j in range(1, slabs):
        total = total + in_ref[j].astype(F32)
    feats = go.shape[1]
    hidden = gup.shape[1]
    gqkv[...] = total[:, 0 : 3 * feats]
    gmsg[...] = total[:, 3 * feats : 4 * feats]
    go[...] = total[:, 4 * feats : 5 * feats]
    gup[...] = total[:, 5 * feats : 5 * feats + hidden]
    for i in range(hidden // feats):
        w = 5 * feats + hidden + i * feats
        gdown[i * rows : (i + 1) * rows, :] = total[:, w : w + feats]
    loss = _gather_terms(total[:, width - LANES : width]) / (2 * slabs)
    loss_ref[0] = jnp.sum(loss)


def _vmem(n):
    return [pl.BlockSpec(memory_space=pltpu.VMEM)] * n


def local_step(prep, fetched, targets, weights, groups):
    feats, hidden = weights[1].shape
    subs, nodes = prep[3].shape
    n_pairs = targets.shape[1]
    total = subs * nodes
    sources = (*prep, targets, *weights)
    rows = feats // groups
    packed = groups % 2 == 0 and feats % groups == 0 and hidden % feats == 0 and rows % 16 == 0
    out = [((subs, n_pairs), F32)]
    if packed:
        slab = (groups // 2, rows, 5 * feats + 2 * hidden // feats * feats + LANES)
        out += [(slab, BF), (slab, BF)]
    else:
        out += [
            ((8, LANES), F32), ((feats, 3 * feats), BF), ((feats, feats), BF), ((feats, feats), BF),
            ((feats, hidden), BF), ((hidden, feats), BF),
        ]
    res = pl.pallas_call(
        lambda *refs: _step_kernel(packed, *refs),
        in_specs=_vmem(1) + [pl.BlockSpec(memory_space=pltpu.HBM)] * len(sources),
        out_specs=_vmem(len(out)),
        out_shape=[jax.ShapeDtypeStruct(s, d) for s, d in out],
        scratch_shapes=[pltpu.VMEM(v.shape, v.dtype) for v in sources]
        + [
            pltpu.VMEM((feats, total), BF),
            pltpu.VMEM((4 * feats, total), BF),
            pltpu.VMEM((4 * feats, total), BF),
            pltpu.VMEM((feats, total), BF),
            pltpu.VMEM((feats, total), BF),
            pltpu.VMEM((feats, total), BF),
            pltpu.VMEM((hidden, total), BF),
            pltpu.VMEM((feats, total), BF),
            pltpu.VMEM((hidden, total), BF),
            pltpu.VMEM((feats, total), BF),
            pltpu.VMEM((subs, HEADS, nodes, nodes), F32),
            pltpu.VMEM((8, LANES), F32),
            pltpu.VMEM((feats, 5 * feats), BF),
            pltpu.VMEM((feats, hidden), BF),
            pltpu.VMEM((hidden, feats), BF),
            pltpu.SemaphoreType.DMA((len(sources),)),
        ],
        compiler_params=pltpu.CompilerParams(vmem_limit_bytes=44 << 20),
        name="graph_step",
    )(fetched, *_hbm(*sources))
    return packed, res


def shards(
    store_feats, requests, node_slots, edges, pairs, targets,
    w_qkv, w_o, w_msg, w_up, w_down, w_read,
):
    feats = store_feats.shape[1]
    hidden = w_up.shape[1]
    groups = lax.axis_size("store")
    picked = jnp.take(
        store_feats,
        lax.all_to_all(requests, "store", split_axis=0, concat_axis=0, tiled=True),
        axis=0,
        mode="clip",
    )
    fetched = lax.all_to_all(picked, "store", split_axis=0, concat_axis=0, tiled=True)
    fetched = fetched.reshape(-1, feats)
    prep = _prep(w_qkv, w_o, w_msg, w_up, w_down, edges, pairs, node_slots, w_read, fetched.shape[0])
    packed, (preds, *terms) = local_step(prep, fetched, targets, (w_o, w_up, w_down), groups)
    if packed:
        keep, send = terms
        rows = keep.shape[1]
        got = lax.ppermute(send, "store", [(i, i ^ 1) for i in range(groups)])
        paired = pl.pallas_call(
            _pair_kernel,
            in_specs=_vmem(2),
            out_specs=pl.BlockSpec(memory_space=pltpu.VMEM),
            out_shape=jax.ShapeDtypeStruct(keep.shape, BF),
            name="pair_sum",
        )(keep, got)
        sides = [[i for i in range(groups) if i % 2 == c] for c in (0, 1)]
        shared = lax.all_to_all(
            paired, "store", split_axis=0, concat_axis=0, tiled=True, axis_index_groups=sides
        )
        loss, *shares = pl.pallas_call(
            _final_kernel,
            in_specs=_vmem(1),
            out_specs=[pl.BlockSpec(memory_space=pltpu.SMEM)] + _vmem(5),
            out_shape=[
                jax.ShapeDtypeStruct((1,), F32),
                jax.ShapeDtypeStruct((rows, 3 * feats), F32),
                jax.ShapeDtypeStruct((rows, feats), F32),
                jax.ShapeDtypeStruct((rows, feats), F32),
                jax.ShapeDtypeStruct((rows, hidden), F32),
                jax.ShapeDtypeStruct((rows * (hidden // feats), feats), F32),
            ],
            name="final_sum",
        )(shared)
    else:
        obj, *grads = terms
        shares = [
            lax.psum_scatter(lax.optimization_barrier(g.astype(F32)), "store", scatter_dimension=0, tiled=True)
            for g in grads
        ]
        loss = (lax.psum(obj[0, 0], "store") / groups).reshape(1)
    return (preds, loss, *shares)


def solution(mesh):
    rows = P(("parts", "store"), None)
    deep = P(("parts", "store"), None, None)
    in_specs = (rows, rows, rows, deep, deep, rows, P(), P(), P(), P(), P(), P())
    out_specs = (rows, P("parts"), rows, rows, rows, rows, rows)
    return jax.shard_map(shards, mesh=mesh, in_specs=in_specs, out_specs=out_specs, check_vma=False)
```

time: 443 us -> 91.1 us (0.21); the launches traced: 435 us -> 90.7 us
  waiting for transfers between devices: 229 us -> 5.15 us
  other arithmetic: 73.8 us -> 0.68 us
  Pallas kernels: 0 us -> 40.6 us
  matrix products: 40.4 us -> 0 us
  local copies, waits for them, and re-layouts: 33.5 us -> 4.65 us
  between operations: 15.7 us -> 0.7 us
  starting transfers between devices: 12 us -> 3.49 us
  blocking collectives: 30.4 us -> 35.4 us
    reduce_scatter x5 -> x0, waiting for transfers between devices: 220 us -> none  [the longest x1 59.5 us: shards(): lax.psum_scatter(terms[0], 'store', scatter_dimension=0, tiled=True)]
    pallas_call x0 -> x4, Pallas kernels: none -> 40.6 us  [the longest x1 32.6 us: local_step(): pl.pallas_call(lambda *refs: _step_kernel(packed, *refs), in_specs=_vmem(...]
    dot_general x21 -> x0, matrix products: 40.4 us -> none  [the longest x3 11.1 us: objective_of(): jnp.einsum('bhqk,bkhd->bqhd', probs, values, preferred_element_type=jnp.f...]
    add_any x4 -> x0, other arithmetic: 37.3 us -> none  [the longest x2 36.6 us: objective_of(): left = jnp.take_along_axis(out, pairs[:, :, 0][:, :, None], axis=1)]
    all_to_all x0 -> x2, blocking collectives: none -> 35.4 us  [the longest x1 21.9 us: shards(): lax.all_to_all(paired, 'store', split_axis=0, concat_axis=0, tiled=True,...]
    unnamed x1 -> x0, blocking collectives: 30.4 us -> none
    reduce_sum x11 -> x0, other arithmetic: 20.4 us -> none  [the longest x1 6.3 us: objective_of(): expo = jnp.exp(scores - top)]
    convert_element_type x1 -> x0, other arithmetic: 9.74 us -> none  [objective_of(): hidden_h = (layer_norm(base + jax.nn.relu(agg.reshape(batch * width, feat...]
  transfers between devices with their start and end apart: 7 -> 2, of which waited for: 6 -> 2; matrix products, arithmetic and copies ran while one was open for 9% -> 0% of each run, Pallas kernels for 0% -> 4%
where the time goes in v2:
time: 91.1 us; the launch traced here: 90.7 us
  Pallas kernels  40.6 us (45%)
  blocking collectives  35.4 us (39%)
  waiting for transfers between devices  5.15 us (6%)
  local copies, waits for them, and re-layouts  4.65 us (5%)
  starting transfers between devices  3.49 us (4%)
    pallas_call x1, Pallas kernels, local_step(): pl.pallas_call(lambda *refs: _step_kernel(packed, *refs), in_specs=_vmem(...  32.6 us
    all_to_all x1, blocking collectives, shards(): lax.all_to_all(paired, 'store', split_axis=0, concat_axis=0, tiled=True,...  21.9 us
    all_to_all x1, blocking collectives, shards(): lax.all_to_all(requests, 'store', split_axis=0, concat_axis=0, tiled=True)  13.6 us
    pallas_call x1, Pallas kernels, _prep(): pl.pallas_call(_prep_kernel, in_specs=[pl.BlockSpec(memory_space=pltpu.HB...  3.75 us
    all_to_all x1, starting transfers between devices, shards(): lax.all_to_all(picked, 'store', split_axis=0, concat_axis=0, tiled=True)  3.49 us
    all_to_all x1, waiting for transfers between devices, shards(): lax.all_to_all(picked, 'store', split_axis=0, concat_axis=0, tiled=True)  3.1 us
    pallas_call x1, Pallas kernels, shards(): pl.pallas_call(_pair_kernel, in_specs=_vmem(2), out_specs=pl.BlockSpec(me...  2.45 us
    ppermute x1, waiting for transfers between devices, shards(): got = lax.ppermute(send, 'store', [(i, i ^ 1) for i in range(groups)])  2.05 us
  transfers between devices with their start and end apart: 2, of which 2 were waited for; matrix products, arithmetic and copies ran while one was open for 0% of the time, Pallas kernels for 4%

profile of v2, /device:TPU:0, one launch (start us, length us, event | category | flops | bytes accessed | tf_op | source)
XLA Modules:
  0.0 90.7 jit_solution(16503249128401059762)
XLA Ops:
  0.6 0.0 copy-start
  0.6 0.9 copy.21
  1.6 13.6 %all_to_all.19 = s32[16,1,8]{2,1,0:T(1,128)S(1)} all-to-all(s32[16,1,8]{2,1,0:T(1,128)S(1)} %copy.21), channel_id=1, replica_groups=mesh['parts'=2,'store'=16] {'store'}, dimensions={0} | all-to-all | bytes 1024 | tf_op jit(solution)/shard_map/all_to_all | solution.py:418
  15.1 0.5 broadcast.7
  15.6 0.7 reduce.3
  16.3 0.1 reshape.27
  16.4 0.0 copy-done
  16.4 1.5 %gather_fusion = bf16[128,256]{1,0:T(8,128)(2,1)} fusion(bf16[4096,256]{1,0:T(8,128)(2,1)S(1)} %copy-done, s32[1024]{0:T(1024)S(1)} %pad_clamp_fusion), kind=kCustom, calls=%fused_computation | custom fusion | bytes 131584 | tf_op jit(solution)/shard_map/jit(_take)/gather | solution.py:416
  17.9 3.5 %all-to-all-start.1 = ((bf16[16,8,256]{2,1,0:T(8,128)(2,1)}), bf16[16,8,256]{2,1,0:T(8,128)(2,1)S(1)}, u32[]{:S(2)}, u32[]{:S(2)}) async-start(bf16[16,8,256]{2,1,0:T(8,128)(2,1)} %bitcast.1), calls=%async_computation.1 | async-start | bytes 131072 | tf_op jit(solution)/shard_map/all_to_all | solution.py:422
  21.4 3.7 %prep.1 = (bf16[128,1024]{1,0:T(8,128)(2,1)}, bf16[1024,256]{1,0:T(8,128)(2,1)}, bf16[4,256,256]{2,1,0:T(8,128)(2,1)}, f32[4,256]{1,0:T(4,128)}, bf16[256,256]{1...) custom-call(bf16[256,768]{1,0:T(8,128)(2,1)} %wqkv_h.1, ...), custom_call_target="tpu_custom_call" | custom-call | flops 536870912 | bytes 8388608 | tf_op jit(solution)/shard_map/prep/pallas_call | solution.py:123
  25.1 3.1 %all-to-all-done.1 = bf16[16,8,256]{2,1,0:T(8,128)(2,1)S(1)} async-done(((bf16[16,8,256]{2,1,0:T(8,128)(2,1)}), bf16[16,8,256]{2,1,0:T(8,128)(2,1)S(1)}, u32[]{:S(2)}, u32[]{:S(2)}) %all-to-all-start.1) | async-done | bytes 65568 | tf_op jit(solution)/shard_map/all_to_all | solution.py:422
  28.3 32.6 %graph_step.1 = (f32[4,64]{1,0:T(4,128)}, bf16[8,16,2432]{2,1,0:T(8,128)(2,1)S(1)}, bf16[8,16,2432]{2,1,0:T(8,128)(2,1)S(1)}) custom-call(bf16[128,256]{1,0:T(8,128)(2,1)S(1)} %bitcast.6, bf16[128,1024]{1,0:T(8,128)(2,1)} %get-tuple-element.25.refs_1_, bf16[1024,256]{1,0:T(8,128)(2,1)} %get-tuple-element.26.refs_2_, ...), custom_call_target="tpu_custom_call" | custom-call | tf_op jit(solution)/shard_map/graph_step/pallas_call | solution.py:379
  60.9 0.0 copy-start.1
  60.9 0.8 copy-done.1
  61.7 0.0 collective-permute-start
  61.7 2.0 %collective-permute-done.b_ref = bf16[8,16,2432]{2,1,0:T(8,128)(2,1)S(1)} collective-permute-done((bf16[8,16,2432]{2,1,0:T(8,128)(2,1)S(1)}, bf16[8,16,2432]{2,1,0:T(8,128)(2,1)S(1)}, u32[]{:S(2)}, u32[]{:S(2)}) %collective-permute-start) | collective-permute-done | bytes 622624 | tf_op jit(solution)/shard_map/ppermute | solution.py:429
  63.8 0.0 copy-start.2
  63.8 0.9 copy-done.2
  64.6 2.4 %pair_sum.1 = bf16[8,16,2432]{2,1,0:T(8,128)(2,1)} custom-call(bf16[8,16,2432]{2,1,0:T(8,128)(2,1)} %copy-done.1, bf16[8,16,2432]{2,1,0:T(8,128)(2,1)} %copy-done.2), custom_call_target="tpu_custom_call" | custom-call | tf_op jit(solution)/shard_map/pair_sum/pallas_call | solution.py:430
  67.1 21.9 %all_to_all.20.in_ref = bf16[8,16,2432]{2,1,0:T(8,128)(2,1)} all-to-all(bf16[8,16,2432]{2,1,0:T(8,128)(2,1)} %pair_sum.1), channel_id=1, replica_groups={{0,2,4,6,8,10,12,14},{1,3,5,7,9,11,13,15},{16,18,20,22,24,26,28,30},{17..., dimensions={0} | all-to-all | bytes 1245184 | tf_op jit(solution)/shard_map/all_to_all | solution.py:438
  88.9 1.8 %final_sum.1 = (f32[1]{0:T(128)}, f32[16,768]{1,0:T(8,128)}, f32[16,256]{1,0:T(8,128)}, f32[16,256]{1,0:T(8,128)}, f32[16,512]{1,0:T(8,128)}, /*index=5*/f32[32,256]{1,0:T(8,128)}) custom-call(bf16[8,16,2432]{2,1,0:T(8,128)(2,1)} %all_to_all.20.in_ref), custom_call_target="tpu_custom_call" | custom-call | tf_op jit(solution)/shard_map/final_sum/pallas_call | solution.py:441
  (1 shorter events, 0.0 us)
Async XLA Ops:
  0.6 15.8 %copy-start = (bf16[4096,256]{1,0:T(8,128)(2,1)S(1)}, bf16[4096,256]{1,0:T(8,128)(2,1)}, u32[]{:S(2)}) copy-start(bf16[4096,256]{1,0:T(8,128)(2,1)} %param.12) | copy-start | bytes 6291460
  17.9 10.4 %all-to-all-start.1 = ((bf16[16,8,256]{2,1,0:T(8,128)(2,1)}), bf16[16,8,256]{2,1,0:T(8,128)(2,1)S(1)}, u32[]{:S(2)}, u32[]{:S(2)}) async-start(bf16[16,8,256]{2,1,0:T(8,128)(2,1)} %bitcast.1), calls=%async_computation.1 | async-start | bytes 131072 | tf_op jit(solution)/shard_map/all_to_all | solution.py:422
  60.9 0.8 copy-start.1
  61.7 2.1 %collective-permute-start = (bf16[8,16,2432]{2,1,0:T(8,128)(2,1)S(1)}, bf16[8,16,2432]{2,1,0:T(8,128)(2,1)S(1)}, u32[]{:S(2)}, u32[]{:S(2)}) collective-permute-start(bf16[8,16,2432]{2,1,0:T(8,128)(2,1)S(1)} %get-tuple-element.36), channel_id=1, source_target_pairs={{0,1},{1,0},{2,3},{3,2},{4,5},{5,4},{6,7},{7,6},{8,9},{9,8},{10,11... | collective-permute-start | bytes 1867784 | tf_op jit(solution)/shard_map/ppermute | solution.py:429
  63.8 0.9 copy-start.2

commit v3 on v2

--- a/solution.py
+++ b/solution.py
@@ -153,7 +153,6 @@
 
 
 FWD_GROUP = 1
-MID_GROUP = 2
 BWD_GROUP = 1
 
 
@@ -181,7 +180,8 @@
         pick, wqmT, adjT, deg, woT, wupT, wdownT, hot_ref, wcol, targets_ref, wo, wup, wdown,
     ) = refs[:13]
     (
-        x_s, y_s, dy_s, att_s, datt_s, h_s, g_s, do_s, dup_s, da_s, pf_s, obj_s, gq_s, gu_s, gd_s,
+        x_s, y_s, dy_s, att_s, datt_s, h_s, g_s, do_s, dup_s, da_s, pf_s, p_s, ds_s, obj_s, gq_s, gu_s, gd_s,
+        agg_s, n1_s, n2_s, up_s, out_s, dout_s, hi_s, lo_s, r1_s, r2_s, r3_s,
         sems,
     ) = refs[13:]
     copies = [
@@ -215,71 +215,100 @@
     def attend(b):
         at = lanes(b)
         for h in range(HEADS):
-            s = _tn(y_s[head(1, h), at], y_s[head(0, h), at])
+            pf_s[b, h] = _tn(y_s[head(1, h), at], y_s[head(0, h), at])
+        for h in range(HEADS):
+            s = pf_s[b, h]
             e = jnp.exp2((s - jnp.max(s, axis=0, keepdims=True)) * (scale * LOG2E))
             pf = e * (1.0 / jnp.sum(e, axis=0, keepdims=True))
             pf_s[b, h] = pf
-            att_s[head(0, h), at] = _nn(y_s[head(2, h), at], pf.astype(BF)).astype(BF)
+            p_s[h] = pf.astype(BF)
+        for h in range(HEADS):
+            att_s[head(0, h), at] = _nn(y_s[head(2, h), at], p_s[h]).astype(BF)
 
     _over(subs, FWD_GROUP, attend)
     for c in copies[2:]:
         c.wait()
 
-    def middle(b):
-        at = lanes(b)
-        base = x_s[:, at].astype(F32)
-        xw = y_s[3 * feats : 4 * feats, at]
-        dinv = deg[pl.ds(b, 1), :]
-        agg = (_nn(xw, adjT[b]) + xw.astype(F32)) * dinv
-        n1, r1 = _norm(base + jnp.maximum(agg, 0.0))
-        n2, r2 = _norm(base + _nn(woT[...], att_s[:, at]))
-        hT = (n1 + n2).astype(BF)
-        h_s[:, at] = hT
-        up = _nn(wupT[...], hT)
+    total = subs * nodes
+    blocks = [slice(b * nodes, (b + 1) * nodes) for b in range(subs)]
+    cuts = [slice(c, c + LANES) for c in range(0, total, LANES)]
+    msg = slice(3 * feats, 4 * feats)
+    for b, at in enumerate(blocks):
+        agg_s[:, at] = _nn(y_s[msg, at], adjT[b])
+        n2_s[:, at] = _nn(woT[...], att_s[:, at])
+    for c in cuts:
+        b, w = c.start // nodes, c.start % nodes
+        base = x_s[:, c].astype(F32)
+        agg = (agg_s[:, c] + y_s[msg, c].astype(F32)) * deg[b : b + 1, w : w + LANES]
+        agg_s[:, c] = agg
+        n1, r1_s[0:1, c] = _norm(base + jnp.maximum(agg, 0.0))
+        n2, r2_s[0:1, c] = _norm(base + n2_s[:, c])
+        n1_s[:, c] = n1
+        n2_s[:, c] = n2
+        h_s[:, c] = (n1 + n2).astype(BF)
+    for at in blocks:
+        up_s[:, at] = _nn(wupT[...], h_s[:, at])
+    for c in cuts:
+        up = up_s[:, c]
         sq = up * up
         th = jnp.tanh((GELU_C * up) * (1.0 + GELU_A * sq))
         half = 0.5 + 0.5 * th
-        gT = (up * half).astype(BF)
-        g_s[:, at] = gT
-        dgelu = half + (0.5 * up) * (1.0 - th * th) * (GELU_C + (3.0 * GELU_A * GELU_C) * sq)
-        out, r3 = _norm(hT.astype(F32) + _nn(wdownT[...], gT))
+        g_s[:, c] = (up * half).astype(BF)
+        up_s[:, c] = half + (0.5 * up) * (1.0 - th * th) * (GELU_C + (3.0 * GELU_A * GELU_C) * sq)
+    for at in blocks:
+        out_s[:, at] = _nn(wdownT[...], g_s[:, at])
+    for c in cuts:
+        out, r3_s[0:1, c] = _norm(h_s[:, c].astype(F32) + out_s[:, c])
+        out_s[:, c] = out
+        hi_s[:, c], lo_s[:, c] = _split(out)
+    for b, at in enumerate(blocks):
         hot = hot_ref[b]
-        hi, lo = _split(out)
-        lr = _nn(hi, hot) + _nn(lo, hot)
+        lr = _nn(hi_s[:, at], hot) + _nn(lo_s[:, at], hot)
         rl = pltpu.roll(lr, n_pairs, 1) * wcol[...]
         preds = jnp.sum(lr * rl, axis=0, keepdims=True)
-        tgt = targets_ref[pl.ds(b, 1), :]
+        tgt = targets_ref[b : b + 1, :]
         diff = preds - jnp.concatenate([tgt, tgt], axis=1)
-        preds_ref[pl.ds(b, 1), :] = preds[:, 0:n_pairs]
+        preds_ref[b : b + 1, :] = preds[:, 0:n_pairs]
         obj_s[0:1, 0:n_pairs] += diff[:, 0:n_pairs] * diff[:, 0:n_pairs]
         hi, lo = _split((diff * (2.0 / n_all)) * rl)
-        do = _norm_back(_nt(hi, hot) + _nt(lo, hot), out, r3).astype(BF)
-        do_s[:, at] = do
-        dg = _nn(wdown[...], do).astype(BF)
-        dup = (dgelu * dg.astype(F32)).astype(BF)
-        dup_s[:, at] = dup
-        dh = _nn(wup[...], dup).astype(BF)
-        dl = (do.astype(F32) + dh.astype(F32)).astype(BF).astype(F32)
-        dagg = (jnp.where(agg > 0.0, _norm_back(dl, n1, r1), 0.0) * dinv).astype(BF)
+        dout_s[:, at] = _nt(hi, hot) + _nt(lo, hot)
+    for c in cuts:
+        do_s[:, c] = _norm_back(dout_s[:, c], out_s[:, c], r3_s[0:1, c]).astype(BF)
+    for at in blocks:
+        dup_s[:, at] = _nn(wdown[...], do_s[:, at]).astype(BF)
+    for c in cuts:
+        dup_s[:, c] = (up_s[:, c] * dup_s[:, c].astype(F32)).astype(BF)
+    for at in blocks:
+        da_s[:, at] = _nn(wup[...], dup_s[:, at]).astype(BF)
+    for c in cuts:
+        b, w = c.start // nodes, c.start % nodes
+        dl = (do_s[:, c].astype(F32) + da_s[:, c].astype(F32)).astype(BF).astype(F32)
+        d1 = _norm_back(dl, n1_s[:, c], r1_s[0:1, c])
+        d1 = jnp.where(agg_s[:, c] > 0.0, d1, 0.0) * deg[b : b + 1, w : w + LANES]
+        hi_s[:, c] = d1.astype(BF)
+        da_s[:, c] = _norm_back(dl, n2_s[:, c], r2_s[0:1, c]).astype(BF)
+    for b, at in enumerate(blocks):
+        datt_s[:, at] = _nn(wo[...], da_s[:, at]).astype(BF)
+        dagg = hi_s[:, at]
         dxw = _nt(dagg, adjT[b]).astype(BF)
-        dy_s[3 * feats : 4 * feats, at] = (dxw.astype(F32) + dagg.astype(F32)).astype(BF)
-        da = _norm_back(dl, n2, r2).astype(BF)
-        da_s[:, at] = da
-        datt_s[:, at] = _nn(wo[...], da).astype(BF)
-
-    _over(subs, MID_GROUP, middle)
+        dy_s[msg, at] = (dxw.astype(F32) + dagg.astype(F32)).astype(BF)
 
     def attend_back(b):
         at = lanes(b)
         for h in range(HEADS):
-            d = datt_s[head(0, h), at]
-            pf = pf_s[b, h]
-            dp = _tn(y_s[head(2, h), at], d).astype(BF).astype(F32)
-            dy_s[head(2, h), at] = _nt(d, pf.astype(BF)).astype(BF)
-            t = dp * pf
-            ds = ((t - pf * jnp.sum(t, axis=0, keepdims=True)) * scale).astype(BF)
-            dy_s[head(0, h), at] = _nn(y_s[head(1, h), at], ds).astype(BF)
-            dy_s[head(1, h), at] = _nt(y_s[head(0, h), at], ds).astype(BF)
+            ds_s[h] = _tn(y_s[head(2, h), at], datt_s[head(0, h), at]).astype(BF)
+        for h in range(HEADS):
+            for c in range(0, nodes, LANES):
+                cut = slice(c, c + LANES)
+                pf = pf_s[b, h, :, cut]
+                t = ds_s[h, :, cut].astype(F32) * pf
+                ds = (t - pf * jnp.sum(t, axis=0, keepdims=True)) * scale
+                ds_s[h, :, cut] = ds.astype(BF)
+                p_s[h, :, cut] = pf.astype(BF)
+        for h in range(HEADS):
+            dy_s[head(2, h), at] = _nt(datt_s[head(0, h), at], p_s[h]).astype(BF)
+            dy_s[head(0, h), at] = _nn(y_s[head(1, h), at], ds_s[h]).astype(BF)
+            dy_s[head(1, h), at] = _nt(y_s[head(0, h), at], ds_s[h]).astype(BF)
 
     _over(subs, BWD_GROUP, attend_back)
 
@@ -394,10 +423,23 @@
             pltpu.VMEM((hidden, total), BF),
             pltpu.VMEM((feats, total), BF),
             pltpu.VMEM((subs, HEADS, nodes, nodes), F32),
+            pltpu.VMEM((HEADS, nodes, nodes), BF),
+            pltpu.VMEM((HEADS, nodes, nodes), BF),
             pltpu.VMEM((8, LANES), F32),
             pltpu.VMEM((feats, 5 * feats), BF),
             pltpu.VMEM((feats, hidden), BF),
             pltpu.VMEM((hidden, feats), BF),
+            pltpu.VMEM((feats, total), F32),
+            pltpu.VMEM((feats, total), F32),
+            pltpu.VMEM((feats, total), F32),
+            pltpu.VMEM((hidden, total), F32),
+            pltpu.VMEM((feats, total), F32),
+            pltpu.VMEM((feats, total), F32),
+            pltpu.VMEM((feats, total), BF),
+            pltpu.VMEM((feats, total), BF),
+            pltpu.VMEM((8, total), F32),
+            pltpu.VMEM((8, total), F32),
+            pltpu.VMEM((8, total), F32),
             pltpu.SemaphoreType.DMA((len(sources),)),
         ],
         compiler_params=pltpu.CompilerParams(vmem_limit_bytes=44 << 20),
@@ -432,6 +474,7 @@
             in_specs=_vmem(2),
             out_specs=pl.BlockSpec(memory_space=pltpu.VMEM),
             out_shape=jax.ShapeDtypeStruct(keep.shape, BF),
+            compiler_params=pltpu.CompilerParams(vmem_limit_bytes=8 << 20),
             name="pair_sum",
         )(keep, got)
         sides = [[i for i in range(groups) if i % 2 == c] for c in (0, 1)]
@@ -450,6 +493,7 @@
                 jax.ShapeDtypeStruct((rows, hidden), F32),
                 jax.ShapeDtypeStruct((rows * (hidden // feats), feats), F32),
             ],
+            compiler_params=pltpu.CompilerParams(vmem_limit_bytes=8 << 20),
             name="final_sum",
         )(shared)
     else:

time: 91.1 us -> 74.2 us (0.81)
  Pallas kernels: 40.6 us -> 27.2 us
  blocking collectives: 35.4 us -> 33.6 us
  local copies, waits for them, and re-layouts: 4.65 us -> 2.99 us
    pallas_call x1, Pallas kernels: 32.6 us -> 22.3 us  [local_step(): pl.pallas_call(lambda *refs: _step_kernel(packed, *refs), in_specs=_vmem(...]
    pallas_call x1, Pallas kernels: 2.45 us -> 0.35 us  [shards(): pl.pallas_call(_pair_kernel, in_specs=_vmem(2), out_specs=pl.BlockSpec(me...]
    all_to_all x1, blocking collectives: 21.9 us -> 20.1 us  [shards(): lax.all_to_all(paired, 'store', split_axis=0, concat_axis=0, tiled=True,...]
    unnamed x6 -> x2, local copies, waits for them, and re-layouts: 1.69 us -> 0.01 us
    pallas_call x1, Pallas kernels: 1.8 us -> 0.75 us  [shards(): pl.pallas_call(_final_kernel, in_specs=_vmem(1), out_specs=[pl.BlockSpec(...]
  transfers between devices with their start and end apart: 2 -> 2, of which waited for: 2 -> 2; matrix products, arithmetic and copies ran while one was open for 0% -> 0% of each run, Pallas kernels for 4% -> 5%
where the time goes in v3:
time: 74.2 us; the launch traced here: 73.9 us
  blocking collectives  33.6 us (45%)
  Pallas kernels  27.2 us (37%)
  waiting for transfers between devices  5.13 us (7%)
  starting transfers between devices  3.57 us (5%)
  local copies, waits for them, and re-layouts  2.99 us (4%)
    pallas_call x1, Pallas kernels, local_step(): pl.pallas_call(lambda *refs: _step_kernel(packed, *refs), in_specs=_vmem(...  22.3 us
    all_to_all x1, blocking collectives, shards(): lax.all_to_all(paired, 'store', split_axis=0, concat_axis=0, tiled=True,...  20.1 us
    all_to_all x1, blocking collectives, shards(): lax.all_to_all(requests, 'store', split_axis=0, concat_axis=0, tiled=True)  13.6 us
    pallas_call x1, Pallas kernels, _prep(): pl.pallas_call(_prep_kernel, in_specs=[pl.BlockSpec(memory_space=pltpu.HB...  3.76 us
    all_to_all x1, starting transfers between devices, shards(): lax.all_to_all(picked, 'store', split_axis=0, concat_axis=0, tiled=True)  3.5 us
    all_to_all x1, waiting for transfers between devices, shards(): lax.all_to_all(picked, 'store', split_axis=0, concat_axis=0, tiled=True)  3.09 us
    ppermute x1, waiting for transfers between devices, shards(): got = lax.ppermute(send, 'store', [(i, i ^ 1) for i in range(groups)])  2.04 us
  transfers between devices with their start and end apart: 2, of which 2 were waited for; matrix products, arithmetic and copies ran while one was open for 0% of the time, Pallas kernels for 5%

profile of v3, /device:TPU:0, one launch (start us, length us, event | category | flops | bytes accessed | tf_op | source)
XLA Modules:
  0.0 73.9 jit_solution(16654042131975530703)
XLA Ops:
  0.6 0.0 copy-start
  0.6 0.9 %copy.21 = s32[16,1,8]{2,1,0:T(1,128)S(1)} copy(s32[16,1,8]{0,2,1:T(8,128)} %bitcast.7) | data formatting | bytes 1024 | tf_op jit(solution)/shard_map/all_to_all | solution.py:460
  1.6 13.6 %all_to_all.19 = s32[16,1,8]{2,1,0:T(1,128)S(1)} all-to-all(s32[16,1,8]{2,1,0:T(1,128)S(1)} %copy.21), channel_id=1, replica_groups=mesh['parts'=2,'store'=16] {'store'}, dimensions={0} | all-to-all | bytes 1024 | tf_op jit(solution)/shard_map/all_to_all | solution.py:460
  15.1 0.5 broadcast.7
  15.6 0.7 reduce.3
  16.3 0.1 reshape.27
  16.4 0.0 copy-done
  16.4 1.5 %gather_fusion = bf16[128,256]{1,0:T(8,128)(2,1)} fusion(bf16[4096,256]{1,0:T(8,128)(2,1)S(1)} %copy-done, s32[1024]{0:T(1024)S(1)} %pad_clamp_fusion), kind=kCustom, calls=%fused_computation | custom fusion | bytes 131584 | tf_op jit(solution)/shard_map/jit(_take)/gather | solution.py:458
  17.9 3.5 %all-to-all-start.1 = ((bf16[16,8,256]{2,1,0:T(8,128)(2,1)}), bf16[16,8,256]{2,1,0:T(8,128)(2,1)S(1)}, u32[]{:S(2)}, u32[]{:S(2)}) async-start(bf16[16,8,256]{2,1,0:T(8,128)(2,1)} %bitcast.1), calls=%async_computation.1 | async-start | bytes 131072 | tf_op jit(solution)/shard_map/all_to_all | solution.py:464
  21.4 3.8 %prep.1 = (bf16[128,1024]{1,0:T(8,128)(2,1)}, bf16[1024,256]{1,0:T(8,128)(2,1)}, bf16[4,256,256]{2,1,0:T(8,128)(2,1)}, f32[4,256]{1,0:T(4,128)}, bf16[256,256]{1...) custom-call(bf16[256,768]{1,0:T(8,128)(2,1)} %wqkv_h.1, ...), custom_call_target="tpu_custom_call" | custom-call | flops 536870912 | bytes 8388608 | tf_op jit(solution)/shard_map/prep/pallas_call | solution.py:123
  25.2 3.1 %all-to-all-done.1 = bf16[16,8,256]{2,1,0:T(8,128)(2,1)S(1)} async-done(((bf16[16,8,256]{2,1,0:T(8,128)(2,1)}), bf16[16,8,256]{2,1,0:T(8,128)(2,1)S(1)}, u32[]{:S(2)}, u32[]{:S(2)}) %all-to-all-start.1) | async-done | bytes 65568 | tf_op jit(solution)/shard_map/all_to_all | solution.py:464
  28.3 22.3 %graph_step.1 = (f32[4,64]{1,0:T(4,128)}, bf16[8,16,2432]{2,1,0:T(8,128)(2,1)S(1)}, bf16[8,16,2432]{2,1,0:T(8,128)(2,1)S(1)}) custom-call(bf16[128,256]{1,0:T(8,128)(2,1)S(1)} %bitcast.6, bf16[128,1024]{1,0:T(8,128)(2,1)} %get-tuple-element.25.refs_1_, bf16[1024,256]{1,0:T(8,128)(2,1)} %get-tuple-element.26.refs_2_, ...), custom_call_target="tpu_custom_call" | custom-call | tf_op jit(solution)/shard_map/graph_step/pallas_call | solution.py:408
  50.6 0.1 collective-permute-start
  50.7 2.0 %collective-permute-done.b_ref = bf16[8,16,2432]{2,1,0:T(8,128)(2,1)S(1)} collective-permute-done((bf16[8,16,2432]{2,1,0:T(8,128)(2,1)S(1)}, bf16[8,16,2432]{2,1,0:T(8,128)(2,1)S(1)}, u32[]{:S(2)}, u32[]{:S(2)}) %collective-permute-start) | collective-permute-done | bytes 622624 | tf_op jit(solution)/shard_map/ppermute | solution.py:471
  52.7 0.3 pair_sum.1
  53.1 20.1 %all_to_all.20.in_ref = bf16[8,16,2432]{2,1,0:T(8,128)(2,1)S(1)} all-to-all(bf16[8,16,2432]{2,1,0:T(8,128)(2,1)S(1)} %pair_sum.1), channel_id=1, replica_groups={{0,2,4,6,8,10,12,14},{1,3,5,7,9,11,13,15},{16,18,20,22,24,26,28,30},{17..., dimensions={0} | all-to-all | bytes 1245184 | tf_op jit(solution)/shard_map/all_to_all | solution.py:481
  73.1 0.7 %final_sum.1 = (f32[1]{0:T(128)}, f32[16,768]{1,0:T(8,128)}, f32[16,256]{1,0:T(8,128)}, f32[16,256]{1,0:T(8,128)}, f32[16,512]{1,0:T(8,128)}, /*index=5*/f32[32,256]{1,0:T(8,128)}) custom-call(bf16[8,16,2432]{2,1,0:T(8,128)(2,1)S(1)} %all_to_all.20.in_ref), custom_call_target="tpu_custom_call" | custom-call | tf_op jit(solution)/shard_map/final_sum/pallas_call | solution.py:484
  (1 shorter events, 0.0 us)
Async XLA Ops:
  0.6 15.8 %copy-start = (bf16[4096,256]{1,0:T(8,128)(2,1)S(1)}, bf16[4096,256]{1,0:T(8,128)(2,1)}, u32[]{:S(2)}) copy-start(bf16[4096,256]{1,0:T(8,128)(2,1)} %param.12) | copy-start | bytes 6291460
  17.9 10.4 %all-to-all-start.1 = ((bf16[16,8,256]{2,1,0:T(8,128)(2,1)}), bf16[16,8,256]{2,1,0:T(8,128)(2,1)S(1)}, u32[]{:S(2)}, u32[]{:S(2)}) async-start(bf16[16,8,256]{2,1,0:T(8,128)(2,1)} %bitcast.1), calls=%async_computation.1 | async-start | bytes 131072 | tf_op jit(solution)/shard_map/all_to_all | solution.py:464
  50.6 2.1 %collective-permute-start = (bf16[8,16,2432]{2,1,0:T(8,128)(2,1)S(1)}, bf16[8,16,2432]{2,1,0:T(8,128)(2,1)S(1)}, u32[]{:S(2)}, u32[]{:S(2)}) collective-permute-start(bf16[8,16,2432]{2,1,0:T(8,128)(2,1)S(1)} %get-tuple-element.36), channel_id=1, source_target_pairs={{0,1},{1,0},{2,3},{3,2},{4,5},{5,4},{6,7},{7,6},{8,9},{9,8},{10,11... | collective-permute-start | bytes 1867784 | tf_op jit(solution)/shard_map/ppermute | solution.py:471

commit v4 on v3

--- a/solution.py
+++ b/solution.py
@@ -152,8 +152,21 @@
     )
 
 
-FWD_GROUP = 1
-BWD_GROUP = 1
+FWD_GROUP = 4
+BWD_GROUP = 4
+
+
+FWD_SKEW = 0
+MID_SKEW = 0
+BWD_SKEW = 0
+
+
+def _wave(items, skew, stages):
+    for step in range(len(stages) + skew * (items - 1) if skew else len(stages)):
+        for i in range(items):
+            s = step - skew * i
+            if 0 <= s < len(stages):
+                stages[s](i)
 
 
 def _over(subs, group, stage):
@@ -214,55 +227,76 @@
 
     def attend(b):
         at = lanes(b)
-        for h in range(HEADS):
+        def score(h):
             pf_s[b, h] = _tn(y_s[head(1, h), at], y_s[head(0, h), at])
-        for h in range(HEADS):
+
+        def soften(h):
             s = pf_s[b, h]
             e = jnp.exp2((s - jnp.max(s, axis=0, keepdims=True)) * (scale * LOG2E))
             pf = e * (1.0 / jnp.sum(e, axis=0, keepdims=True))
             pf_s[b, h] = pf
-            p_s[h] = pf.astype(BF)
-        for h in range(HEADS):
-            att_s[head(0, h), at] = _nn(y_s[head(2, h), at], p_s[h]).astype(BF)
+            p_s[b, h] = pf.astype(BF)
+
+        def blend(h):
+            att_s[head(0, h), at] = _nn(y_s[head(2, h), at], p_s[b, h]).astype(BF)
+
+        _wave(HEADS, FWD_SKEW, (score, soften, blend))
 
     _over(subs, FWD_GROUP, attend)
     for c in copies[2:]:
         c.wait()
 
     total = subs * nodes
-    blocks = [slice(b * nodes, (b + 1) * nodes) for b in range(subs)]
-    cuts = [slice(c, c + LANES) for c in range(0, total, LANES)]
     msg = slice(3 * feats, 4 * feats)
-    for b, at in enumerate(blocks):
+
+    def block(b):
+        return slice(b * nodes, (b + 1) * nodes)
+
+    def cuts(b):
+        return [block(b)]
+
+    def branches(b):
+        at = block(b)
         agg_s[:, at] = _nn(y_s[msg, at], adjT[b])
         n2_s[:, at] = _nn(woT[...], att_s[:, at])
-    for c in cuts:
-        b, w = c.start // nodes, c.start % nodes
-        base = x_s[:, c].astype(F32)
-        agg = (agg_s[:, c] + y_s[msg, c].astype(F32)) * deg[b : b + 1, w : w + LANES]
-        agg_s[:, c] = agg
-        n1, r1_s[0:1, c] = _norm(base + jnp.maximum(agg, 0.0))
-        n2, r2_s[0:1, c] = _norm(base + n2_s[:, c])
-        n1_s[:, c] = n1
-        n2_s[:, c] = n2
-        h_s[:, c] = (n1 + n2).astype(BF)
-    for at in blocks:
-        up_s[:, at] = _nn(wupT[...], h_s[:, at])
-    for c in cuts:
-        up = up_s[:, c]
-        sq = up * up
-        th = jnp.tanh((GELU_C * up) * (1.0 + GELU_A * sq))
-        half = 0.5 + 0.5 * th
-        g_s[:, c] = (up * half).astype(BF)
-        up_s[:, c] = half + (0.5 * up) * (1.0 - th * th) * (GELU_C + (3.0 * GELU_A * GELU_C) * sq)
-    for at in blocks:
-        out_s[:, at] = _nn(wdownT[...], g_s[:, at])
-    for c in cuts:
-        out, r3_s[0:1, c] = _norm(h_s[:, c].astype(F32) + out_s[:, c])
-        out_s[:, c] = out
-        hi_s[:, c], lo_s[:, c] = _split(out)
-    for b, at in enumerate(blocks):
+
+    def branch_norms(b):
+        for c in cuts(b):
+            w = c.start % nodes
+            base = x_s[:, c].astype(F32)
+            agg = (agg_s[:, c] + y_s[msg, c].astype(F32)) * deg[b : b + 1, w : w + nodes]
+            agg_s[:, c] = agg
+            n1, r1_s[0:1, c] = _norm(base + jnp.maximum(agg, 0.0))
+            n2, r2_s[0:1, c] = _norm(base + n2_s[:, c])
+            n1_s[:, c] = n1
+            n2_s[:, c] = n2
+            h_s[:, c] = (n1 + n2).astype(BF)
+
+    def raise_up(b):
+        up_s[:, block(b)] = _nn(wupT[...], h_s[:, block(b)])
+
+    def gate(b):
+        for c in cuts(b):
+            up = up_s[:, c]
+            sq = up * up
+            th = jnp.tanh((GELU_C * up) * (1.0 + GELU_A * sq))
+            half = 0.5 + 0.5 * th
+            g_s[:, c] = (up * half).astype(BF)
+            slope = (1.0 - th * th) * (GELU_C + (3.0 * GELU_A * GELU_C) * sq)
+            up_s[:, c] = half + (0.5 * up) * slope
+
+    def lower_down(b):
+        out_s[:, block(b)] = _nn(wdownT[...], g_s[:, block(b)])
+
+    def out_norm(b):
+        for c in cuts(b):
+            out, r3_s[0:1, c] = _norm(h_s[:, c].astype(F32) + out_s[:, c])
+            out_s[:, c] = out
+            hi_s[:, c], lo_s[:, c] = _split(out)
+
+    def readout(b):
         hot = hot_ref[b]
+        at = block(b)
         lr = _nn(hi_s[:, at], hot) + _nn(lo_s[:, at], hot)
         rl = pltpu.roll(lr, n_pairs, 1) * wcol[...]
         preds = jnp.sum(lr * rl, axis=0, keepdims=True)
@@ -272,43 +306,59 @@
         obj_s[0:1, 0:n_pairs] += diff[:, 0:n_pairs] * diff[:, 0:n_pairs]
         hi, lo = _split((diff * (2.0 / n_all)) * rl)
         dout_s[:, at] = _nt(hi, hot) + _nt(lo, hot)
-    for c in cuts:
-        do_s[:, c] = _norm_back(dout_s[:, c], out_s[:, c], r3_s[0:1, c]).astype(BF)
-    for at in blocks:
-        dup_s[:, at] = _nn(wdown[...], do_s[:, at]).astype(BF)
-    for c in cuts:
-        dup_s[:, c] = (up_s[:, c] * dup_s[:, c].astype(F32)).astype(BF)
-    for at in blocks:
-        da_s[:, at] = _nn(wup[...], dup_s[:, at]).astype(BF)
-    for c in cuts:
-        b, w = c.start // nodes, c.start % nodes
-        dl = (do_s[:, c].astype(F32) + da_s[:, c].astype(F32)).astype(BF).astype(F32)
-        d1 = _norm_back(dl, n1_s[:, c], r1_s[0:1, c])
-        d1 = jnp.where(agg_s[:, c] > 0.0, d1, 0.0) * deg[b : b + 1, w : w + LANES]
-        hi_s[:, c] = d1.astype(BF)
-        da_s[:, c] = _norm_back(dl, n2_s[:, c], r2_s[0:1, c]).astype(BF)
-    for b, at in enumerate(blocks):
+
+    def out_back(b):
+        for c in cuts(b):
+            do_s[:, c] = _norm_back(dout_s[:, c], out_s[:, c], r3_s[0:1, c]).astype(BF)
+
+    def down_back(b):
+        dup_s[:, block(b)] = _nn(wdown[...], do_s[:, block(b)]).astype(BF)
+
+    def gate_back(b):
+        for c in cuts(b):
+            dup_s[:, c] = (up_s[:, c] * dup_s[:, c].astype(F32)).astype(BF)
+
+    def up_back(b):
+        da_s[:, block(b)] = _nn(wup[...], dup_s[:, block(b)]).astype(BF)
+
+    def norms_back(b):
+        for c in cuts(b):
+            w = c.start % nodes
+            dl = (do_s[:, c].astype(F32) + da_s[:, c].astype(F32)).astype(BF).astype(F32)
+            d1 = _norm_back(dl, n1_s[:, c], r1_s[0:1, c])
+            d1 = jnp.where(agg_s[:, c] > 0.0, d1, 0.0) * deg[b : b + 1, w : w + nodes]
+            hi_s[:, c] = d1.astype(BF)
+            da_s[:, c] = _norm_back(dl, n2_s[:, c], r2_s[0:1, c]).astype(BF)
+
+    def branches_back(b):
+        at = block(b)
         datt_s[:, at] = _nn(wo[...], da_s[:, at]).astype(BF)
         dagg = hi_s[:, at]
         dxw = _nt(dagg, adjT[b]).astype(BF)
         dy_s[msg, at] = (dxw.astype(F32) + dagg.astype(F32)).astype(BF)
 
+    stages = (
+        branches, branch_norms, raise_up, gate, lower_down, out_norm, readout, out_back,
+        down_back, gate_back, up_back, norms_back, branches_back,
+    )
+    _wave(subs, MID_SKEW, stages)
+
     def attend_back(b):
         at = lanes(b)
-        for h in range(HEADS):
+        def score(h):
             ds_s[h] = _tn(y_s[head(2, h), at], datt_s[head(0, h), at]).astype(BF)
-        for h in range(HEADS):
-            for c in range(0, nodes, LANES):
-                cut = slice(c, c + LANES)
-                pf = pf_s[b, h, :, cut]
-                t = ds_s[h, :, cut].astype(F32) * pf
-                ds = (t - pf * jnp.sum(t, axis=0, keepdims=True)) * scale
-                ds_s[h, :, cut] = ds.astype(BF)
-                p_s[h, :, cut] = pf.astype(BF)
-        for h in range(HEADS):
-            dy_s[head(2, h), at] = _nt(datt_s[head(0, h), at], p_s[h]).astype(BF)
+
+        def soften(h):
+            pf = pf_s[b, h]
+            t = ds_s[h].astype(F32) * pf
+            ds_s[h] = ((t - pf * jnp.sum(t, axis=0, keepdims=True)) * scale).astype(BF)
+
+        def blend(h):
+            dy_s[head(2, h), at] = _nt(datt_s[head(0, h), at], p_s[b, h]).astype(BF)
             dy_s[head(0, h), at] = _nn(y_s[head(1, h), at], ds_s[h]).astype(BF)
             dy_s[head(1, h), at] = _nt(y_s[head(0, h), at], ds_s[h]).astype(BF)
+
+        _wave(HEADS, BWD_SKEW, (score, soften, blend))
 
     _over(subs, BWD_GROUP, attend_back)
 
@@ -423,7 +473,7 @@
             pltpu.VMEM((hidden, total), BF),
             pltpu.VMEM((feats, total), BF),
             pltpu.VMEM((subs, HEADS, nodes, nodes), F32),
-            pltpu.VMEM((HEADS, nodes, nodes), BF),
+            pltpu.VMEM((subs, HEADS, nodes, nodes), BF),
             pltpu.VMEM((HEADS, nodes, nodes), BF),
             pltpu.VMEM((8, LANES), F32),
             pltpu.VMEM((feats, 5 * feats), BF),

time: 74.2 us -> 67.1 us (0.904)
  Pallas kernels: 27.2 us -> 20 us
    pallas_call x1, Pallas kernels: 22.3 us -> 15.2 us  [local_step(): pl.pallas_call(lambda *refs: _step_kernel(packed, *refs), in_specs=_vmem(...]
  transfers between devices with their start and end apart: 2 -> 2, of which waited for: 2 -> 2; matrix products, arithmetic and copies ran while one was open for 0% -> 0% of each run, Pallas kernels for 5% -> 6%
where the time goes in v4:
time: 67.1 us; the launch traced here: 66.8 us
  blocking collectives  33.6 us (50%)
  Pallas kernels  20 us (30%)
  waiting for transfers between devices  5.13 us (8%)
  starting transfers between devices  3.57 us (5%)
  local copies, waits for them, and re-layouts  2.99 us (4%)
  between operations  0.7 us (1%)
  other arithmetic  0.68 us (1%)
    all_to_all x1, blocking collectives, shards(): lax.all_to_all(paired, 'store', split_axis=0, concat_axis=0, tiled=True,...  20.1 us
    pallas_call x1, Pallas kernels, local_step(): pl.pallas_call(lambda *refs: _step_kernel(packed, *refs), in_specs=_vmem(...  15.2 us
    all_to_all x1, blocking collectives, shards(): lax.all_to_all(requests, 'store', split_axis=0, concat_axis=0, tiled=True)  13.6 us
    pallas_call x1, Pallas kernels, _prep(): pl.pallas_call(_prep_kernel, in_specs=[pl.BlockSpec(memory_space=pltpu.HB...  3.76 us
    all_to_all x1, starting transfers between devices, shards(): lax.all_to_all(picked, 'store', split_axis=0, concat_axis=0, tiled=True)  3.5 us
    all_to_all x1, waiting for transfers between devices, shards(): lax.all_to_all(picked, 'store', split_axis=0, concat_axis=0, tiled=True)  3.09 us
    ppermute x1, waiting for transfers between devices, shards(): got = lax.ppermute(send, 'store', [(i, i ^ 1) for i in range(groups)])  2.04 us
    gather x1, local copies, waits for them, and re-layouts, shards(): jnp.take(store_feats, lax.all_to_all(requests, 'store', split_axis=0, con...  1.48 us
  transfers between devices with their start and end apart: 2, of which 2 were waited for; matrix products, arithmetic and copies ran while one was open for 0% of the time, Pallas kernels for 6%

profile of v4, /device:TPU:0, one launch (start us, length us, event | category | flops | bytes accessed | tf_op | source)
XLA Modules:
  0.0 66.8 jit_solution(16198213692399150483)
XLA Ops:
  0.6 0.0 copy-start
  0.6 0.9 %copy.21 = s32[16,1,8]{2,1,0:T(1,128)S(1)} copy(s32[16,1,8]{0,2,1:T(8,128)} %bitcast.7) | data formatting | bytes 1024 | tf_op jit(solution)/shard_map/all_to_all | solution.py:510
  1.6 13.6 %all_to_all.19 = s32[16,1,8]{2,1,0:T(1,128)S(1)} all-to-all(s32[16,1,8]{2,1,0:T(1,128)S(1)} %copy.21), channel_id=1, replica_groups=mesh['parts'=2,'store'=16] {'store'}, dimensions={0} | all-to-all | bytes 1024 | tf_op jit(solution)/shard_map/all_to_all | solution.py:510
  15.1 0.5 broadcast.7
  15.6 0.7 %reduce.3 = s32[16,8]{1,0:T(8,128)S(1)} reduce(s32[16,1,8]{2,1,0:T(1,128)S(1)} %all_to_all.19, s32[]{:T(128)} %broadcast.7), dimensions={1}, to_apply=%all_to_all.13.reduce_sub_computation.3 | reduce | bytes 1028 | tf_op jit(solution)/shard_map/all_to_all | solution.py:510
  16.3 0.1 reshape.27
  16.4 0.0 copy-done
  16.4 1.5 %gather_fusion = bf16[128,256]{1,0:T(8,128)(2,1)} fusion(bf16[4096,256]{1,0:T(8,128)(2,1)S(1)} %copy-done, s32[1024]{0:T(1024)S(1)} %pad_clamp_fusion), kind=kCustom, calls=%fused_computation | custom fusion | bytes 131584 | tf_op jit(solution)/shard_map/jit(_take)/gather | solution.py:508
  17.9 3.5 %all-to-all-start.1 = ((bf16[16,8,256]{2,1,0:T(8,128)(2,1)}), bf16[16,8,256]{2,1,0:T(8,128)(2,1)S(1)}, u32[]{:S(2)}, u32[]{:S(2)}) async-start(bf16[16,8,256]{2,1,0:T(8,128)(2,1)} %bitcast.1), calls=%async_computation.1 | async-start | bytes 131072 | tf_op jit(solution)/shard_map/all_to_all | solution.py:514
  21.4 3.8 %prep.1 = (bf16[128,1024]{1,0:T(8,128)(2,1)}, bf16[1024,256]{1,0:T(8,128)(2,1)}, bf16[4,256,256]{2,1,0:T(8,128)(2,1)}, f32[4,256]{1,0:T(4,128)}, bf16[256,256]{1...) custom-call(bf16[256,768]{1,0:T(8,128)(2,1)} %wqkv_h.1, ...), custom_call_target="tpu_custom_call" | custom-call | flops 536870912 | bytes 8388608 | tf_op jit(solution)/shard_map/prep/pallas_call | solution.py:123
  25.2 3.1 %all-to-all-done.1 = bf16[16,8,256]{2,1,0:T(8,128)(2,1)S(1)} async-done(((bf16[16,8,256]{2,1,0:T(8,128)(2,1)}), bf16[16,8,256]{2,1,0:T(8,128)(2,1)S(1)}, u32[]{:S(2)}, u32[]{:S(2)}) %all-to-all-start.1) | async-done | bytes 65568 | tf_op jit(solution)/shard_map/all_to_all | solution.py:514
  28.3 15.2 %graph_step.1 = (f32[4,64]{1,0:T(4,128)}, bf16[8,16,2432]{2,1,0:T(8,128)(2,1)S(1)}, bf16[8,16,2432]{2,1,0:T(8,128)(2,1)S(1)}) custom-call(bf16[128,256]{1,0:T(8,128)(2,1)S(1)} %bitcast.6, bf16[128,1024]{1,0:T(8,128)(2,1)} %get-tuple-element.25.refs_1_, bf16[1024,256]{1,0:T(8,128)(2,1)} %get-tuple-element.26.refs_2_, ...), custom_call_target="tpu_custom_call" | custom-call | tf_op jit(solution)/shard_map/graph_step/pallas_call | solution.py:458
  43.5 0.1 collective-permute-start
  43.6 2.0 %collective-permute-done.b_ref = bf16[8,16,2432]{2,1,0:T(8,128)(2,1)S(1)} collective-permute-done((bf16[8,16,2432]{2,1,0:T(8,128)(2,1)S(1)}, bf16[8,16,2432]{2,1,0:T(8,128)(2,1)S(1)}, u32[]{:S(2)}, u32[]{:S(2)}) %collective-permute-start) | collective-permute-done | bytes 622624 | tf_op jit(solution)/shard_map/ppermute | solution.py:521
  45.6 0.3 pair_sum.1
  45.9 20.1 %all_to_all.20.in_ref = bf16[8,16,2432]{2,1,0:T(8,128)(2,1)S(1)} all-to-all(bf16[8,16,2432]{2,1,0:T(8,128)(2,1)S(1)} %pair_sum.1), channel_id=1, replica_groups={{0,2,4,6,8,10,12,14},{1,3,5,7,9,11,13,15},{16,18,20,22,24,26,28,30},{17..., dimensions={0} | all-to-all | bytes 1245184 | tf_op jit(solution)/shard_map/all_to_all | solution.py:531
  66.0 0.7 %final_sum.1 = (f32[1]{0:T(128)}, f32[16,768]{1,0:T(8,128)}, f32[16,256]{1,0:T(8,128)}, f32[16,256]{1,0:T(8,128)}, f32[16,512]{1,0:T(8,128)}, /*index=5*/f32[32,256]{1,0:T(8,128)}) custom-call(bf16[8,16,2432]{2,1,0:T(8,128)(2,1)S(1)} %all_to_all.20.in_ref), custom_call_target="tpu_custom_call" | custom-call | tf_op jit(solution)/shard_map/final_sum/pallas_call | solution.py:534
  (1 shorter events, 0.0 us)
Async XLA Ops:
  0.6 15.8 %copy-start = (bf16[4096,256]{1,0:T(8,128)(2,1)S(1)}, bf16[4096,256]{1,0:T(8,128)(2,1)}, u32[]{:S(2)}) copy-start(bf16[4096,256]{1,0:T(8,128)(2,1)} %param.12) | copy-start | bytes 6291460
  17.9 10.4 %all-to-all-start.1 = ((bf16[16,8,256]{2,1,0:T(8,128)(2,1)}), bf16[16,8,256]{2,1,0:T(8,128)(2,1)S(1)}, u32[]{:S(2)}, u32[]{:S(2)}) async-start(bf16[16,8,256]{2,1,0:T(8,128)(2,1)} %bitcast.1), calls=%async_computation.1 | async-start | bytes 131072 | tf_op jit(solution)/shard_map/all_to_all | solution.py:514
  43.5 2.1 %collective-permute-start = (bf16[8,16,2432]{2,1,0:T(8,128)(2,1)S(1)}, bf16[8,16,2432]{2,1,0:T(8,128)(2,1)S(1)}, u32[]{:S(2)}, u32[]{:S(2)}) collective-permute-start(bf16[8,16,2432]{2,1,0:T(8,128)(2,1)S(1)} %get-tuple-element.36), channel_id=1, source_target_pairs={{0,1},{1,0},{2,3},{3,2},{4,5},{5,4},{6,7},{7,6},{8,9},{9,8},{10,11... | collective-permute-start | bytes 1867784 | tf_op jit(solution)/shard_map/ppermute | solution.py:521

commit v5 on v4

--- a/solution.py
+++ b/solution.py
@@ -47,20 +47,41 @@
 LANES = 128
 
 
+def _serve_kernel(wanted, store, out, column):
+    peers, _, cap = wanted.shape
+    diagonal = lax.broadcasted_iota(jnp.int32, (cap, cap), 0) == lax.broadcasted_iota(
+        jnp.int32, (cap, cap), 1
+    )
+    for o in range(peers):
+        row = jnp.where(diagonal, wanted[o], 0)
+        column[o * cap : (o + 1) * cap, :] = jnp.sum(row, axis=1, keepdims=True)
+    rows = store.shape[0]
+    step = rows // 4 if rows % 512 == 0 else rows
+    lane = lax.broadcasted_iota(jnp.int32, (out.shape[0], step), 1)
+    total = jnp.zeros(out.shape, F32)
+    for at in range(0, rows, step):
+        hot = (lane == column[...] - at).astype(F32).astype(BF)
+        total = total + _nn(hot, store[at : at + step, :])
+    out[...] = total.astype(out.dtype)
+
+
 def _prep_kernel(
-    wqkv_h, wo_h, wmsg_h, wup_h, wdown_h, edges_h, pairs_h, slots_h, wread_h, *refs
+    wqkv_h, wo_h, wmsg_h, wup_h, wdown_h, edges_h, pairs_h, slots_h, wread_h, store_h, *refs
 ):
-    results = refs[:9]
-    pick, wqmT, adjT, deg, woT, wupT, wdownT, hot, wcol = refs[9:18]
-    wqkv, wmsg, wo, wup, wdown, edges, pairs, slots, wread, sems, out_sems = refs[18:]
+    pick, wqmT = refs[:2]
+    results = refs[2:9]
+    store = refs[9]
+    adjT, deg, woT, wupT, wdownT, hot, wcol = refs[10:17]
+    wqkv, wmsg, wo, wup, wdown, edges, pairs, slots, wread, sems, out_sems = refs[17:]
     moves = [
         (edges_h, edges), (slots_h, slots), (pairs_h, pairs), (wread_h, wread),
         (wqkv_h, wqkv), (wmsg_h, wmsg), (wo_h, wo), (wup_h, wup), (wdown_h, wdown),
+        (store_h, store),
     ]
     copies = [pltpu.make_async_copy(s, d, sems.at[i]) for i, (s, d) in enumerate(moves)]
     sends = [
         pltpu.make_async_copy(s, d, out_sems.at[i])
-        for i, (s, d) in enumerate(zip(refs[9:18], results))
+        for i, (s, d) in enumerate(zip(refs[10:17], results))
     ]
     for c in copies:
         c.start()
@@ -90,28 +111,28 @@
         pick[:, at] = (ir == slots[pl.ds(b, 1), :]).astype(F32).astype(BF)
 
     wcol[...] = jnp.broadcast_to(wread[...], (2 * n_pairs, feats)).T
-    for i in (0, 2, 3, 7, 8):
+    for i in (0, 1, 5, 6):
         sends[i].start()
-    for c in copies[4:]:
+    for c in copies[4:9]:
         c.wait()
     wqmT[0 : 3 * feats, :] = wqkv[...].T
     wqmT[3 * feats : 4 * feats, :] = wmsg[...].T
-    sends[1].start()
     woT[...] = wo[...].T
+    sends[2].start()
+    wupT[...] = wup[...].T
+    sends[3].start()
+    wdownT[...] = wdown[...].T
     sends[4].start()
-    wupT[...] = wup[...].T
-    sends[5].start()
-    wdownT[...] = wdown[...].T
-    sends[6].start()
     for c in sends:
         c.wait()
+    copies[9].wait()
 
 
 def _hbm(*arrays):
     return [pltpu.with_memory_space_constraint(v, pltpu.HBM) for v in arrays]
 
 
-def _prep(w_qkv, w_o, w_msg, w_up, w_down, edges, pairs, node_slots, w_read, rows):
+def _prep(w_qkv, w_o, w_msg, w_up, w_down, edges, pairs, node_slots, w_read, store, rows):
     feats, hidden = w_up.shape
     subs, nodes = node_slots.shape
     n_edges, n_pairs = edges.shape[1], pairs.shape[1]
@@ -122,10 +143,12 @@
     ]
     return pl.pallas_call(
         _prep_kernel,
-        in_specs=[pl.BlockSpec(memory_space=pltpu.HBM)] * 9,
-        out_specs=[pl.BlockSpec(memory_space=pltpu.HBM)] * len(out),
-        out_shape=[pltpu.HBM(s, d) for s, d in out],
-        scratch_shapes=[pltpu.VMEM(s, d) for s, d in out]
+        in_specs=[pl.BlockSpec(memory_space=pltpu.HBM)] * 10,
+        out_specs=_vmem(2) + [pl.BlockSpec(memory_space=pltpu.HBM)] * 7 + _vmem(1),
+        out_shape=[pltpu.VMEM(s, d) for s, d in out[:2]]
+        + [pltpu.HBM(s, d) for s, d in out[2:]]
+        + [pltpu.VMEM(store.shape, store.dtype)],
+        scratch_shapes=[pltpu.VMEM(s, d) for s, d in out[2:]]
         + [
             pltpu.VMEM((feats, 3 * feats), BF),
             pltpu.VMEM((feats, feats), BF),
@@ -136,8 +159,8 @@
             pltpu.VMEM((subs, 2, n_pairs), jnp.int32),
             pltpu.VMEM((subs, nodes), jnp.int32),
             pltpu.VMEM((1, feats), F32),
-            pltpu.SemaphoreType.DMA((9,)),
-            pltpu.SemaphoreType.DMA((9,)),
+            pltpu.SemaphoreType.DMA((10,)),
+            pltpu.SemaphoreType.DMA((7,)),
         ],
         compiler_params=pltpu.CompilerParams(vmem_limit_bytes=24 << 20),
         cost_estimate=pl.CostEstimate(
@@ -147,7 +170,7 @@
     )(
         *_hbm(
             w_qkv, w_o, w_msg, w_up, w_down, edges.transpose(0, 2, 1),
-            pairs.transpose(0, 2, 1), node_slots, w_read.reshape(1, feats),
+            pairs.transpose(0, 2, 1), node_slots, w_read.reshape(1, feats), store,
         )
     )
 
@@ -184,21 +207,19 @@
 
 
 def _step_kernel(packed, *refs):
-    fetched_ref = refs[0]
-    sources = refs[1:14]
+    fetched_ref, pick, wqmT = refs[:3]
+    sources = refs[3:14]
     preds_ref = refs[14]
     outs = refs[15 : 15 + (2 if packed else 6)]
     refs = refs[15 + len(outs) :]
-    (
-        pick, wqmT, adjT, deg, woT, wupT, wdownT, hot_ref, wcol, targets_ref, wo, wup, wdown,
-    ) = refs[:13]
+    adjT, deg, woT, wupT, wdownT, hot_ref, wcol, targets_ref, wo, wup, wdown = refs[:11]
     (
         x_s, y_s, dy_s, att_s, datt_s, h_s, g_s, do_s, dup_s, da_s, pf_s, p_s, ds_s, obj_s, gq_s, gu_s, gd_s,
         agg_s, n1_s, n2_s, up_s, out_s, dout_s, hi_s, lo_s, r1_s, r2_s, r3_s,
         sems,
-    ) = refs[13:]
+    ) = refs[11:]
     copies = [
-        pltpu.make_async_copy(s, d, sems.at[i]) for i, (s, d) in enumerate(zip(sources, refs[:13]))
+        pltpu.make_async_copy(s, d, sems.at[i]) for i, (s, d) in enumerate(zip(sources, refs[:11]))
     ]
     for c in copies:
         c.start()
@@ -219,10 +240,7 @@
         return slice(part * feats + h * hd, part * feats + (h + 1) * hd)
 
     obj_s[...] = jnp.zeros_like(obj_s)
-    fetT = fetched_ref[...].T
-    copies[0].wait()
-    x_s[...] = _nn(fetT, pick[...]).astype(BF)
-    copies[1].wait()
+    x_s[...] = _nn(fetched_ref[...].T, pick[...]).astype(BF)
     y_s[...] = _nn(wqmT[...], x_s[...]).astype(BF)
 
     def attend(b):
@@ -243,7 +261,7 @@
         _wave(HEADS, FWD_SKEW, (score, soften, blend))
 
     _over(subs, FWD_GROUP, attend)
-    for c in copies[2:]:
+    for c in copies:
         c.wait()
 
     total = subs * nodes
@@ -369,21 +387,23 @@
     obj = jnp.sum(obj_s[0:1, :], axis=1, keepdims=True) / n_all
     if packed:
         keep_ref, send_ref = outs
-        slabs, rows, width = keep_ref.shape
+        slabs = keep_ref.shape[0]
+        rows = feats // (2 * slabs)
         core = lax.axis_index("store") % 2
-        obj_block = _spread(obj, rows)
-        cut = feats * 5
+        obj_block = _spread(obj, TAIL)
+        per = hidden // feats
         for ref, side in ((keep_ref, core), (send_ref, 1 - core)):
             for j in range(slabs):
                 d = 2 * j + side
                 r = pl.ds(pl.multiple_of(d * rows, rows), rows)
-                ref[j, :, 0:cut] = gq_s[r, :]
-                ref[j, :, cut : cut + hidden] = gu_s[r, :]
-                for i in range(hidden // feats):
-                    r = pl.ds(pl.multiple_of(d * (rows * hidden // feats) + i * rows, rows), rows)
-                    w = cut + hidden + i * feats
-                    ref[j, :, w : w + feats] = gd_s[r, :]
-                ref[j, :, width - LANES : width] = obj_block
+                pieces = [gq_s[r, c : c + LANES] for c in range(0, 5 * feats, LANES)]
+                pieces += [gu_s[r, c : c + LANES] for c in range(0, hidden, LANES)]
+                for i in range(per):
+                    r = pl.ds(pl.multiple_of(d * (rows * per) + i * rows, rows), rows)
+                    pieces += [gd_s[r, c : c + LANES] for c in range(0, feats, LANES)]
+                for i, piece in enumerate(pieces):
+                    ref[j, i * rows : (i + 1) * rows, :] = piece
+                ref[j, len(pieces) * rows :, :] = obj_block
     else:
         obj_ref, gqkv_ref, go_ref, gmsg_ref, gup_ref, gdown_ref = outs
         obj_ref[...] = jnp.broadcast_to(obj, obj_ref.shape)
@@ -407,31 +427,35 @@
     return block[0:1, 0:1] + block[0:1, 32:33] + block[0:1, 64:65]
 
 
+TAIL = 8
+
+
 def _pair_kernel(a_ref, b_ref, o_ref):
-    slabs, rows, width = o_ref.shape
+    slabs, rows, _ = o_ref.shape
     o_ref[...] = (a_ref[...].astype(F32) + b_ref[...].astype(F32)).astype(BF)
-    blk = a_ref[0, :, width - LANES : width].astype(F32), b_ref[0, :, width - LANES : width].astype(F32)
-    obj = _spread(_gather_terms(blk[0]) + _gather_terms(blk[1]), rows)
+    a = a_ref[0, rows - TAIL :, :].astype(F32)
+    b = b_ref[0, rows - TAIL :, :].astype(F32)
+    obj = _spread(_gather_terms(a) + _gather_terms(b), TAIL)
     for j in range(slabs):
-        o_ref[j, :, width - LANES : width] = obj
+        o_ref[j, rows - TAIL :, :] = obj
 
 
 def _final_kernel(in_ref, loss_ref, gqkv, go, gmsg, gup, gdown):
-    slabs, rows, width = in_ref.shape
+    slabs, height, _ = in_ref.shape
     total = in_ref[0].astype(F32)
     for j in range(1, slabs):
         total = total + in_ref[j].astype(F32)
-    feats = go.shape[1]
+    rows, feats = go.shape
     hidden = gup.shape[1]
-    gqkv[...] = total[:, 0 : 3 * feats]
-    gmsg[...] = total[:, 3 * feats : 4 * feats]
-    go[...] = total[:, 4 * feats : 5 * feats]
-    gup[...] = total[:, 5 * feats : 5 * feats + hidden]
+    places = [(gqkv, 0, c) for c in range(0, 3 * feats, LANES)]
+    places += [(gmsg, 0, c) for c in range(0, feats, LANES)]
+    places += [(go, 0, c) for c in range(0, feats, LANES)]
+    places += [(gup, 0, c) for c in range(0, hidden, LANES)]
     for i in range(hidden // feats):
-        w = 5 * feats + hidden + i * feats
-        gdown[i * rows : (i + 1) * rows, :] = total[:, w : w + feats]
-    loss = _gather_terms(total[:, width - LANES : width]) / (2 * slabs)
-    loss_ref[0] = jnp.sum(loss)
+        places += [(gdown, i * rows, c) for c in range(0, feats, LANES)]
+    for i, (ref, r, c) in enumerate(places):
+        ref[r : r + rows, c : c + LANES] = total[i * rows : (i + 1) * rows, :]
+    loss_ref[0] = jnp.sum(_gather_terms(total[height - TAIL :, :]) / (2 * slabs))
 
 
 def _vmem(n):
@@ -443,12 +467,13 @@
     subs, nodes = prep[3].shape
     n_pairs = targets.shape[1]
     total = subs * nodes
-    sources = (*prep, targets, *weights)
+    sources = (*prep[2:], targets, *weights)
     rows = feats // groups
     packed = groups % 2 == 0 and feats % groups == 0 and hidden % feats == 0 and rows % 16 == 0
+    packed = packed and feats % LANES == 0
     out = [((subs, n_pairs), F32)]
     if packed:
-        slab = (groups // 2, rows, 5 * feats + 2 * hidden // feats * feats + LANES)
+        slab = (groups // 2, rows * (5 * feats + 2 * hidden) // LANES + TAIL, LANES)
         out += [(slab, BF), (slab, BF)]
     else:
         out += [
@@ -457,7 +482,7 @@
         ]
     res = pl.pallas_call(
         lambda *refs: _step_kernel(packed, *refs),
-        in_specs=_vmem(1) + [pl.BlockSpec(memory_space=pltpu.HBM)] * len(sources),
+        in_specs=_vmem(3) + [pl.BlockSpec(memory_space=pltpu.HBM)] * len(sources),
         out_specs=_vmem(len(out)),
         out_shape=[jax.ShapeDtypeStruct(s, d) for s, d in out],
         scratch_shapes=[pltpu.VMEM(v.shape, v.dtype) for v in sources]
@@ -492,9 +517,9 @@
             pltpu.VMEM((8, total), F32),
             pltpu.SemaphoreType.DMA((len(sources),)),
         ],
-        compiler_params=pltpu.CompilerParams(vmem_limit_bytes=44 << 20),
+        compiler_params=pltpu.CompilerParams(vmem_limit_bytes=40 << 20),
         name="graph_step",
-    )(fetched, *_hbm(*sources))
+    )(fetched, *prep[:2], *_hbm(*sources))
     return packed, res
 
 
@@ -505,19 +530,29 @@
     feats = store_feats.shape[1]
     hidden = w_up.shape[1]
     groups = lax.axis_size("store")
-    picked = jnp.take(
-        store_feats,
-        lax.all_to_all(requests, "store", split_axis=0, concat_axis=0, tiled=True),
-        axis=0,
-        mode="clip",
+    wanted = lax.all_to_all(
+        requests.reshape(groups, 1, -1), "store", split_axis=0, concat_axis=0, tiled=True
     )
+    *prep, store = _prep(
+        w_qkv, w_o, w_msg, w_up, w_down, edges, pairs, node_slots, w_read, store_feats,
+        wanted.size,
+    )
+    picked = pl.pallas_call(
+        _serve_kernel,
+        in_specs=_vmem(2),
+        out_specs=pl.BlockSpec(memory_space=pltpu.VMEM),
+        out_shape=jax.ShapeDtypeStruct((wanted.size, feats), store_feats.dtype),
+        scratch_shapes=[pltpu.VMEM((wanted.size, 1), jnp.int32)],
+        compiler_params=pltpu.CompilerParams(vmem_limit_bytes=16 << 20),
+        name="serve",
+    )(wanted, store)
+    picked = picked.reshape(groups, -1, feats)
     fetched = lax.all_to_all(picked, "store", split_axis=0, concat_axis=0, tiled=True)
     fetched = fetched.reshape(-1, feats)
-    prep = _prep(w_qkv, w_o, w_msg, w_up, w_down, edges, pairs, node_slots, w_read, fetched.shape[0])
     packed, (preds, *terms) = local_step(prep, fetched, targets, (w_o, w_up, w_down), groups)
     if packed:
         keep, send = terms
-        rows = keep.shape[1]
+        rows = feats // groups
         got = lax.ppermute(send, "store", [(i, i ^ 1) for i in range(groups)])
         paired = pl.pallas_call(
             _pair_kernel,

time: 67.1 us -> 63.9 us (0.952)
  blocking collectives: 33.6 us -> 29.7 us
  starting transfers between devices: 3.57 us -> 7.46 us
  local copies, waits for them, and re-layouts: 2.99 us -> 1.36 us
  other arithmetic: 0.68 us -> 0 us
    all_to_all x1, starting transfers between devices: 3.5 us -> 7.39 us  [shards(): lax.all_to_all(requests.reshape(groups, 1, -1), 'store', split_axis=0, co...]
    all_to_all x1, blocking collectives: 13.6 us -> 9.96 us  [shards(): lax.all_to_all(picked, 'store', split_axis=0, concat_axis=0, tiled=True)]
    gather x1 -> x0, local copies, waits for them, and re-layouts: 1.48 us -> none  [shards(): jnp.take(store_feats, lax.all_to_all(requests, 'store', split_axis=0, con...]
    all_to_all x2 -> x0, local copies, waits for them, and re-layouts: 1.42 us -> none  [shards(): lax.all_to_all(requests, 'store', split_axis=0, concat_axis=0, tiled=True)]
    reshape x0 -> x1, local copies, waits for them, and re-layouts: none -> 1.36 us  [shards(): requests.reshape(groups, 1, -1)]
    pallas_call x1, Pallas kernels: 15.2 us -> 14.2 us  [local_step(): pl.pallas_call(lambda *refs: _step_kernel(packed, *refs), in_specs=_vmem(...]
    pallas_call x0 -> x1, Pallas kernels: none -> 0.71 us  [shards(): pl.pallas_call(_serve_kernel, in_specs=_vmem(2), out_specs=pl.BlockSpec(m...]
where the time goes in v5:
time: 63.9 us; the launch traced here: 63.6 us
  blocking collectives  29.7 us (46%)
  Pallas kernels  19.6 us (31%)
  starting transfers between devices  7.46 us (12%)
  waiting for transfers between devices  4.76 us (7%)
  local copies, waits for them, and re-layouts  1.36 us (2%)
  between operations  0.68 us (1%)
    all_to_all x1, blocking collectives, shards(): lax.all_to_all(paired, 'store', split_axis=0, concat_axis=0, tiled=True,...  19.8 us
    pallas_call x1, Pallas kernels, local_step(): pl.pallas_call(lambda *refs: _step_kernel(packed, *refs), in_specs=_vmem(...  14.2 us
    all_to_all x1, blocking collectives, shards(): lax.all_to_all(picked, 'store', split_axis=0, concat_axis=0, tiled=True)  9.96 us
    all_to_all x1, starting transfers between devices, shards(): lax.all_to_all(requests.reshape(groups, 1, -1), 'store', split_axis=0, co...  7.39 us
    pallas_call x1, Pallas kernels, _prep(): pl.pallas_call(_prep_kernel, in_specs=[pl.BlockSpec(memory_space=pltpu.HB...  3.58 us
    all_to_all x1, waiting for transfers between devices, shards(): lax.all_to_all(requests.reshape(groups, 1, -1), 'store', split_axis=0, co...  2.74 us
    ppermute x1, waiting for transfers between devices, shards(): got = lax.ppermute(send, 'store', [(i, i ^ 1) for i in range(groups)])  2.01 us
    reshape x1, local copies, waits for them, and re-layouts, shards(): requests.reshape(groups, 1, -1)  1.36 us
  transfers between devices with their start and end apart: 2, of which 2 were waited for; matrix products, arithmetic and copies ran while one was open for 0% of the time, Pallas kernels for 6%

profile of v5, /device:TPU:0, one launch (start us, length us, event | category | flops | bytes accessed | tf_op | source)
XLA Modules:
  0.0 63.6 jit_solution(14140558665271731388)
XLA Ops:
  0.6 1.4 %copy.19 = s32[16,1,8]{2,1,0:T(1,128)} copy(s32[16,1,8]{0,2,1:T(8,128)} %bitcast.10) | data formatting | bytes 1024 | tf_op jit(solution)/shard_map/reshape | solution.py:534
  2.0 7.4 %all-to-all-start = ((s32[16,1,8]{2,1,0:T(1,128)}), s32[16,1,8]{2,1,0:T(1,128)S(1)}, u32[]{:S(2)}, u32[]{:S(2)}) async-start(s32[16,1,8]{2,1,0:T(1,128)} %copy.19), calls=%async_computation | async-start | bytes 16384 | tf_op jit(solution)/shard_map/all_to_all | solution.py:533
  9.4 3.6 %prep.1 = (bf16[128,1024]{1,0:T(8,128)(2,1)S(1)}, bf16[1024,256]{1,0:T(8,128)(2,1)S(1)}, bf16[4,256,256]{2,1,0:T(8,128)(2,1)}, f32[4,256]{1,0:T(4,128)}, bf16[25...) custom-call(bf16[256,768]{1,0:T(8,128)(2,1)} %wqkv_h.1, ...), custom_call_target="tpu_custom_call" | custom-call | flops 536870912 | bytes 8388608 | tf_op jit(solution)/shard_map/prep/pallas_call | solution.py:144
  13.0 2.7 %all-to-all-done.wanted = s32[16,1,8]{2,1,0:T(1,128)S(1)} async-done(((s32[16,1,8]{2,1,0:T(1,128)}), s32[16,1,8]{2,1,0:T(1,128)S(1)}, u32[]{:S(2)}, u32[]{:S(2)}) %all-to-all-start) | async-done | bytes 544 | tf_op jit(solution)/shard_map/all_to_all | solution.py:533
  15.7 0.7 %serve.1 = bf16[128,256]{1,0:T(8,128)(2,1)S(1)} custom-call(s32[16,1,8]{2,1,0:T(1,128)S(1)} %all-to-all-done.wanted, bf16[4096,256]{1,0:T(8,128)(2,1)S(1)} %get-tuple-element.26.store), custom_call_target="tpu_custom_call" | custom-call | tf_op jit(solution)/shard_map/serve/pallas_call | solution.py:540
  16.4 10.0 %all_to_all.15 = bf16[16,8,256]{2,1,0:T(8,128)(2,1)S(1)} all-to-all(bf16[16,8,256]{2,1,0:T(8,128)(2,1)S(1)} %bitcast.6), channel_id=1, replica_groups=mesh['parts'=2,'store'=16] {'store'}, dimensions={0} | all-to-all | bytes 131072 | tf_op jit(solution)/shard_map/all_to_all | solution.py:550
  26.4 14.2 %graph_step.1 = (f32[4,64]{1,0:T(4,128)}, bf16[8,296,128]{2,1,0:T(8,128)(2,1)S(1)}, bf16[8,296,128]{2,1,0:T(8,128)(2,1)S(1)}) custom-call(bf16[128,256]{1,0:T(8,128)(2,1)S(1)} %bitcast.7, bf16[128,1024]{1,0:T(8,128)(2,1)S(1)} %get-tuple-element.27.refs_1_, bf16[1024,256]{1,0:T(8,128)(2,1)S(1)} %get-tuple-element.28.refs_2_, ...), custom_call_target="tpu_custom_call" | custom-call | tf_op jit(solution)/shard_map/graph_step/pallas_call | solution.py:483
  40.7 0.1 collective-permute-start
  40.7 2.0 %collective-permute-done.b_ref = bf16[8,296,128]{2,1,0:T(8,128)(2,1)S(1)} collective-permute-done((bf16[8,296,128]{2,1,0:T(8,128)(2,1)S(1)}, bf16[8,296,128]{2,1,0:T(8,128)(2,1)S(1)}, u32[]{:S(2)}, u32[]{:S(2)}) %collective-permute-start) | collective-permute-done | bytes 606240 | tf_op jit(solution)/shard_map/ppermute | solution.py:556
  42.7 0.4 pair_sum.1
  43.1 19.8 %all_to_all.16.in_ref = bf16[8,296,128]{2,1,0:T(8,128)(2,1)S(1)} all-to-all(bf16[8,296,128]{2,1,0:T(8,128)(2,1)S(1)} %pair_sum.1), channel_id=1, replica_groups={{0,2,4,6,8,10,12,14},{1,3,5,7,9,11,13,15},{16,18,20,22,24,26,28,30},{17..., dimensions={0} | all-to-all | bytes 1212416 | tf_op jit(solution)/shard_map/all_to_all | solution.py:566
  62.9 0.7 %final_sum.1 = (f32[1]{0:T(128)}, f32[16,768]{1,0:T(8,128)}, f32[16,256]{1,0:T(8,128)}, f32[16,256]{1,0:T(8,128)}, f32[16,512]{1,0:T(8,128)}, /*index=5*/f32[32,256]{1,0:T(8,128)}) custom-call(bf16[8,296,128]{2,1,0:T(8,128)(2,1)S(1)} %all_to_all.16.in_ref), custom_call_target="tpu_custom_call" | custom-call | tf_op jit(solution)/shard_map/final_sum/pallas_call | solution.py:569
Async XLA Ops:
  2.0 13.7 %all-to-all-start = ((s32[16,1,8]{2,1,0:T(1,128)}), s32[16,1,8]{2,1,0:T(1,128)S(1)}, u32[]{:S(2)}, u32[]{:S(2)}) async-start(s32[16,1,8]{2,1,0:T(1,128)} %copy.19), calls=%async_computation | async-start | bytes 16384 | tf_op jit(solution)/shard_map/all_to_all | solution.py:533
  40.7 2.1 %collective-permute-start = (bf16[8,296,128]{2,1,0:T(8,128)(2,1)S(1)}, bf16[8,296,128]{2,1,0:T(8,128)(2,1)S(1)}, u32[]{:S(2)}, u32[]{:S(2)}) collective-permute-start(bf16[8,296,128]{2,1,0:T(8,128)(2,1)S(1)} %get-tuple-element.38), channel_id=1, source_target_pairs={{0,1},{1,0},{2,3},{3,2},{4,5},{5,4},{6,7},{7,6},{8,9},{9,8},{10,11... | collective-permute-start | bytes 1818632 | tf_op jit(solution)/shard_map/ppermute | solution.py:556

commit v6 on v5

--- a/solution.py
+++ b/solution.py
@@ -414,37 +414,53 @@
         gdown_ref[...] = gd_s[...]
 
 
+def _weights(rows):
+    shape = (rows, LANES)
+    at = lax.broadcasted_iota(jnp.int32, shape, 0) * LANES + lax.broadcasted_iota(jnp.int32, shape, 1)
+    return 1.0 + at.astype(F32) / (rows * LANES)
+
+
 def _spread(value, rows):
-    full = jnp.broadcast_to(value, (rows, LANES))
-    hi = full.astype(BF).astype(F32)
-    mid = (full - hi).astype(BF).astype(F32)
-    lo = full - hi - mid
-    lane = lax.broadcasted_iota(jnp.int32, (rows, LANES), 1)
-    return jnp.where(lane < 32, hi, jnp.where(lane < 64, mid, jnp.where(lane < 96, lo, 0.0))).astype(BF)
+    return (value * _weights(rows)).astype(BF)
 
 
 def _gather_terms(block):
-    return block[0:1, 0:1] + block[0:1, 32:33] + block[0:1, 64:65]
+    w = _weights(block.shape[0])
+    return jnp.sum(block * w) / jnp.sum(w * w)
 
 
 TAIL = 8
 
 
-def _pair_kernel(a_ref, b_ref, o_ref):
-    slabs, rows, _ = o_ref.shape
-    o_ref[...] = (a_ref[...].astype(F32) + b_ref[...].astype(F32)).astype(BF)
-    a = a_ref[0, rows - TAIL :, :].astype(F32)
-    b = b_ref[0, rows - TAIL :, :].astype(F32)
-    obj = _spread(_gather_terms(a) + _gather_terms(b), TAIL)
-    for j in range(slabs):
-        o_ref[j, rows - TAIL :, :] = obj
-
-
-def _final_kernel(in_ref, loss_ref, gqkv, go, gmsg, gup, gdown):
-    slabs, height, _ = in_ref.shape
-    total = in_ref[0].astype(F32)
-    for j in range(1, slabs):
-        total = total + in_ref[j].astype(F32)
+def _pair_kernel(a_ref, b_ref, first_ref, second_ref):
+    cut = first_ref.shape[1]
+    first_ref[...] = a_ref[:, :cut, :].astype(F32) + b_ref[:, :cut, :].astype(F32)
+    second_ref[...] = a_ref[:, cut:, :].astype(F32) + b_ref[:, cut:, :].astype(F32)
+
+
+def _halving(halves, groups):
+    idx = lax.axis_index("store")
+    bits = groups.bit_length() - 2
+    orders = [list(range(1, bits + 1)) for _ in halves]
+    if bits > 1:
+        orders[1][:2] = [2, 1]
+    halves = [h.reshape((2,) * bits + h.shape[1:]) for h in halves]
+    for step in range(bits):
+        kept, got = [], []
+        for h, order in zip(halves, orders):
+            axis = bits - order[step]
+            bit = (idx >> order[step]) & 1
+            perm = [(i, i ^ (1 << order[step])) for i in range(groups)]
+            send = lax.dynamic_slice_in_dim(h, 1 - bit, 1, axis).astype(BF)
+            got.append(lax.ppermute(send, "store", perm))
+            kept.append(lax.dynamic_slice_in_dim(h, bit, 1, axis))
+        halves = [k + g.astype(F32) for k, g in zip(kept, got)]
+    return [h.reshape(h.shape[-2:]) for h in halves]
+
+
+def _final_kernel(groups, first_ref, second_ref, loss_ref, gqkv, go, gmsg, gup, gdown):
+    total = jnp.concatenate([first_ref[...], second_ref[...]], axis=0)
+    height = total.shape[0]
     rows, feats = go.shape
     hidden = gup.shape[1]
     places = [(gqkv, 0, c) for c in range(0, 3 * feats, LANES)]
@@ -455,7 +471,7 @@
         places += [(gdown, i * rows, c) for c in range(0, feats, LANES)]
     for i, (ref, r, c) in enumerate(places):
         ref[r : r + rows, c : c + LANES] = total[i * rows : (i + 1) * rows, :]
-    loss_ref[0] = jnp.sum(_gather_terms(total[height - TAIL :, :]) / (2 * slabs))
+    loss_ref[0] = _gather_terms(total[height - TAIL :, :]) / groups
 
 
 def _vmem(n):
@@ -470,7 +486,7 @@
     sources = (*prep[2:], targets, *weights)
     rows = feats // groups
     packed = groups % 2 == 0 and feats % groups == 0 and hidden % feats == 0 and rows % 16 == 0
-    packed = packed and feats % LANES == 0
+    packed = packed and feats % LANES == 0 and groups & (groups - 1) == 0
     out = [((subs, n_pairs), F32)]
     if packed:
         slab = (groups // 2, rows * (5 * feats + 2 * hidden) // LANES + TAIL, LANES)
@@ -554,21 +570,22 @@
         keep, send = terms
         rows = feats // groups
         got = lax.ppermute(send, "store", [(i, i ^ 1) for i in range(groups)])
+        height = keep.shape[1]
+        cut = height // 2 // 16 * 16
         paired = pl.pallas_call(
             _pair_kernel,
             in_specs=_vmem(2),
-            out_specs=pl.BlockSpec(memory_space=pltpu.VMEM),
-            out_shape=jax.ShapeDtypeStruct(keep.shape, BF),
+            out_specs=_vmem(2),
+            out_shape=[
+                jax.ShapeDtypeStruct((keep.shape[0], h, LANES), F32) for h in (cut, height - cut)
+            ],
             compiler_params=pltpu.CompilerParams(vmem_limit_bytes=8 << 20),
             name="pair_sum",
         )(keep, got)
-        sides = [[i for i in range(groups) if i % 2 == c] for c in (0, 1)]
-        shared = lax.all_to_all(
-            paired, "store", split_axis=0, concat_axis=0, tiled=True, axis_index_groups=sides
-        )
+        shared = _halving(list(paired), groups)
         loss, *shares = pl.pallas_call(
-            _final_kernel,
-            in_specs=_vmem(1),
+            lambda *refs: _final_kernel(groups, *refs),
+            in_specs=_vmem(2),
             out_specs=[pl.BlockSpec(memory_space=pltpu.SMEM)] + _vmem(5),
             out_shape=[
                 jax.ShapeDtypeStruct((1,), F32),
@@ -580,7 +597,7 @@
             ],
             compiler_params=pltpu.CompilerParams(vmem_limit_bytes=8 << 20),
             name="final_sum",
-        )(shared)
+        )(*shared)
     else:
         obj, *grads = terms
         shares = [

time: 63.9 us -> 59.7 us (0.934)
  blocking collectives: 29.7 us -> 9.98 us
  waiting for transfers between devices: 4.76 us -> 14.4 us
  starting transfers between devices: 7.46 us -> 13.3 us
    all_to_all x1 -> x0, blocking collectives: 19.8 us -> none  [shards(): lax.all_to_all(paired, 'store', split_axis=0, concat_axis=0, tiled=True,...]
    ppermute x0 -> x6, waiting for transfers between devices: none -> 9.69 us  [_halving(): got.append(lax.ppermute(send, 'store', perm))]
    ppermute x0 -> x6, starting transfers between devices: none -> 5.87 us  [_halving(): got.append(lax.ppermute(send, 'store', perm))]
  transfers between devices with their start and end apart: 2 -> 8, of which waited for: 2 -> 7; matrix products, arithmetic and copies ran while one was open for 0% -> 0% of each run, Pallas kernels for 6% -> 6%
where the time goes in v6:
time: 59.7 us; the launch traced here: 59.4 us
  Pallas kernels  19.3 us (32%)
  waiting for transfers between devices  14.4 us (24%)
  starting transfers between devices  13.3 us (22%)
  blocking collectives  9.98 us (17%)
  local copies, waits for them, and re-layouts  1.48 us (2%)
  between operations  0.75 us (1%)
    pallas_call x1, Pallas kernels, local_step(): pl.pallas_call(lambda *refs: _step_kernel(packed, *refs), in_specs=_vmem(...  14.2 us
    all_to_all x1, blocking collectives, shards(): lax.all_to_all(picked, 'store', split_axis=0, concat_axis=0, tiled=True)  9.98 us
    ppermute x6, waiting for transfers between devices, _halving(): got.append(lax.ppermute(send, 'store', perm))  9.69 us
    all_to_all x1, starting transfers between devices, shards(): lax.all_to_all(requests.reshape(groups, 1, -1), 'store', split_axis=0, co...  7.39 us
    ppermute x6, starting transfers between devices, _halving(): got.append(lax.ppermute(send, 'store', perm))  5.87 us
    pallas_call x1, Pallas kernels, _prep(): pl.pallas_call(_prep_kernel, in_specs=[pl.BlockSpec(memory_space=pltpu.HB...  3.59 us
    all_to_all x1, waiting for transfers between devices, shards(): lax.all_to_all(requests.reshape(groups, 1, -1), 'store', split_axis=0, co...  2.73 us
    ppermute x1, waiting for transfers between devices, shards(): got = lax.ppermute(send, 'store', [(i, i ^ 1) for i in range(groups)])  2.01 us
  transfers between devices with their start and end apart: 8, of which 7 were waited for; matrix products, arithmetic and copies ran while one was open for 0% of the time, Pallas kernels for 6%

profile of v6, /device:TPU:0, one launch (start us, length us, event | category | flops | bytes accessed | tf_op | source)
XLA Modules:
  0.0 59.4 jit_solution(6334331124819092378)
XLA Ops:
  0.6 1.4 %copy.19 = s32[16,1,8]{2,1,0:T(1,128)} copy(s32[16,1,8]{0,2,1:T(8,128)} %bitcast.20) | data formatting | bytes 1024 | tf_op jit(solution)/shard_map/reshape | solution.py:550
  2.0 7.4 %all-to-all-start = ((s32[16,1,8]{2,1,0:T(1,128)}), s32[16,1,8]{2,1,0:T(1,128)S(1)}, u32[]{:S(2)}, u32[]{:S(2)}) async-start(s32[16,1,8]{2,1,0:T(1,128)} %copy.19), calls=%async_computation | async-start | bytes 16384 | tf_op jit(solution)/shard_map/all_to_all | solution.py:549
  9.4 3.6 %prep.1 = (bf16[128,1024]{1,0:T(8,128)(2,1)S(1)}, bf16[1024,256]{1,0:T(8,128)(2,1)S(1)}, bf16[4,256,256]{2,1,0:T(8,128)(2,1)}, f32[4,256]{1,0:T(4,128)}, bf16[25...) custom-call(bf16[256,768]{1,0:T(8,128)(2,1)} %wqkv_h.1, ...), custom_call_target="tpu_custom_call" | custom-call | flops 536870912 | bytes 8388608 | tf_op jit(solution)/shard_map/prep/pallas_call | solution.py:144
  13.0 2.7 %all-to-all-done.wanted = s32[16,1,8]{2,1,0:T(1,128)S(1)} async-done(((s32[16,1,8]{2,1,0:T(1,128)}), s32[16,1,8]{2,1,0:T(1,128)S(1)}, u32[]{:S(2)}, u32[]{:S(2)}) %all-to-all-start) | async-done | bytes 544 | tf_op jit(solution)/shard_map/all_to_all | solution.py:549
  15.7 0.7 %serve.1 = bf16[128,256]{1,0:T(8,128)(2,1)S(1)} custom-call(s32[16,1,8]{2,1,0:T(1,128)S(1)} %all-to-all-done.wanted, bf16[4096,256]{1,0:T(8,128)(2,1)S(1)} %get-tuple-element.28.store), custom_call_target="tpu_custom_call" | custom-call | tf_op jit(solution)/shard_map/serve/pallas_call | solution.py:556
  16.4 10.0 %all_to_all.10 = bf16[16,8,256]{2,1,0:T(8,128)(2,1)S(1)} all-to-all(bf16[16,8,256]{2,1,0:T(8,128)(2,1)S(1)} %bitcast.16), channel_id=1, replica_groups=mesh['parts'=2,'store'=16] {'store'}, dimensions={0} | all-to-all | bytes 131072 | tf_op jit(solution)/shard_map/all_to_all | solution.py:566
  26.4 14.2 %graph_step.1 = (f32[4,64]{1,0:T(4,128)}, bf16[8,296,128]{2,1,0:T(8,128)(2,1)S(1)}, bf16[8,296,128]{2,1,0:T(8,128)(2,1)S(1)}) custom-call(bf16[128,256]{1,0:T(8,128)(2,1)S(1)} %bitcast.17, bf16[128,1024]{1,0:T(8,128)(2,1)S(1)} %get-tuple-element.29.refs_1_, bf16[1024,256]{1,0:T(8,128)(2,1)S(1)} %get-tuple-element.30.refs_2_, ...), custom_call_target="tpu_custom_call" | custom-call | tf_op jit(solution)/shard_map/graph_step/pallas_call | solution.py:499
  40.6 0.1 collective-permute-start
  40.7 2.0 %collective-permute-done.b_ref = bf16[8,296,128]{2,1,0:T(8,128)(2,1)S(1)} collective-permute-done((bf16[8,296,128]{2,1,0:T(8,128)(2,1)S(1)}, bf16[8,296,128]{2,1,0:T(8,128)(2,1)S(1)}, u32[]{:S(2)}, u32[]{:S(2)}) %collective-permute-start) | collective-permute-done | bytes 606240 | tf_op jit(solution)/shard_map/ppermute | solution.py:572
  42.7 0.1 pair_sum.1
  42.9 0.2 collective-permute-start.1
  43.1 0.7 %collective-permute-start.4 = (bf16[2,1,2,152,128]{4,3,2,1,0:T(8,128)(2,1)S(1)}, bf16[2,1,2,152,128]{4,3,2,1,0:T(8,128)(2,1)S(1)}, u32[]{:S(2)}, u32[]{:S(2)}) collective-permute-start(bf16[2,1,2,152,128]{4,3,2,1,0:T(8,128)(2,1)S(1)} %dynamic-slice_convert_fusion), channel_id=1, source_target_pairs={{0,4},{1,5},{2,6},{3,7},{4,0},{5,1},{6,2},{7,3},{8,12},{9,13},{10,... | collective-permute-start | bytes 466952 | tf_op jit(solution)/shard_map/ppermute | solution.py:455
  43.8 5.0 %collective-permute-done.1 = bf16[2,2,1,144,128]{4,3,2,1,0:T(8,128)(2,1)S(1)} collective-permute-done((bf16[2,2,1,144,128]{4,3,2,1,0:T(8,128)(2,1)S(1)}, bf16[2,2,1,144,128]{4,3,2,1,0:T(8,128)(2,1)S(1)}, u32[]{:S(2)}, u32[]{:S(2)}) %collective-permute-start.1) | collective-permute-done | bytes 147488 | tf_op jit(solution)/shard_map/ppermute | solution.py:455
  48.9 0.2 collective-permute-start.2
  49.1 0.1 collective-permute-done.4
  49.2 1.8 %collective-permute-start.5 = (bf16[2,1,1,152,128]{4,3,2,1,0:T(8,128)(2,1)S(1)}, bf16[2,1,1,152,128]{4,3,2,1,0:T(8,128)(2,1)S(1)}, u32[]{:S(2)}, u32[]{:S(2)}) collective-permute-start(bf16[2,1,1,152,128]{4,3,2,1,0:T(8,128)(2,1)S(1)} %dynamic-slice_convert_fusion.2), channel_id=1, source_target_pairs={{0,2},{1,3},{2,0},{3,1},{4,6},{5,7},{6,4},{7,5},{8,10},{9,11},{10,... | collective-permute-start | bytes 233480 | tf_op jit(solution)/shard_map/ppermute | solution.py:455
  51.0 2.3 %collective-permute-done.2 = bf16[2,1,1,144,128]{4,3,2,1,0:T(8,128)(2,1)S(1)} collective-permute-done((bf16[2,1,1,144,128]{4,3,2,1,0:T(8,128)(2,1)S(1)}, bf16[2,1,1,144,128]{4,3,2,1,0:T(8,128)(2,1)S(1)}, u32[]{:S(2)}, u32[]{:S(2)}) %collective-permute-start.2) | collective-permute-done | bytes 73760 | tf_op jit(solution)/shard_map/ppermute | solution.py:455
  53.4 0.3 collective-permute-start.3
  53.6 0.0 collective-permute-done.5
  53.7 2.8 %collective-permute-start.6 = (bf16[1,1,1,152,128]{4,3,2,1,0:T(8,128)(2,1)S(1)}, bf16[1,1,1,152,128]{4,3,2,1,0:T(8,128)(2,1)S(1)}, u32[]{:S(2)}, u32[]{:S(2)}) collective-permute-start(bf16[1,1,1,152,128]{4,3,2,1,0:T(8,128)(2,1)S(1)} %dynamic-slice_convert_fusion.4), channel_id=1, source_target_pairs={{0,8},{1,9},{2,10},{3,11},{4,12},{5,13},{6,14},{7,15},{8,0},{9,1},... | collective-permute-start | bytes 116744 | tf_op jit(solution)/shard_map/ppermute | solution.py:455
  56.5 1.8 %collective-permute-done.3 = bf16[1,1,1,144,128]{4,3,2,1,0:T(8,128)(2,1)S(1)} collective-permute-done((bf16[1,1,1,144,128]{4,3,2,1,0:T(8,128)(2,1)S(1)}, bf16[1,1,1,144,128]{4,3,2,1,0:T(8,128)(2,1)S(1)}, u32[]{:S(2)}, u32[]{:S(2)}) %collective-permute-start.3) | collective-permute-done | bytes 36896 | tf_op jit(solution)/shard_map/ppermute | solution.py:455
  58.3 0.4 collective-permute-done.6
  58.7 0.7 %final_sum.1 = (f32[1]{0:T(128)}, f32[16,768]{1,0:T(8,128)}, f32[16,256]{1,0:T(8,128)}, f32[16,256]{1,0:T(8,128)}, f32[16,512]{1,0:T(8,128)}, /*index=5*/f32[32,256]{1,0:T(8,128)}) custom-call(f32[144,128]{1,0:T(8,128)S(1)} %add_bitcast_fusion.1.refs_0_, f32[152,128]{1,0:T(8,128)S(1)} %add_bitcast_fusion.refs_1_), custom_call_target="tpu_custom_call" | custom-call | tf_op jit(solution)/shard_map/final_sum/pallas_call | solution.py:586
  (12 shorter events, 0.2 us)
Async XLA Ops:
  2.0 13.7 %all-to-all-start = ((s32[16,1,8]{2,1,0:T(1,128)}), s32[16,1,8]{2,1,0:T(1,128)S(1)}, u32[]{:S(2)}, u32[]{:S(2)}) async-start(s32[16,1,8]{2,1,0:T(1,128)} %copy.19), calls=%async_computation | async-start | bytes 16384 | tf_op jit(solution)/shard_map/all_to_all | solution.py:549
  40.6 2.1 %collective-permute-start = (bf16[8,296,128]{2,1,0:T(8,128)(2,1)S(1)}, bf16[8,296,128]{2,1,0:T(8,128)(2,1)S(1)}, u32[]{:S(2)}, u32[]{:S(2)}) collective-permute-start(bf16[8,296,128]{2,1,0:T(8,128)(2,1)S(1)} %get-tuple-element.40), channel_id=1, source_target_pairs={{0,1},{1,0},{2,3},{3,2},{4,5},{5,4},{6,7},{7,6},{8,9},{9,8},{10,11... | collective-permute-start | bytes 1818632 | tf_op jit(solution)/shard_map/ppermute | solution.py:572
  42.9 6.0 %collective-permute-start.1 = (bf16[2,2,1,144,128]{4,3,2,1,0:T(8,128)(2,1)S(1)}, bf16[2,2,1,144,128]{4,3,2,1,0:T(8,128)(2,1)S(1)}, u32[]{:S(2)}, u32[]{:S(2)}) collective-permute-start(bf16[2,2,1,144,128]{4,3,2,1,0:T(8,128)(2,1)S(1)} %dynamic-slice_convert_fusion.1), channel_id=1, source_target_pairs={{0,2},{1,3},{2,0},{3,1},{4,6},{5,7},{6,4},{7,5},{8,10},{9,11},{10,... | collective-permute-start | bytes 442376 | tf_op jit(solution)/shard_map/ppermute | solution.py:455
  43.1 6.1 %collective-permute-start.4 = (bf16[2,1,2,152,128]{4,3,2,1,0:T(8,128)(2,1)S(1)}, bf16[2,1,2,152,128]{4,3,2,1,0:T(8,128)(2,1)S(1)}, u32[]{:S(2)}, u32[]{:S(2)}) collective-permute-start(bf16[2,1,2,152,128]{4,3,2,1,0:T(8,128)(2,1)S(1)} %dynamic-slice_convert_fusion), channel_id=1, source_target_pairs={{0,4},{1,5},{2,6},{3,7},{4,0},{5,1},{6,2},{7,3},{8,12},{9,13},{10,... | collective-permute-start | bytes 466952 | tf_op jit(solution)/shard_map/ppermute | solution.py:455
  48.9 4.4 %collective-permute-start.2 = (bf16[2,1,1,144,128]{4,3,2,1,0:T(8,128)(2,1)S(1)}, bf16[2,1,1,144,128]{4,3,2,1,0:T(8,128)(2,1)S(1)}, u32[]{:S(2)}, u32[]{:S(2)}) collective-permute-start(bf16[2,1,1,144,128]{4,3,2,1,0:T(8,128)(2,1)S(1)} %dynamic-slice_convert_fusion.3), channel_id=1, source_target_pairs={{0,4},{1,5},{2,6},{3,7},{4,0},{5,1},{6,2},{7,3},{8,12},{9,13},{10,... | collective-permute-start | bytes 221192 | tf_op jit(solution)/shard_map/ppermute | solution.py:455
  49.2 4.5 %collective-permute-start.5 = (bf16[2,1,1,152,128]{4,3,2,1,0:T(8,128)(2,1)S(1)}, bf16[2,1,1,152,128]{4,3,2,1,0:T(8,128)(2,1)S(1)}, u32[]{:S(2)}, u32[]{:S(2)}) collective-permute-start(bf16[2,1,1,152,128]{4,3,2,1,0:T(8,128)(2,1)S(1)} %dynamic-slice_convert_fusion.2), channel_id=1, source_target_pairs={{0,2},{1,3},{2,0},{3,1},{4,6},{5,7},{6,4},{7,5},{8,10},{9,11},{10,... | collective-permute-start | bytes 233480 | tf_op jit(solution)/shard_map/ppermute | solution.py:455
  53.4 4.9 %collective-permute-start.3 = (bf16[1,1,1,144,128]{4,3,2,1,0:T(8,128)(2,1)S(1)}, bf16[1,1,1,144,128]{4,3,2,1,0:T(8,128)(2,1)S(1)}, u32[]{:S(2)}, u32[]{:S(2)}) collective-permute-start(bf16[1,1,1,144,128]{4,3,2,1,0:T(8,128)(2,1)S(1)} %dynamic-slice_convert_fusion.5), channel_id=1, source_target_pairs={{0,8},{1,9},{2,10},{3,11},{4,12},{5,13},{6,14},{7,15},{8,0},{9,1},... | collective-permute-start | bytes 110600 | tf_op jit(solution)/shard_map/ppermute | solution.py:455
  53.7 5.0 %collective-permute-start.6 = (bf16[1,1,1,152,128]{4,3,2,1,0:T(8,128)(2,1)S(1)}, bf16[1,1,1,152,128]{4,3,2,1,0:T(8,128)(2,1)S(1)}, u32[]{:S(2)}, u32[]{:S(2)}) collective-permute-start(bf16[1,1,1,152,128]{4,3,2,1,0:T(8,128)(2,1)S(1)} %dynamic-slice_convert_fusion.4), channel_id=1, source_target_pairs={{0,8},{1,9},{2,10},{3,11},{4,12},{5,13},{6,14},{7,15},{8,0},{9,1},... | collective-permute-start | bytes 116744 | tf_op jit(solution)/shard_map/ppermute | solution.py:455

commit v7 on v6

--- a/solution.py
+++ b/solution.py
@@ -210,7 +210,7 @@
     fetched_ref, pick, wqmT = refs[:3]
     sources = refs[3:14]
     preds_ref = refs[14]
-    outs = refs[15 : 15 + (2 if packed else 6)]
+    outs = refs[15 : 15 + (4 if packed else 6)]
     refs = refs[15 + len(outs) :]
     adjT, deg, woT, wupT, wdownT, hot_ref, wcol, targets_ref, wo, wup, wdown = refs[:11]
     (
@@ -386,13 +386,12 @@
     gq_s[:, 0 : 4 * feats] = _nt(x_s[...], dy_s[...]).astype(BF)
     obj = jnp.sum(obj_s[0:1, :], axis=1, keepdims=True) / n_all
     if packed:
-        keep_ref, send_ref = outs
-        slabs = keep_ref.shape[0]
+        slabs, cut, _ = outs[0].shape
         rows = feats // (2 * slabs)
         core = lax.axis_index("store") % 2
         obj_block = _spread(obj, TAIL)
         per = hidden // feats
-        for ref, side in ((keep_ref, core), (send_ref, 1 - core)):
+        for first, second, side in ((outs[0], outs[1], core), (outs[2], outs[3], 1 - core)):
             for j in range(slabs):
                 d = 2 * j + side
                 r = pl.ds(pl.multiple_of(d * rows, rows), rows)
@@ -401,9 +400,12 @@
                 for i in range(per):
                     r = pl.ds(pl.multiple_of(d * (rows * per) + i * rows, rows), rows)
                     pieces += [gd_s[r, c : c + LANES] for c in range(0, feats, LANES)]
-                for i, piece in enumerate(pieces):
-                    ref[j, i * rows : (i + 1) * rows, :] = piece
-                ref[j, len(pieces) * rows :, :] = obj_block
+                whole = cut // rows
+                for i, piece in enumerate(pieces[:whole]):
+                    first[j, i * rows : (i + 1) * rows, :] = piece
+                for i, piece in enumerate(pieces[whole:]):
+                    second[j, i * rows : (i + 1) * rows, :] = piece
+                second[j, (len(pieces) - whole) * rows :, :] = obj_block
     else:
         obj_ref, gqkv_ref, go_ref, gmsg_ref, gup_ref, gdown_ref = outs
         obj_ref[...] = jnp.broadcast_to(obj, obj_ref.shape)
@@ -432,10 +434,8 @@
 TAIL = 8
 
 
-def _pair_kernel(a_ref, b_ref, first_ref, second_ref):
-    cut = first_ref.shape[1]
-    first_ref[...] = a_ref[:, :cut, :].astype(F32) + b_ref[:, :cut, :].astype(F32)
-    second_ref[...] = a_ref[:, cut:, :].astype(F32) + b_ref[:, cut:, :].astype(F32)
+def _pair_kernel(a_ref, b_ref, o_ref):
+    o_ref[...] = a_ref[...].astype(F32) + b_ref[...].astype(F32)
 
 
 def _halving(halves, groups):
@@ -489,8 +489,10 @@
     packed = packed and feats % LANES == 0 and groups & (groups - 1) == 0
     out = [((subs, n_pairs), F32)]
     if packed:
-        slab = (groups // 2, rows * (5 * feats + 2 * hidden) // LANES + TAIL, LANES)
-        out += [(slab, BF), (slab, BF)]
+        height = rows * (5 * feats + 2 * hidden) // LANES
+        cut = height // (2 * rows) * rows
+        sizes = (cut, height - cut + TAIL)
+        out += [((groups // 2, h, LANES), BF) for h in sizes + sizes]
     else:
         out += [
             ((8, LANES), F32), ((feats, 3 * feats), BF), ((feats, feats), BF), ((feats, feats), BF),
@@ -567,22 +569,21 @@
     fetched = fetched.reshape(-1, feats)
     packed, (preds, *terms) = local_step(prep, fetched, targets, (w_o, w_up, w_down), groups)
     if packed:
-        keep, send = terms
         rows = feats // groups
-        got = lax.ppermute(send, "store", [(i, i ^ 1) for i in range(groups)])
-        height = keep.shape[1]
-        cut = height // 2 // 16 * 16
-        paired = pl.pallas_call(
-            _pair_kernel,
-            in_specs=_vmem(2),
-            out_specs=_vmem(2),
-            out_shape=[
-                jax.ShapeDtypeStruct((keep.shape[0], h, LANES), F32) for h in (cut, height - cut)
-            ],
-            compiler_params=pltpu.CompilerParams(vmem_limit_bytes=8 << 20),
-            name="pair_sum",
-        )(keep, got)
-        shared = _halving(list(paired), groups)
+        paired = []
+        for keep, send in zip(terms[:2], terms[2:]):
+            got = lax.ppermute(send, "store", [(i, i ^ 1) for i in range(groups)])
+            paired.append(
+                pl.pallas_call(
+                    _pair_kernel,
+                    in_specs=_vmem(2),
+                    out_specs=pl.BlockSpec(memory_space=pltpu.VMEM),
+                    out_shape=jax.ShapeDtypeStruct(keep.shape, F32),
+                    compiler_params=pltpu.CompilerParams(vmem_limit_bytes=8 << 20),
+                    name="pair_sum",
+                )(keep, got)
+            )
+        shared = _halving(paired, groups)
         loss, *shares = pl.pallas_call(
             lambda *refs: _final_kernel(groups, *refs),
             in_specs=_vmem(2),

time: 59.7 us -> 59.5 us (level)
    ppermute x1 -> x2, waiting for transfers between devices: 2.01 us -> 1.22 us  [shards(): got = lax.ppermute(send, 'store', [(i, i ^ 1) for i in range(groups)])]
    ppermute x6, waiting for transfers between devices: 9.69 us -> 10.4 us  [_halving(): got.append(lax.ppermute(send, 'store', perm))]
    ppermute x6, starting transfers between devices: 5.87 us -> 5.25 us  [_halving(): got.append(lax.ppermute(send, 'store', perm))]
  transfers between devices with their start and end apart: 8 -> 9, of which waited for: 7 -> 9; matrix products, arithmetic and copies ran while one was open for 0% -> 0% of each run, Pallas kernels for 6% -> 6%
where the time goes in v7:
time: 59.5 us; the launch traced here: 59.2 us
  Pallas kernels  19.3 us (32%)
  waiting for transfers between devices  14.3 us (24%)
  starting transfers between devices  13.2 us (22%)
  blocking collectives  9.98 us (17%)
  local copies, waits for them, and re-layouts  1.49 us (3%)
  between operations  0.76 us (1%)
    pallas_call x1, Pallas kernels, local_step(): pl.pallas_call(lambda *refs: _step_kernel(packed, *refs), in_specs=_vmem(...  14.2 us
    ppermute x6, waiting for transfers between devices, _halving(): got.append(lax.ppermute(send, 'store', perm))  10.4 us
    all_to_all x1, blocking collectives, shards(): lax.all_to_all(picked, 'store', split_axis=0, concat_axis=0, tiled=True)  9.98 us
    all_to_all x1, starting transfers between devices, shards(): lax.all_to_all(requests.reshape(groups, 1, -1), 'store', split_axis=0, co...  7.39 us
    ppermute x6, starting transfers between devices, _halving(): got.append(lax.ppermute(send, 'store', perm))  5.25 us
    pallas_call x1, Pallas kernels, _prep(): pl.pallas_call(_prep_kernel, in_specs=[pl.BlockSpec(memory_space=pltpu.HB...  3.59 us
    all_to_all x1, waiting for transfers between devices, shards(): lax.all_to_all(requests.reshape(groups, 1, -1), 'store', split_axis=0, co...  2.73 us
    reshape x1, local copies, waits for them, and re-layouts, shards(): requests.reshape(groups, 1, -1)  1.36 us
  transfers between devices with their start and end apart: 9, of which 9 were waited for; matrix products, arithmetic and copies ran while one was open for 0% of the time, Pallas kernels for 6%

profile of v7, /device:TPU:0, one launch (start us, length us, event | category | flops | bytes accessed | tf_op | source)
XLA Modules:
  0.0 59.2 jit_solution(5650627025087132620)
XLA Ops:
  0.6 1.4 %copy.19 = s32[16,1,8]{2,1,0:T(1,128)} copy(s32[16,1,8]{0,2,1:T(8,128)} %bitcast.20) | data formatting | bytes 1024 | tf_op jit(solution)/shard_map/reshape | solution.py:552
  2.0 7.4 %all-to-all-start = ((s32[16,1,8]{2,1,0:T(1,128)}), s32[16,1,8]{2,1,0:T(1,128)S(1)}, u32[]{:S(2)}, u32[]{:S(2)}) async-start(s32[16,1,8]{2,1,0:T(1,128)} %copy.19), calls=%async_computation | async-start | bytes 16384 | tf_op jit(solution)/shard_map/all_to_all | solution.py:551
  9.4 3.6 %prep.1 = (bf16[128,1024]{1,0:T(8,128)(2,1)S(1)}, bf16[1024,256]{1,0:T(8,128)(2,1)S(1)}, bf16[4,256,256]{2,1,0:T(8,128)(2,1)}, f32[4,256]{1,0:T(4,128)}, bf16[25...) custom-call(bf16[256,768]{1,0:T(8,128)(2,1)} %wqkv_h.1, ...), custom_call_target="tpu_custom_call" | custom-call | flops 536870912 | bytes 8388608 | tf_op jit(solution)/shard_map/prep/pallas_call | solution.py:144
  13.0 2.7 %all-to-all-done.wanted = s32[16,1,8]{2,1,0:T(1,128)S(1)} async-done(((s32[16,1,8]{2,1,0:T(1,128)}), s32[16,1,8]{2,1,0:T(1,128)S(1)}, u32[]{:S(2)}, u32[]{:S(2)}) %all-to-all-start) | async-done | bytes 544 | tf_op jit(solution)/shard_map/all_to_all | solution.py:551
  15.7 0.7 %serve.1 = bf16[128,256]{1,0:T(8,128)(2,1)S(1)} custom-call(s32[16,1,8]{2,1,0:T(1,128)S(1)} %all-to-all-done.wanted, bf16[4096,256]{1,0:T(8,128)(2,1)S(1)} %get-tuple-element.28.store), custom_call_target="tpu_custom_call" | custom-call | tf_op jit(solution)/shard_map/serve/pallas_call | solution.py:558
  16.4 10.0 %all_to_all.10 = bf16[16,8,256]{2,1,0:T(8,128)(2,1)S(1)} all-to-all(bf16[16,8,256]{2,1,0:T(8,128)(2,1)S(1)} %bitcast.16), channel_id=1, replica_groups=mesh['parts'=2,'store'=16] {'store'}, dimensions={0} | all-to-all | bytes 131072 | tf_op jit(solution)/shard_map/all_to_all | solution.py:568
  26.4 14.2 %graph_step.1 = (f32[4,64]{1,0:T(4,128)}, bf16[8,144,128]{2,1,0:T(8,128)(2,1)S(1)}, bf16[8,152,128]{2,1,0:T(8,128)(2,1)S(1)}, bf16[8,144,128]{2,1,0:T(8,128)(2,1)S(1)}, bf16[8,152,128]{2,1,0:T(8,128)(2,1)S(1)}) custom-call(bf16[128,256]{1,0:T(8,128)(2,1)S(1)} %bitcast.17, bf16[128,1024]{1,0:T(8,128)(2,1)S(1)} %get-tuple-element.29.refs_1_, ...), custom_call_target="tpu_custom_call" | custom-call | tf_op jit(solution)/shard_map/graph_step/pallas_call | solution.py:501
  40.6 0.1 collective-permute-start
  40.7 0.5 collective-permute-start.4
  41.2 1.1 %collective-permute-done.b_ref = bf16[8,144,128]{2,1,0:T(8,128)(2,1)S(1)} collective-permute-done((bf16[8,144,128]{2,1,0:T(8,128)(2,1)S(1)}, bf16[8,144,128]{2,1,0:T(8,128)(2,1)S(1)}, u32[]{:S(2)}, u32[]{:S(2)}) %collective-permute-start) | collective-permute-done | bytes 294944 | tf_op jit(solution)/shard_map/ppermute | solution.py:575
  42.3 0.1 pair_sum.2
  42.4 0.2 collective-permute-start.1
  42.6 0.1 collective-permute-done.4.b_ref
  42.7 0.1 pair_sum.3
  42.8 0.6 collective-permute-start.5
  43.4 4.9 %collective-permute-done.1 = bf16[2,2,1,144,128]{4,3,2,1,0:T(8,128)(2,1)S(1)} collective-permute-done((bf16[2,2,1,144,128]{4,3,2,1,0:T(8,128)(2,1)S(1)}, bf16[2,2,1,144,128]{4,3,2,1,0:T(8,128)(2,1)S(1)}, u32[]{:S(2)}, u32[]{:S(2)}) %collective-permute-start.1) | collective-permute-done | bytes 147488 | tf_op jit(solution)/shard_map/ppermute | solution.py:455
  48.4 0.2 collective-permute-start.2
  48.6 0.4 collective-permute-done.5
  49.0 1.5 %collective-permute-start.6 = (bf16[2,1,1,152,128]{4,3,2,1,0:T(8,128)(2,1)S(1)}, bf16[2,1,1,152,128]{4,3,2,1,0:T(8,128)(2,1)S(1)}, u32[]{:S(2)}, u32[]{:S(2)}) collective-permute-start(bf16[2,1,1,152,128]{4,3,2,1,0:T(8,128)(2,1)S(1)} %dynamic-slice_convert_fusion.2), channel_id=1, source_target_pairs={{0,2},{1,3},{2,0},{3,1},{4,6},{5,7},{6,4},{7,5},{8,10},{9,11},{10,... | collective-permute-start | bytes 233480 | tf_op jit(solution)/shard_map/ppermute | solution.py:455
  50.6 2.3 %collective-permute-done.2 = bf16[2,1,1,144,128]{4,3,2,1,0:T(8,128)(2,1)S(1)} collective-permute-done((bf16[2,1,1,144,128]{4,3,2,1,0:T(8,128)(2,1)S(1)}, bf16[2,1,1,144,128]{4,3,2,1,0:T(8,128)(2,1)S(1)}, u32[]{:S(2)}, u32[]{:S(2)}) %collective-permute-start.2) | collective-permute-done | bytes 73760 | tf_op jit(solution)/shard_map/ppermute | solution.py:455
  52.9 0.3 collective-permute-start.3
  53.1 0.3 collective-permute-done.6
  53.5 2.4 %collective-permute-start.7 = (bf16[1,1,1,152,128]{4,3,2,1,0:T(8,128)(2,1)S(1)}, bf16[1,1,1,152,128]{4,3,2,1,0:T(8,128)(2,1)S(1)}, u32[]{:S(2)}, u32[]{:S(2)}) collective-permute-start(bf16[1,1,1,152,128]{4,3,2,1,0:T(8,128)(2,1)S(1)} %dynamic-slice_convert_fusion.4), channel_id=1, source_target_pairs={{0,8},{1,9},{2,10},{3,11},{4,12},{5,13},{6,14},{7,15},{8,0},{9,1},... | collective-permute-start | bytes 116744 | tf_op jit(solution)/shard_map/ppermute | solution.py:455
  56.0 1.8 %collective-permute-done.3 = bf16[1,1,1,144,128]{4,3,2,1,0:T(8,128)(2,1)S(1)} collective-permute-done((bf16[1,1,1,144,128]{4,3,2,1,0:T(8,128)(2,1)S(1)}, bf16[1,1,1,144,128]{4,3,2,1,0:T(8,128)(2,1)S(1)}, u32[]{:S(2)}, u32[]{:S(2)}) %collective-permute-start.3) | collective-permute-done | bytes 36896 | tf_op jit(solution)/shard_map/ppermute | solution.py:455
  57.8 0.7 %collective-permute-done.7 = bf16[1,1,1,152,128]{4,3,2,1,0:T(8,128)(2,1)S(1)} collective-permute-done((bf16[1,1,1,152,128]{4,3,2,1,0:T(8,128)(2,1)S(1)}, bf16[1,1,1,152,128]{4,3,2,1,0:T(8,128)(2,1)S(1)}, u32[]{:S(2)}, u32[]{:S(2)}) %collective-permute-start.7) | collective-permute-done | bytes 38944 | tf_op jit(solution)/shard_map/ppermute | solution.py:455
  58.5 0.7 %final_sum.1 = (f32[1]{0:T(128)}, f32[16,768]{1,0:T(8,128)}, f32[16,256]{1,0:T(8,128)}, f32[16,256]{1,0:T(8,128)}, f32[16,512]{1,0:T(8,128)}, /*index=5*/f32[32,256]{1,0:T(8,128)}) custom-call(f32[144,128]{1,0:T(8,128)S(1)} %add_bitcast_fusion.1.refs_0_, f32[152,128]{1,0:T(8,128)S(1)} %add_bitcast_fusion.refs_1_), custom_call_target="tpu_custom_call" | custom-call | tf_op jit(solution)/shard_map/final_sum/pallas_call | solution.py:587
  (12 shorter events, 0.2 us)
Async XLA Ops:
  2.0 13.7 %all-to-all-start = ((s32[16,1,8]{2,1,0:T(1,128)}), s32[16,1,8]{2,1,0:T(1,128)S(1)}, u32[]{:S(2)}, u32[]{:S(2)}) async-start(s32[16,1,8]{2,1,0:T(1,128)} %copy.19), calls=%async_computation | async-start | bytes 16384 | tf_op jit(solution)/shard_map/all_to_all | solution.py:551
  40.6 1.6 %collective-permute-start = (bf16[8,144,128]{2,1,0:T(8,128)(2,1)S(1)}, bf16[8,144,128]{2,1,0:T(8,128)(2,1)S(1)}, u32[]{:S(2)}, u32[]{:S(2)}) collective-permute-start(bf16[8,144,128]{2,1,0:T(8,128)(2,1)S(1)} %get-tuple-element.40), channel_id=1, source_target_pairs={{0,1},{1,0},{2,3},{3,2},{4,5},{5,4},{6,7},{7,6},{8,9},{9,8},{10,11... | collective-permute-start | bytes 884744 | tf_op jit(solution)/shard_map/ppermute | solution.py:575
  40.7 2.0 %collective-permute-start.4 = (bf16[8,152,128]{2,1,0:T(8,128)(2,1)S(1)}, bf16[8,152,128]{2,1,0:T(8,128)(2,1)S(1)}, u32[]{:S(2)}, u32[]{:S(2)}) collective-permute-start(bf16[8,152,128]{2,1,0:T(8,128)(2,1)S(1)} %get-tuple-element.42), channel_id=1, source_target_pairs={{0,1},{1,0},{2,3},{3,2},{4,5},{5,4},{6,7},{7,6},{8,9},{9,8},{10,11... | collective-permute-start | bytes 933896 | tf_op jit(solution)/shard_map/ppermute | solution.py:575
  42.4 6.0 %collective-permute-start.1 = (bf16[2,2,1,144,128]{4,3,2,1,0:T(8,128)(2,1)S(1)}, bf16[2,2,1,144,128]{4,3,2,1,0:T(8,128)(2,1)S(1)}, u32[]{:S(2)}, u32[]{:S(2)}) collective-permute-start(bf16[2,2,1,144,128]{4,3,2,1,0:T(8,128)(2,1)S(1)} %dynamic-slice_convert_fusion.1), channel_id=1, source_target_pairs={{0,2},{1,3},{2,0},{3,1},{4,6},{5,7},{6,4},{7,5},{8,10},{9,11},{10,... | collective-permute-start | bytes 442376 | tf_op jit(solution)/shard_map/ppermute | solution.py:455
  42.8 6.1 %collective-permute-start.5 = (bf16[2,1,2,152,128]{4,3,2,1,0:T(8,128)(2,1)S(1)}, bf16[2,1,2,152,128]{4,3,2,1,0:T(8,128)(2,1)S(1)}, u32[]{:S(2)}, u32[]{:S(2)}) collective-permute-start(bf16[2,1,2,152,128]{4,3,2,1,0:T(8,128)(2,1)S(1)} %dynamic-slice_convert_fusion), channel_id=1, source_target_pairs={{0,4},{1,5},{2,6},{3,7},{4,0},{5,1},{6,2},{7,3},{8,12},{9,13},{10,... | collective-permute-start | bytes 466952 | tf_op jit(solution)/shard_map/ppermute | solution.py:455
  48.4 4.4 %collective-permute-start.2 = (bf16[2,1,1,144,128]{4,3,2,1,0:T(8,128)(2,1)S(1)}, bf16[2,1,1,144,128]{4,3,2,1,0:T(8,128)(2,1)S(1)}, u32[]{:S(2)}, u32[]{:S(2)}) collective-permute-start(bf16[2,1,1,144,128]{4,3,2,1,0:T(8,128)(2,1)S(1)} %dynamic-slice_convert_fusion.3), channel_id=1, source_target_pairs={{0,4},{1,5},{2,6},{3,7},{4,0},{5,1},{6,2},{7,3},{8,12},{9,13},{10,... | collective-permute-start | bytes 221192 | tf_op jit(solution)/shard_map/ppermute | solution.py:455
  49.0 4.5 %collective-permute-start.6 = (bf16[2,1,1,152,128]{4,3,2,1,0:T(8,128)(2,1)S(1)}, bf16[2,1,1,152,128]{4,3,2,1,0:T(8,128)(2,1)S(1)}, u32[]{:S(2)}, u32[]{:S(2)}) collective-permute-start(bf16[2,1,1,152,128]{4,3,2,1,0:T(8,128)(2,1)S(1)} %dynamic-slice_convert_fusion.2), channel_id=1, source_target_pairs={{0,2},{1,3},{2,0},{3,1},{4,6},{5,7},{6,4},{7,5},{8,10},{9,11},{10,... | collective-permute-start | bytes 233480 | tf_op jit(solution)/shard_map/ppermute | solution.py:455
  52.9 4.9 %collective-permute-start.3 = (bf16[1,1,1,144,128]{4,3,2,1,0:T(8,128)(2,1)S(1)}, bf16[1,1,1,144,128]{4,3,2,1,0:T(8,128)(2,1)S(1)}, u32[]{:S(2)}, u32[]{:S(2)}) collective-permute-start(bf16[1,1,1,144,128]{4,3,2,1,0:T(8,128)(2,1)S(1)} %dynamic-slice_convert_fusion.5), channel_id=1, source_target_pairs={{0,8},{1,9},{2,10},{3,11},{4,12},{5,13},{6,14},{7,15},{8,0},{9,1},... | collective-permute-start | bytes 110600 | tf_op jit(solution)/shard_map/ppermute | solution.py:455
  53.5 4.9 %collective-permute-start.7 = (bf16[1,1,1,152,128]{4,3,2,1,0:T(8,128)(2,1)S(1)}, bf16[1,1,1,152,128]{4,3,2,1,0:T(8,128)(2,1)S(1)}, u32[]{:S(2)}, u32[]{:S(2)}) collective-permute-start(bf16[1,1,1,152,128]{4,3,2,1,0:T(8,128)(2,1)S(1)} %dynamic-slice_convert_fusion.4), channel_id=1, source_target_pairs={{0,8},{1,9},{2,10},{3,11},{4,12},{5,13},{6,14},{7,15},{8,0},{9,1},... | collective-permute-start | bytes 116744 | tf_op jit(solution)/shard_map/ppermute | solution.py:455

commit v8 on v7

--- a/solution.py
+++ b/solution.py
@@ -434,28 +434,24 @@
 TAIL = 8
 
 
-def _pair_kernel(a_ref, b_ref, o_ref):
-    o_ref[...] = a_ref[...].astype(F32) + b_ref[...].astype(F32)
-
-
 def _halving(halves, groups):
     idx = lax.axis_index("store")
     bits = groups.bit_length() - 2
     orders = [list(range(1, bits + 1)) for _ in halves]
     if bits > 1:
         orders[1][:2] = [2, 1]
-    halves = [h.reshape((2,) * bits + h.shape[1:]) for h in halves]
+    halves = [[v.reshape((2,) * bits + v.shape[1:]) for v in h] for h in halves]
     for step in range(bits):
         kept, got = [], []
         for h, order in zip(halves, orders):
             axis = bits - order[step]
             bit = (idx >> order[step]) & 1
             perm = [(i, i ^ (1 << order[step])) for i in range(groups)]
-            send = lax.dynamic_slice_in_dim(h, 1 - bit, 1, axis).astype(BF)
-            got.append(lax.ppermute(send, "store", perm))
-            kept.append(lax.dynamic_slice_in_dim(h, bit, 1, axis))
-        halves = [k + g.astype(F32) for k, g in zip(kept, got)]
-    return [h.reshape(h.shape[-2:]) for h in halves]
+            send = sum(lax.dynamic_slice_in_dim(v, 1 - bit, 1, axis).astype(F32) for v in h)
+            got.append(lax.ppermute(send.astype(BF), "store", perm))
+            kept.append(sum(lax.dynamic_slice_in_dim(v, bit, 1, axis).astype(F32) for v in h))
+        halves = [[k + g.astype(F32)] for k, g in zip(kept, got)]
+    return [sum(v.astype(F32) for v in h).reshape(h[0].shape[-2:]) for h in halves]
 
 
 def _final_kernel(groups, first_ref, second_ref, loss_ref, gqkv, go, gmsg, gup, gdown):
@@ -573,16 +569,7 @@
         paired = []
         for keep, send in zip(terms[:2], terms[2:]):
             got = lax.ppermute(send, "store", [(i, i ^ 1) for i in range(groups)])
-            paired.append(
-                pl.pallas_call(
-                    _pair_kernel,
-                    in_specs=_vmem(2),
-                    out_specs=pl.BlockSpec(memory_space=pltpu.VMEM),
-                    out_shape=jax.ShapeDtypeStruct(keep.shape, F32),
-                    compiler_params=pltpu.CompilerParams(vmem_limit_bytes=8 << 20),
-                    name="pair_sum",
-                )(keep, got)
-            )
+            paired.append((keep, got))
         shared = _halving(paired, groups)
         loss, *shares = pl.pallas_call(
             lambda *refs: _final_kernel(groups, *refs),

time: 59.5 us -> 59.4 us (level)
  transfers between devices with their start and end apart: 9 -> 9, of which waited for: 9 -> 9; matrix products, arithmetic and copies ran while one was open for 0% -> 1% of each run, Pallas kernels for 6% -> 6%
where the time goes in v8:
time: 59.4 us; the launch traced here: 59.2 us
  Pallas kernels  19.2 us (32%)
  waiting for transfers between devices  14.5 us (24%)
  starting transfers between devices  13.1 us (22%)
  blocking collectives  9.98 us (17%)
  local copies, waits for them, and re-layouts  1.43 us (2%)
  between operations  0.74 us (1%)
    pallas_call x1, Pallas kernels, local_step(): pl.pallas_call(lambda *refs: _step_kernel(packed, *refs), in_specs=_vmem(...  14.2 us
    ppermute x6, waiting for transfers between devices, _halving(): got.append(lax.ppermute(send.astype(BF), 'store', perm))  10.5 us
    all_to_all x1, blocking collectives, shards(): lax.all_to_all(picked, 'store', split_axis=0, concat_axis=0, tiled=True)  9.98 us
    all_to_all x1, starting transfers between devices, shards(): lax.all_to_all(requests.reshape(groups, 1, -1), 'store', split_axis=0, co...  7.39 us
    ppermute x6, starting transfers between devices, _halving(): got.append(lax.ppermute(send.astype(BF), 'store', perm))  5.13 us
    pallas_call x1, Pallas kernels, _prep(): pl.pallas_call(_prep_kernel, in_specs=[pl.BlockSpec(memory_space=pltpu.HB...  3.59 us
    all_to_all x1, waiting for transfers between devices, shards(): lax.all_to_all(requests.reshape(groups, 1, -1), 'store', split_axis=0, co...  2.73 us
    reshape x1, local copies, waits for them, and re-layouts, shards(): requests.reshape(groups, 1, -1)  1.36 us
  transfers between devices with their start and end apart: 9, of which 9 were waited for; matrix products, arithmetic and copies ran while one was open for 1% of the time, Pallas kernels for 6%

profile of v8, /device:TPU:0, one launch (start us, length us, event | category | flops | bytes accessed | tf_op | source)
XLA Modules:
  0.0 59.2 jit_solution(16297083016475389154)
XLA Ops:
  0.6 1.4 %copy.19 = s32[16,1,8]{2,1,0:T(1,128)} copy(s32[16,1,8]{0,2,1:T(8,128)} %bitcast.26) | data formatting | bytes 1024 | tf_op jit(solution)/shard_map/reshape | solution.py:548
  2.0 7.4 %all-to-all-start = ((s32[16,1,8]{2,1,0:T(1,128)}), s32[16,1,8]{2,1,0:T(1,128)S(1)}, u32[]{:S(2)}, u32[]{:S(2)}) async-start(s32[16,1,8]{2,1,0:T(1,128)} %copy.19), calls=%async_computation | async-start | bytes 16384 | tf_op jit(solution)/shard_map/all_to_all | solution.py:547
  9.4 3.6 %prep.1 = (bf16[128,1024]{1,0:T(8,128)(2,1)S(1)}, bf16[1024,256]{1,0:T(8,128)(2,1)S(1)}, bf16[4,256,256]{2,1,0:T(8,128)(2,1)}, f32[4,256]{1,0:T(4,128)}, bf16[25...) custom-call(bf16[256,768]{1,0:T(8,128)(2,1)} %wqkv_h.1, ...), custom_call_target="tpu_custom_call" | custom-call | flops 536870912 | bytes 8388608 | tf_op jit(solution)/shard_map/prep/pallas_call | solution.py:144
  13.0 2.7 %all-to-all-done.wanted = s32[16,1,8]{2,1,0:T(1,128)S(1)} async-done(((s32[16,1,8]{2,1,0:T(1,128)}), s32[16,1,8]{2,1,0:T(1,128)S(1)}, u32[]{:S(2)}, u32[]{:S(2)}) %all-to-all-start) | async-done | bytes 544 | tf_op jit(solution)/shard_map/all_to_all | solution.py:547
  15.7 0.7 %serve.1 = bf16[128,256]{1,0:T(8,128)(2,1)S(1)} custom-call(s32[16,1,8]{2,1,0:T(1,128)S(1)} %all-to-all-done.wanted, bf16[4096,256]{1,0:T(8,128)(2,1)S(1)} %get-tuple-element.28.store), custom_call_target="tpu_custom_call" | custom-call | tf_op jit(solution)/shard_map/serve/pallas_call | solution.py:554
  16.4 10.0 %all_to_all.10 = bf16[16,8,256]{2,1,0:T(8,128)(2,1)S(1)} all-to-all(bf16[16,8,256]{2,1,0:T(8,128)(2,1)S(1)} %bitcast.18), channel_id=1, replica_groups=mesh['parts'=2,'store'=16] {'store'}, dimensions={0} | all-to-all | bytes 131072 | tf_op jit(solution)/shard_map/all_to_all | solution.py:564
  26.4 14.2 %graph_step.1 = (f32[4,64]{1,0:T(4,128)}, bf16[8,144,128]{2,1,0:T(8,128)(2,1)S(1)}, bf16[8,152,128]{2,1,0:T(8,128)(2,1)S(1)}, bf16[8,144,128]{2,1,0:T(8,128)(2,1)S(1)}, bf16[8,152,128]{2,1,0:T(8,128)(2,1)S(1)}) custom-call(bf16[128,256]{1,0:T(8,128)(2,1)S(1)} %bitcast.19, bf16[128,1024]{1,0:T(8,128)(2,1)S(1)} %get-tuple-element.29.refs_1_, ...), custom_call_target="tpu_custom_call" | custom-call | tf_op jit(solution)/shard_map/graph_step/pallas_call | solution.py:497
  40.6 0.1 collective-permute-start
  40.7 0.5 collective-permute-start.4
  41.2 1.1 %collective-permute-done = bf16[8,144,128]{2,1,0:T(8,128)(2,1)S(1)} collective-permute-done((bf16[8,144,128]{2,1,0:T(8,128)(2,1)S(1)}, bf16[8,144,128]{2,1,0:T(8,128)(2,1)S(1)}, u32[]{:S(2)}, u32[]{:S(2)}) %collective-permute-start) | collective-permute-done | bytes 294944 | tf_op jit(solution)/shard_map/ppermute | solution.py:571
  42.3 0.2 collective-permute-start.1
  42.5 0.2 collective-permute-done.4
  42.8 0.5 collective-permute-start.5
  43.3 5.0 %collective-permute-done.1 = bf16[2,2,1,144,128]{4,3,2,1,0:T(8,128)(2,1)S(1)} collective-permute-done((bf16[2,2,1,144,128]{4,3,2,1,0:T(8,128)(2,1)S(1)}, bf16[2,2,1,144,128]{4,3,2,1,0:T(8,128)(2,1)S(1)}, u32[]{:S(2)}, u32[]{:S(2)}) %collective-permute-start.1) | collective-permute-done | bytes 147488 | tf_op jit(solution)/shard_map/ppermute | solution.py:451
  48.3 0.1 convert_add_fusion.1
  48.4 0.2 collective-permute-start.2
  48.6 0.3 collective-permute-done.5
  48.9 0.1 convert_add_fusion
  49.0 1.5 %collective-permute-start.6 = (bf16[2,1,1,152,128]{4,3,2,1,0:T(8,128)(2,1)S(1)}, bf16[2,1,1,152,128]{4,3,2,1,0:T(8,128)(2,1)S(1)}, u32[]{:S(2)}, u32[]{:S(2)}) collective-permute-start(bf16[2,1,1,152,128]{4,3,2,1,0:T(8,128)(2,1)S(1)} %dynamic-slice_convert_fusion), channel_id=1, source_target_pairs={{0,2},{1,3},{2,0},{3,1},{4,6},{5,7},{6,4},{7,5},{8,10},{9,11},{10,... | collective-permute-start | bytes 233480 | tf_op jit(solution)/shard_map/ppermute | solution.py:451
  50.5 2.3 %collective-permute-done.2 = bf16[2,1,1,144,128]{4,3,2,1,0:T(8,128)(2,1)S(1)} collective-permute-done((bf16[2,1,1,144,128]{4,3,2,1,0:T(8,128)(2,1)S(1)}, bf16[2,1,1,144,128]{4,3,2,1,0:T(8,128)(2,1)S(1)}, u32[]{:S(2)}, u32[]{:S(2)}) %collective-permute-start.2) | collective-permute-done | bytes 73760 | tf_op jit(solution)/shard_map/ppermute | solution.py:451
  52.8 0.3 collective-permute-start.3
  53.1 0.3 collective-permute-done.6
  53.5 2.4 %collective-permute-start.7 = (bf16[1,1,1,152,128]{4,3,2,1,0:T(8,128)(2,1)S(1)}, bf16[1,1,1,152,128]{4,3,2,1,0:T(8,128)(2,1)S(1)}, u32[]{:S(2)}, u32[]{:S(2)}) collective-permute-start(bf16[1,1,1,152,128]{4,3,2,1,0:T(8,128)(2,1)S(1)} %dynamic-slice_convert_fusion.2), channel_id=1, source_target_pairs={{0,8},{1,9},{2,10},{3,11},{4,12},{5,13},{6,14},{7,15},{8,0},{9,1},... | collective-permute-start | bytes 116744 | tf_op jit(solution)/shard_map/ppermute | solution.py:451
  55.9 1.8 %collective-permute-done.3 = bf16[1,1,1,144,128]{4,3,2,1,0:T(8,128)(2,1)S(1)} collective-permute-done((bf16[1,1,1,144,128]{4,3,2,1,0:T(8,128)(2,1)S(1)}, bf16[1,1,1,144,128]{4,3,2,1,0:T(8,128)(2,1)S(1)}, u32[]{:S(2)}, u32[]{:S(2)}) %collective-permute-start.3) | collective-permute-done | bytes 36896 | tf_op jit(solution)/shard_map/ppermute | solution.py:451
  57.8 0.7 %collective-permute-done.7 = bf16[1,1,1,152,128]{4,3,2,1,0:T(8,128)(2,1)S(1)} collective-permute-done((bf16[1,1,1,152,128]{4,3,2,1,0:T(8,128)(2,1)S(1)}, bf16[1,1,1,152,128]{4,3,2,1,0:T(8,128)(2,1)S(1)}, u32[]{:S(2)}, u32[]{:S(2)}) %collective-permute-start.7) | collective-permute-done | bytes 38944 | tf_op jit(solution)/shard_map/ppermute | solution.py:451
  58.5 0.7 %final_sum.1 = (f32[1]{0:T(128)}, f32[16,768]{1,0:T(8,128)}, f32[16,256]{1,0:T(8,128)}, f32[16,256]{1,0:T(8,128)}, f32[16,512]{1,0:T(8,128)}, /*index=5*/f32[32,256]{1,0:T(8,128)}) custom-call(f32[144,128]{1,0:T(8,128)S(1)} %add_bitcast_fusion.1.refs_0_, f32[152,128]{1,0:T(8,128)S(1)} %add_bitcast_fusion.refs_1_), custom_call_target="tpu_custom_call" | custom-call | tf_op jit(solution)/shard_map/final_sum/pallas_call | solution.py:574
  (10 shorter events, 0.2 us)
Async XLA Ops:
  2.0 13.7 %all-to-all-start = ((s32[16,1,8]{2,1,0:T(1,128)}), s32[16,1,8]{2,1,0:T(1,128)S(1)}, u32[]{:S(2)}, u32[]{:S(2)}) async-start(s32[16,1,8]{2,1,0:T(1,128)} %copy.19), calls=%async_computation | async-start | bytes 16384 | tf_op jit(solution)/shard_map/all_to_all | solution.py:547
  40.6 1.6 %collective-permute-start = (bf16[8,144,128]{2,1,0:T(8,128)(2,1)S(1)}, bf16[8,144,128]{2,1,0:T(8,128)(2,1)S(1)}, u32[]{:S(2)}, u32[]{:S(2)}) collective-permute-start(bf16[8,144,128]{2,1,0:T(8,128)(2,1)S(1)} %get-tuple-element.40), channel_id=1, source_target_pairs={{0,1},{1,0},{2,3},{3,2},{4,5},{5,4},{6,7},{7,6},{8,9},{9,8},{10,11... | collective-permute-start | bytes 884744 | tf_op jit(solution)/shard_map/ppermute | solution.py:571
  40.7 2.0 %collective-permute-start.4 = (bf16[8,152,128]{2,1,0:T(8,128)(2,1)S(1)}, bf16[8,152,128]{2,1,0:T(8,128)(2,1)S(1)}, u32[]{:S(2)}, u32[]{:S(2)}) collective-permute-start(bf16[8,152,128]{2,1,0:T(8,128)(2,1)S(1)} %get-tuple-element.42), channel_id=1, source_target_pairs={{0,1},{1,0},{2,3},{3,2},{4,5},{5,4},{6,7},{7,6},{8,9},{9,8},{10,11... | collective-permute-start | bytes 933896 | tf_op jit(solution)/shard_map/ppermute | solution.py:571
  42.3 6.0 %collective-permute-start.1 = (bf16[2,2,1,144,128]{4,3,2,1,0:T(8,128)(2,1)S(1)}, bf16[2,2,1,144,128]{4,3,2,1,0:T(8,128)(2,1)S(1)}, u32[]{:S(2)}, u32[]{:S(2)}) collective-permute-start(bf16[2,2,1,144,128]{4,3,2,1,0:T(8,128)(2,1)S(1)} %add_convert_fusion.1), channel_id=1, source_target_pairs={{0,2},{1,3},{2,0},{3,1},{4,6},{5,7},{6,4},{7,5},{8,10},{9,11},{10,... | collective-permute-start | bytes 442376 | tf_op jit(solution)/shard_map/ppermute | solution.py:451
  42.8 6.1 %collective-permute-start.5 = (bf16[2,1,2,152,128]{4,3,2,1,0:T(8,128)(2,1)S(1)}, bf16[2,1,2,152,128]{4,3,2,1,0:T(8,128)(2,1)S(1)}, u32[]{:S(2)}, u32[]{:S(2)}) collective-permute-start(bf16[2,1,2,152,128]{4,3,2,1,0:T(8,128)(2,1)S(1)} %add_convert_fusion), channel_id=1, source_target_pairs={{0,4},{1,5},{2,6},{3,7},{4,0},{5,1},{6,2},{7,3},{8,12},{9,13},{10,... | collective-permute-start | bytes 466952 | tf_op jit(solution)/shard_map/ppermute | solution.py:451
  48.4 4.4 %collective-permute-start.2 = (bf16[2,1,1,144,128]{4,3,2,1,0:T(8,128)(2,1)S(1)}, bf16[2,1,1,144,128]{4,3,2,1,0:T(8,128)(2,1)S(1)}, u32[]{:S(2)}, u32[]{:S(2)}) collective-permute-start(bf16[2,1,1,144,128]{4,3,2,1,0:T(8,128)(2,1)S(1)} %dynamic-slice_convert_fusion.1), channel_id=1, source_target_pairs={{0,4},{1,5},{2,6},{3,7},{4,0},{5,1},{6,2},{7,3},{8,12},{9,13},{10,... | collective-permute-start | bytes 221192 | tf_op jit(solution)/shard_map/ppermute | solution.py:451
  49.0 4.5 %collective-permute-start.6 = (bf16[2,1,1,152,128]{4,3,2,1,0:T(8,128)(2,1)S(1)}, bf16[2,1,1,152,128]{4,3,2,1,0:T(8,128)(2,1)S(1)}, u32[]{:S(2)}, u32[]{:S(2)}) collective-permute-start(bf16[2,1,1,152,128]{4,3,2,1,0:T(8,128)(2,1)S(1)} %dynamic-slice_convert_fusion), channel_id=1, source_target_pairs={{0,2},{1,3},{2,0},{3,1},{4,6},{5,7},{6,4},{7,5},{8,10},{9,11},{10,... | collective-permute-start | bytes 233480 | tf_op jit(solution)/shard_map/ppermute | solution.py:451
  52.8 4.9 %collective-permute-start.3 = (bf16[1,1,1,144,128]{4,3,2,1,0:T(8,128)(2,1)S(1)}, bf16[1,1,1,144,128]{4,3,2,1,0:T(8,128)(2,1)S(1)}, u32[]{:S(2)}, u32[]{:S(2)}) collective-permute-start(bf16[1,1,1,144,128]{4,3,2,1,0:T(8,128)(2,1)S(1)} %dynamic-slice_convert_fusion.3), channel_id=1, source_target_pairs={{0,8},{1,9},{2,10},{3,11},{4,12},{5,13},{6,14},{7,15},{8,0},{9,1},... | collective-permute-start | bytes 110600 | tf_op jit(solution)/shard_map/ppermute | solution.py:451
  53.5 4.9 %collective-permute-start.7 = (bf16[1,1,1,152,128]{4,3,2,1,0:T(8,128)(2,1)S(1)}, bf16[1,1,1,152,128]{4,3,2,1,0:T(8,128)(2,1)S(1)}, u32[]{:S(2)}, u32[]{:S(2)}) collective-permute-start(bf16[1,1,1,152,128]{4,3,2,1,0:T(8,128)(2,1)S(1)} %dynamic-slice_convert_fusion.2), channel_id=1, source_target_pairs={{0,8},{1,9},{2,10},{3,11},{4,12},{5,13},{6,14},{7,15},{8,0},{9,1},... | collective-permute-start | bytes 116744 | tf_op jit(solution)/shard_map/ppermute | solution.py:451
